TPU v7x, 256 devices: a whole 4x4x8 slice. The times are simulated.
256 devices in a mesh: param: 16 (over x, y), slab: 16 (over z, core).
Axes of the slice: x: 4, y: 4, z: 8, core: 2. Of those that a mesh axis runs over, the one named last changes fastest.
Arguments:
- init_state: float32 [16, 128, 256, 128], P('param', None, 'slab'), may hold values from -6 to 6
- coef: float32 [16, 256, 128], P('param', 'slab'), may hold values from 0.06 to 0.16
- source: float32 [256, 128], P('slab'), may hold values from -6 to 6
- amplitudes: float32 [64], replicated, may hold values from 0.5 to 2
- sample_idx: int32 [16, 128], P('param'), may hold values from 0 to 63
- step_counts: int32 [16], P('param'), may hold values from 1 to 8, as said below
- sketch_signs: int32 [5, 128, 64], replicated, may hold values from 0 to 1
Outputs:
- modes: float32 [64, 256, 128], P(None, 'slab', 'param')
Inputs may be any that keep to these rules, and one draw needn't show every extreme that they name: `step_counts`: one group takes all 8 steps and another exactly one.
All inputs are finite; a program needn't handle non-finite values.
Results may differ from a plain program's by a relative error of at most 0.0003.
Values sent between devices are 32-bit elements; how exact they have to be, the bound alone decides.
No kernel may reach another device: no remote copies, remote signals or barrier semaphores. Data moves between devices by JAX's collectives and lax.ppermute only.
A program may use at most 64 MiB of HBM per device.

v0:
```python
import functools
import math

import jax
import jax.numpy as jnp
from jax import lax
from jax.experimental import pallas as pl
from jax.experimental.pallas import tpu as pltpu
from jax.sharding import Mesh
from jax.sharding import PartitionSpec as P

STEPS = 8
SCALE = 1.0 / math.sqrt(128.0)
HI = lax.Precision.HIGHEST
F32 = jnp.float32
VMEM = pl.BlockSpec(memory_space=pltpu.VMEM)
SMEM = pl.BlockSpec(memory_space=pltpu.SMEM)


def mm(a, b):
    return lax.dot_general(
        a, b, (((1,), (0,)), ((), ())), precision=HI, preferred_element_type=F32
    )


def mm_nt(a, b):
    return lax.dot_general(
        a, b, (((1,), (1,)), ((), ())), precision=HI, preferred_element_type=F32
    )


def thirds(x):
    hi = x.astype(jnp.bfloat16)
    rest = x - hi.astype(F32)
    mid = rest.astype(jnp.bfloat16)
    return hi, mid, (rest - mid.astype(F32)).astype(jnp.bfloat16)


def signs_mm(signs, x):
    hi, mid, lo = (jnp.dot(signs, t, preferred_element_type=F32) for t in thirds(x))
    return (hi + (mid + lo)) * SCALE


def mm_signs(x, signs):
    hi, mid, lo = (jnp.dot(t, signs, preferred_element_type=F32) for t in thirds(x))
    return (hi + (mid + lo)) * SCALE


def rows_of(v, i):
    return jnp.broadcast_to(v[i : i + 1, :], v.shape)


def factor(blocks, split):
    work = list(blocks)
    shape_of = work[0].shape
    sub = lax.broadcasted_iota(jnp.int32, shape_of, 0)
    lane = lax.broadcasted_iota(jnp.int32, shape_of, 1)
    base = jnp.where(lane < 64, 0, 64) if split else jnp.zeros(shape_of, jnp.int32)
    done = []
    for kb in range(8):
        cols = []
        for j in range(8):
            index = base + (8 * kb + j)
            cols.append([jnp.take_along_axis(work[i], index, axis=1) for i in range(kb, 8)])
        rows = [rows_of(work[kb], j) for j in range(8)]
        el = [[rows_of(cols[j][0], i) if i <= j else None for j in range(8)] for i in range(8)]
        outs, scaled = [], []
        for p in range(0, 8, 2):
            q = p + 1
            a, b, c = el[p][p], el[p][q], el[q][q]
            det = a * c - b * b
            inv = 1.0 / det
            rp, rq = rows[p], rows[q]
            root = lax.rsqrt(a)
            outs += [rp * root, (a * rq - b * rp) * (root * lax.rsqrt(det))]
            off = b * inv
            scaled += [(c * inv) * rp - off * rq, (a * inv) * rq - off * rp]
            left = {j: c * el[p][j] - b * el[q][j] for j in range(q + 1, 8)}
            right = {j: a * el[q][j] - b * el[p][j] for j in range(q + 1, 8)}
            for j in range(q + 1, 8):
                x, y = left[j] * inv, right[j] * inv
                for i in range(q + 1, j + 1):
                    el[i][j] = el[i][j] - (el[p][i] * left[j] + el[q][i] * right[j]) * inv
                rows[j] = rows[j] - (x * rp + y * rq)
                for n in range(1, 8 - kb):
                    cols[j][n] = cols[j][n] - (cols[p][n] * x + cols[q][n] * y)
        out = outs[0]
        for p in range(1, 8):
            out = jnp.where(sub == p, outs[p], out)
        done.append(out)
        for i in range(kb + 1, 8):
            acc = [cols[p][i - kb] * scaled[p] for p in range(8)]
            while len(acc) > 1:
                acc = [acc[2 * t] + acc[2 * t + 1] for t in range(len(acc) // 2)]
            work[i] = work[i] - acc[0]
    return jnp.concatenate(done, axis=0)


def shift_of(mat, diag):
    trace = jnp.sum(jnp.where(diag, mat, 0.0), keepdims=True)
    return jnp.where(diag, trace * (0.0001 / 64.0), 0.0)


def row_blocks(mat):
    return [mat[8 * i : 8 * i + 8] for i in range(8)]


def compress(yts, signs):
    row = lax.broadcasted_iota(jnp.int32, (64, 128), 0)
    lane = lax.broadcasted_iota(jnp.int32, (64, 128), 1)
    diag = lane == row
    wide = jnp.concatenate([signs, jnp.zeros((128, 64), jnp.bfloat16)], axis=1)
    moments = [mm_signs(yt, wide) for yt in yts]
    firsts = [
        factor(row_blocks(jnp.where(lane == row + 64, 1.0, m + shift_of(m, diag))), False)
        for m in moments
    ]
    linvs = [f[:, 64:] for f in firsts]
    hs = [mm(li, yt) for li, yt in zip(linvs, yts)]
    if len(hs) == 1:
        pad = jnp.zeros((64, 128), F32)
        inner = mm_nt(hs[0], jnp.concatenate([hs[0], pad], axis=0))
        inner = inner + shift_of(inner, diag)
        second = factor(row_blocks(inner), False)
        kts = [jnp.where(lane >= row, second, 0.0)[:, :64]]
    else:
        small = [mm_nt(h, h) for h in hs]
        small = [c + shift_of(c, diag[:, :64]) for c in small]
        second = factor(row_blocks(jnp.concatenate(small, axis=1)), True)
        second = jnp.where((lane & 63) >= row, second, 0.0)
        kts = [second[:, :64], second[:, 64:]]
    return [mm(k, li) for k, li in zip(kts, linvs)], [m[:, :64] for m in moments]


def gram_of(b, moment):
    return mm_nt(mm(b, moment), b)


def sketch_of_pair(first, cross, second, signs_t):
    top = jnp.concatenate([first, cross], axis=1)
    bottom = jnp.concatenate([cross.T, second], axis=1)
    return 0.5 * signs_mm(signs_t, jnp.concatenate([top, bottom], axis=0))


def signs_of(signs_ref, level):
    signs = 2.0 * signs_ref[level].astype(F32) - 1.0
    return signs.astype(jnp.bfloat16), signs.T.astype(jnp.bfloat16)


def both_halves(own_ref, other_ref):
    first = lax.axis_index("core") == 0
    own = own_ref[...]
    other = other_ref[...]
    return jnp.where(first, own, other), jnp.where(first, other, own)


def rest_of(value, by):
    return lax.rem(value + (by + 4), 4)


def exchange_blocks(vals, bit, lane_bit):
    lane = lax.broadcasted_iota(jnp.int32, vals[0].shape, 1)
    low = (lane & lane_bit) == 0
    out = list(vals)
    for i in range(len(vals)):
        if i & bit:
            continue
        a, b = vals[i], vals[i | bit]
        out[i] = jnp.where(low, a, pltpu.roll(b, lane_bit, 1))
        out[i | bit] = jnp.where(low, pltpu.roll(a, 128 - lane_bit, 1), b)
    return out


def flow_kernel(
    count_ref, x_ref, bef_ref, aft_ref, rate_ref, src_ref, amp_ref, signs_ref,
    yt_ref, d0, d1, d2, d3, c_s, h_s, src_s, f_s, field_s, s_s,
):
    for r in range(32):
        if r < 8:
            rate, src = bef_ref[1024 + r : 1025 + r, :], bef_ref[1032 + r : 1033 + r, :]
        elif r < 24:
            rate, src = rate_ref[r - 8 : r - 7, :], src_ref[r - 8 : r - 7, :]
        else:
            rate, src = aft_ref[1000 + r : 1001 + r, :], aft_ref[1008 + r : 1009 + r, :]
        at = slice(8 * r, 8 * r + 8)
        c_s[at, :] = jnp.broadcast_to(rate, (8, 128))
        h_s[at, :] = jnp.broadcast_to(0.5 * rate, (8, 128))
        src_s[at, :] = jnp.broadcast_to(src, (8, 128))
    count = count_ref[0]
    lane = lax.broadcasted_iota(jnp.int32, (8, 128), 1)
    not_first = lane != 0
    not_last = lane != 127

    def block(b, carry):
        amp = amp_ref[pl.ds(pl.multiple_of(b * 8, 8), 8), :]
        old = []
        for r in range(32):
            if r < 8:
                old.append(bef_ref[pl.ds(b * 64 + r, 8, stride=8), :])
            elif r < 24:
                old.append(x_ref[pl.ds(b * 128 + (r - 8), 8, stride=16), :])
            else:
                old.append(aft_ref[pl.ds(b * 64 + (r - 24), 8, stride=8), :])
            f_s[8 * r : 8 * r + 8, :] = amp * src_s[8 * r : 8 * r + 8, :]
        for t in range(STEPS):
            live = t < count
            new = list(old)
            for r in range(t + 1, 31 - t):
                at = slice(8 * r, 8 * r + 8)
                mid = old[r]
                left = jnp.where(not_first, pltpu.roll(mid, 1, 1), 0.0)
                right = jnp.where(not_last, pltpu.roll(mid, 127, 1), 0.0)
                lap = (old[r + 1] + old[r - 1]) + (right + left) - 4.0 * mid
                bend = jnp.tanh(mid)
                val = mid + (c_s[at, :] + h_s[at, :] * (bend * bend)) * lap + f_s[at, :]
                new[r] = jnp.where(live, val, mid)
            old = new
        for r in range(16):
            field_s[r, pl.ds(pl.multiple_of(b * 8, 8), 8), :] = old[8 + r]
        return carry

    lax.fori_loop(0, 16, block, 0)
    _, signs_t = signs_of(signs_ref, 0)
    yt = jnp.zeros((64, 128), F32)
    for q in range(4):
        parts = []
        for i in range(4):
            own = field_s[4 * q + i]
            sk = signs_mm(signs_t, own)
            yt = yt + mm_nt(sk, own)
            parts.append(sk)
        parts = exchange_blocks(exchange_blocks(parts, 1, 8), 2, 16)
        for j in range(4):
            s_s[j, q] = parts[j]
    yt_ref[...] = yt
    place = lax.axis_index("y")
    for d, out in enumerate((d0, d1, d2, d3)):
        out[...] = s_s[rest_of(place, d)]


def cross_kernel(yt_ref, r0, r1, r2, r3, keep_ref, send_ref, all_s, z_s, pay_s):
    place = lax.axis_index("y")
    for d, ref in enumerate((r0, r1, r2, r3)):
        all_s[rest_of(place, -d)] = ref[...]
    slabs = [jnp.zeros((64, 128), F32)] * 3
    for q in range(4):
        s0, s1, s2, s3 = (all_s[g, q] for g in range(4))
        upper = jnp.concatenate([s2, s3], axis=0)
        first = mm_nt(s0, jnp.concatenate([s1, s3], axis=0))
        slabs[1] = slabs[1] + mm_nt(s0, upper)
        slabs[2] = slabs[2] + mm_nt(s1, upper)
        slabs[0] = slabs[0] + jnp.concatenate([first[:, :64], mm_nt(s2, s3)], axis=1)
    for n in range(3):
        z_s[64 * n : 64 * n + 64] = slabs[n]
    for c in range(2):
        pay_s[c, 0:32] = yt_ref[32 * c : 32 * c + 32]
        for d in range(4):
            at = pl.multiple_of(48 * rest_of(place, d) + 24 * c, 8)
            pay_s[c, 32 + 24 * d : 56 + 24 * d] = z_s[pl.ds(at, 24), :]
    core = lax.axis_index("core")
    keep_ref[...] = pay_s[core]
    send_ref[...] = pay_s[1 - core]


def leaf_kernel(own_ref, other_ref, signs_ref, out_ref):
    low, high = both_halves(own_ref, other_ref)
    signs, _ = signs_of(signs_ref, 0)
    (b,), (moment,) = compress([jnp.concatenate([low[:32], high[:32]], axis=0)], signs)
    out_ref[0:64] = jnp.concatenate([b, gram_of(b, moment)], axis=1)
    out_ref[64:88] = low[32:]
    out_ref[88:112] = high[32:]


def middle_kernel(p0, p1, p2, p3, all_ref, signs_ref, out_ref, pay_s, z_s):
    place = lax.axis_index("y")
    for d, ref in enumerate((p0, p1, p2, p3)):
        pay_s[rest_of(place, -d)] = ref[...]
    for g in range(4):
        z_s[48 * g : 48 * g + 48] = pay_s[g, 64:112]
    bs = [pay_s[g, 0:64][:, :64] for g in range(4)]
    grams = [pay_s[g, 0:64][:, 64:] for g in range(4)]
    inside = z_s[0:64]
    crosses = [mm_nt(mm(bs[0], inside[:, :64]), bs[1]), mm_nt(mm(bs[2], inside[:, 64:]), bs[3])]
    signs, signs_t = signs_of(signs_ref, 1)
    yts = [
        sketch_of_pair(grams[2 * n], crosses[n], grams[2 * n + 1], signs_t) for n in range(2)
    ]
    ups, moments = compress(yts, signs)
    half = 0.5**0.5
    ws = []
    for n in range(2):
        low = signs_mm(signs_t[:, :64], bs[2 * n])
        high = signs_mm(signs_t[:, 64:], bs[2 * n + 1])
        ws.append(mm(ups[n], jnp.concatenate([low, high], axis=1)) * half)
    cross = mm_nt(mm(ws[0], z_s[64:192]), ws[1])
    signs, signs_t = signs_of(signs_ref, 2)
    first, second = (gram_of(u, m) for u, m in zip(ups, moments))
    (b,), (moment,) = compress([sketch_of_pair(first, cross, second, signs_t)], signs)
    low = signs_mm(signs_t[:, :64], ws[0])
    high = signs_mm(signs_t[:, 64:], ws[1])
    w = mm(b, jnp.concatenate([low, high], axis=1)) * half
    for q in range(4):
        out_ref[64 * q : 64 * q + 64] = mm(
            w, jnp.concatenate([all_ref[g, q] for g in range(4)], axis=0)
        )
    gram = gram_of(b, moment)
    out_ref[256:288] = jnp.concatenate([gram[:32], gram[32:]], axis=1)


def upper_kernel(r0, r1, r2, r3, signs_ref, s_ref, keep_ref, send_ref, all_s, pay_s):
    place = lax.axis_index("x")
    for d, ref in enumerate((r0, r1, r2, r3)):
        all_s[rest_of(place, -d)] = ref[0:256]
    _, signs_t = signs_of(signs_ref, 3)
    slabs = [jnp.zeros((64, 64), F32)] * 3
    for q in range(4):
        at = slice(64 * q, 64 * q + 64)
        sks = []
        for n in range(2):
            low, high = all_s[2 * n, at], all_s[2 * n + 1, at]
            sk = signs_mm(signs_t, jnp.concatenate([low, high], axis=0)) * (0.5**0.5)
            s_ref[n, q] = sk
            sks.append(sk)
            slabs[n] = slabs[n] + mm_nt(low, high)
        slabs[2] = slabs[2] + mm_nt(*sks)
    for c in range(2):
        at = slice(32 * c, 32 * c + 32)
        pay_s[c, 0:32] = jnp.concatenate([slabs[0][at], slabs[1][at]], axis=1)
        pay_s[c, 32:48] = jnp.concatenate(
            [slabs[2][32 * c : 32 * c + 16], slabs[2][32 * c + 16 : 32 * c + 32]], axis=1
        )
    core = lax.axis_index("core")
    keep_ref[...] = pay_s[core]
    send_ref[...] = pay_s[1 - core]


def last_kernel(own_ref, other_ref, r0, r1, r2, r3, s_ref, signs_ref, out_ref, gram_s):
    place = lax.axis_index("x")
    for d, ref in enumerate((r0, r1, r2, r3)):
        gram_s[rest_of(place, -d)] = ref[256:288]
    grams = []
    for g in range(4):
        packed = gram_s[g]
        grams.append(jnp.concatenate([packed[:, :64], packed[:, 64:]], axis=0))
    low, high = both_halves(own_ref, other_ref)
    pairs = jnp.concatenate([low[:32], high[:32]], axis=0)
    inside = jnp.concatenate(
        [low[32:, :64], low[32:, 64:], high[32:, :64], high[32:, 64:]], axis=0
    )
    signs, signs_t = signs_of(signs_ref, 3)
    yts = [
        sketch_of_pair(grams[2 * n], pairs[:, 64 * n : 64 * n + 64], grams[2 * n + 1], signs_t)
        for n in range(2)
    ]
    bs, moments = compress(yts, signs)
    cross = mm_nt(mm(bs[0], inside), bs[1])
    first, second = (gram_of(u, m) for u, m in zip(bs, moments))
    signs, signs_t = signs_of(signs_ref, 4)
    (b,), _ = compress([sketch_of_pair(first, cross, second, signs_t)], signs)
    lower = signs_mm(signs_t[:, :64], bs[0])
    upper = signs_mm(signs_t[:, 64:], bs[1])
    w = mm(b, jnp.concatenate([lower, upper], axis=1)) * (0.5**0.5)
    lane = lax.broadcasted_iota(jnp.int32, (128, 128), 1)
    block = lax.shift_right_logical(lane, 5)
    mine = jnp.zeros((128, 128), F32)
    for q in range(4):
        own = jnp.concatenate([s_ref[0, q], s_ref[1, q]], axis=0)
        turned = pltpu.roll(own, lax.rem(32 * q - 32 * place + 128, 128), 1)
        mine = jnp.where(block == q, turned, mine)
    out_ref[...] = mm(w, mine)


def call(kernel, out_shapes, smem, *args, scratch=()):
    specs = [SMEM] * smem + [VMEM] * (len(args) - smem)
    return pl.pallas_call(
        kernel,
        out_shape=out_shapes,
        in_specs=specs,
        out_specs=jax.tree.map(lambda _: VMEM, out_shapes),
        scratch_shapes=list(scratch),
    )(*args)


def shape(*dims):
    return jax.ShapeDtypeStruct(dims, F32)


def shift(value, axis, by):
    n = lax.axis_size(axis)
    return lax.ppermute(value, axis, [(i, (i + by) % n) for i in range(n)])


def from_ring(value, axis):
    return [value] + [shift(value, axis, d) for d in (1, 2, 3)]


def total(parts):
    return (parts[0] + parts[1]) + (parts[2] + parts[3])


def sum_over(value, axis):
    peers = lax.axis_size(axis)
    sent = jnp.broadcast_to(value[None], (peers, *value.shape))
    return lax.all_to_all(sent, axis, 0, 0, tiled=True).sum(axis=0)


def per_device(init_state, coef, source, amplitudes, sample_idx, step_counts, sketch_signs):
    field = init_state[0]
    rate = coef[0]
    table = amplitudes.shape[0]
    picks = sample_idx[0][:, None] == jnp.arange(table, dtype=jnp.int32)[None, :]
    amp = 0.1 * jnp.sum(jnp.where(picks, amplitudes[None, :], 0.0), axis=1)
    amp = jnp.broadcast_to(amp[:, None], (128, 128))

    slabs = ("z", "core")
    n = lax.axis_size(slabs)
    up = [(i, i + 1) for i in range(n - 1)]
    down = [(i + 1, i) for i in range(n - 1)]
    tail = jnp.concatenate([field[:, 8:], rate[None, 8:], source[None, 8:]], axis=0)
    head = jnp.concatenate([field[:, :8], rate[None, :8], source[None, :8]], axis=0)
    bef = lax.ppermute(tail, slabs, up)
    aft = lax.ppermute(head, slabs, down)

    yt, *chunks = call(
        flow_kernel,
        (shape(64, 128),) + (shape(4, 64, 128),) * 4,
        1,
        step_counts,
        field.reshape(2048, 128),
        bef.reshape(1040, 128),
        aft.reshape(1040, 128),
        rate,
        source,
        amp,
        sketch_signs,
        scratch=[pltpu.VMEM((256, 128), F32)] * 4
        + [pltpu.VMEM((16, 128, 128), F32), pltpu.VMEM((4, 4, 64, 128), F32)],
    )
    got = [chunks[0]] + [shift(chunks[d], "y", d) for d in (1, 2, 3)]
    keep, send, sketches = call(
        cross_kernel,
        (shape(128, 128), shape(128, 128), shape(4, 4, 64, 128)),
        0,
        yt,
        *got,
        scratch=[pltpu.VMEM((192, 128), F32), pltpu.VMEM((2, 128, 128), F32)],
    )
    half = keep + shift(send, "core", 1)
    quarters = [half[32:56]] + [shift(half[32 + 24 * d : 56 + 24 * d], "y", d) for d in (1, 2, 3)]
    own = sum_over(jnp.concatenate([half[:32], total(quarters)], axis=0), "z")
    leaf = call(leaf_kernel, shape(112, 128), 0, own, shift(own, "core", 1), sketch_signs)
    piece = call(
        middle_kernel,
        shape(288, 128),
        0,
        *from_ring(leaf, "y"),
        sketches,
        sketch_signs,
        scratch=[pltpu.VMEM((4, 112, 128), F32), pltpu.VMEM((192, 128), F32)],
    )
    pieces = from_ring(piece, "x")
    s, keep, send = call(
        upper_kernel,
        (shape(2, 4, 64, 128), shape(48, 128), shape(48, 128)),
        0,
        *pieces,
        sketch_signs,
        scratch=[pltpu.VMEM((4, 256, 128), F32), pltpu.VMEM((2, 48, 128), F32)],
    )
    half = keep + shift(send, "core", 1)
    own = sum_over(total(from_ring(half, "y")), "z")
    out = call(
        last_kernel,
        shape(64, 128),
        0,
        own,
        shift(own, "core", 1),
        *pieces,
        s,
        sketch_signs,
        scratch=[pltpu.VMEM((4, 32, 128), F32)],
    )
    return out.reshape(64, 16, 8)


def solution(mesh):
    fine = Mesh(mesh.devices.reshape(4, 4, 8, 2), ("x", "y", "z", "core"))
    group, slab = ("x", "y"), ("z", "core")
    return jax.shard_map(
        per_device,
        mesh=fine,
        in_specs=(
            P(group, None, slab, None),
            P(group, slab, None),
            P(slab, None),
            P(),
            P(group, None),
            P(group),
            P(),
        ),
        out_specs=P(None, slab, group),
        check_vma=False,
    )
```

profile of v0, /device:TPU:1, one launch (start us, length us, event | category | flops | bytes accessed | tf_op | source)
XLA Modules:
  0.0 159.8 jit_solution(2567727682284710364)
XLA Ops:
  0.0 0.7 fusion.3
  0.7 1.3 fusion.1
  2.0 4.9 %collective-permute-start = (f32[130,8,128]{2,1,0:T(8,128)S(1)}, f32[130,8,128]{2,1,0:T(8,128)S(1)}, u32[]{:S(2)}, u32[]{:S(2)}) collective-permute-start(f32[130,8,128]{2,1,0:T(8,128)S(1)} %pad_maximum_fusion), channel_id=1, source_target_pairs={{0,1},{1,2},{2,3},{3,4},{4,5},{5,6},{6,7},{7,8},{8,9},{9,10},{10,1... | collective-permute-start | bytes 1597448 | tf_op jit(solution)/shard_map/ppermute | solution.py:421
  7.0 2.1 %collective-permute-start.1 = (f32[130,8,128]{2,1,0:T(8,128)S(1)}, f32[130,8,128]{2,1,0:T(8,128)S(1)}, u32[]{:S(2)}, u32[]{:S(2)}) collective-permute-start(f32[130,8,128]{2,1,0:T(8,128)S(1)} %pad_maximum_fusion.1), channel_id=1, source_target_pairs={{1,0},{2,1},{3,2},{4,3},{5,4},{6,5},{7,6},{8,7},{9,8},{10,9},{11,1... | collective-permute-start | bytes 1597448 | tf_op jit(solution)/shard_map/ppermute | solution.py:422
  9.7 0.9 copy.20.signs_ref
  10.7 0.7 copy-done.17
  11.3 0.0 copy-done.18
  11.3 0.1 select_reduce_fusion
  11.4 1.7 %collective-permute-done = f32[130,8,128]{2,1,0:T(8,128)S(1)} collective-permute-done((f32[130,8,128]{2,1,0:T(8,128)S(1)}, f32[130,8,128]{2,1,0:T(8,128)S(1)}, u32[]{:S(2)}, u32[]{:S(2)}) %collective-permute-start) | collective-permute-done | bytes 532512 | tf_op jit(solution)/shard_map/ppermute | solution.py:421
  13.2 4.6 %collective-permute-done.1 = f32[130,8,128]{2,1,0:T(8,128)S(1)} collective-permute-done((f32[130,8,128]{2,1,0:T(8,128)S(1)}, f32[130,8,128]{2,1,0:T(8,128)S(1)}, u32[]{:S(2)}, u32[]{:S(2)}) %collective-permute-start.1) | collective-permute-done | bytes 532512 | tf_op jit(solution)/shard_map/ppermute | solution.py:422
  17.8 0.8 broadcast_in_dim.44.amp_ref
  18.6 17.6 %shard_map.73 = (f32[64,128]{1,0:T(8,128)}, f32[4,64,128]{2,1,0:T(8,128)}, f32[4,64,128]{2,1,0:T(8,128)}, f32[4,64,128]{2,1,0:T(8,128)}, f32[4,64,128]{2,1,0:T(8,128)}) custom-call(s32[1]{0:T(128)S(6)} %copy.26.count_ref, f32[2048,128]{1,0:T(8,128)} %bitcast.12, f32[1040,128]{1,0:T(8,128)} %bitcast.13, f32[1040,128]{1,0:T(8,128)} %bitcast.14, ...), custom_call_target="tpu_custom_call" | custom-call | tf_op jit(solution)/shard_map/pallas_call | solution.py:375
  36.2 1.3 collective-permute-start.2
  37.5 2.6 %collective-permute-start.3 = (f32[4,64,128]{2,1,0:T(8,128)}, f32[4,64,128]{2,1,0:T(8,128)S(1)}, u32[]{:S(2)}, u32[]{:S(2)}) collective-permute-start(f32[4,64,128]{2,1,0:T(8,128)} %get-tuple-element.19), channel_id=1, source_target_pairs={{0,32},{16,48},{32,0},{48,16},{1,33},{17,49},{33,1},{49,17},{2,34}... | collective-permute-start | bytes 393224 | tf_op jit(solution)/shard_map/ppermute | solution.py:390
  40.1 1.1 collective-permute-start.4
  41.2 0.3 collective-permute-done.2.r1
  41.5 2.6 %collective-permute-done.3.r2 = f32[4,64,128]{2,1,0:T(8,128)S(1)} collective-permute-done((f32[4,64,128]{2,1,0:T(8,128)}, f32[4,64,128]{2,1,0:T(8,128)S(1)}, u32[]{:S(2)}, u32[]{:S(2)}) %collective-permute-start.3) | collective-permute-done | bytes 131104 | tf_op jit(solution)/shard_map/ppermute | solution.py:390
  44.1 0.1 collective-permute-done.4.r3
  44.1 0.6 copy-done.7
  44.7 0.1 copy-done.8
  44.8 3.8 %shard_map.74 = (f32[128,128]{1,0:T(8,128)}, f32[128,128]{1,0:T(8,128)}, f32[4,4,64,128]{3,2,1,0:T(8,128)}) custom-call(f32[64,128]{1,0:T(8,128)} %get-tuple-element.16.yt_ref, f32[4,64,128]{2,1,0:T(8,128)} %get-tuple-element.17.r0, f32[4,64,128]{2,1,0:T(8,128)} %copy-done.6, f32[4,64,128]{2,1,0:T(8,128)} %copy-done.7, f32[4,64,128]{2,1,0:T(8,128)} %copy-done.8), custom_call_target="tpu_custom_call" | custom-call | tf_op jit(solution)/shard_map/pallas_call | solution.py:375
  48.6 1.5 collective-permute-done.5
  50.0 0.9 add.24
  50.9 2.4 %collective-permute-start.8 = (f32[24,128]{1,0:T(8,128)S(1)}, f32[24,128]{1,0:T(8,128)S(1)}, u32[]{:S(2)}, u32[]{:S(2)}) collective-permute-start(f32[24,128]{1,0:T(8,128)S(1)} %get-tuple-element.29), channel_id=1, source_target_pairs={{0,48},{16,0},{32,16},{48,32},{1,49},{17,1},{33,17},{49,33},{2,50}... | collective-permute-start | bytes 36872 | tf_op jit(solution)/shard_map/ppermute | solution.py:390
  53.3 0.4 collective-permute-start.7
  53.7 0.4 collective-permute-start.6
  54.1 0.0 collective-permute-done.8
  54.1 3.2 %collective-permute-done.7 = f32[24,128]{1,0:T(8,128)S(1)} collective-permute-done((f32[24,128]{1,0:T(8,128)S(1)}, f32[24,128]{1,0:T(8,128)S(1)}, u32[]{:S(2)}, u32[]{:S(2)}) %collective-permute-start.7) | collective-permute-done | bytes 12320 | tf_op jit(solution)/shard_map/ppermute | solution.py:390
  57.3 0.1 collective-permute-done.6
  57.5 19.2 %all_to_all.10 = f32[8,56,128]{2,1,0:T(8,128)S(1)} all-to-all(f32[8,56,128]{2,1,0:T(8,128)S(1)} %broadcast_in_dim.45), channel_id=1, replica_groups=mesh['x'=4,'y'=4,'z'=8,'core'=2] {'z'}, dimensions={0} | all-to-all | bytes 458752 | tf_op jit(solution)/shard_map/all_to_all | solution.py:404
  76.7 3.7 %collective-permute-start.9 = (f32[56,128]{1,0:T(8,128)S(1)}, f32[56,128]{1,0:T(8,128)S(1)}, u32[]{:S(2)}, u32[]{:S(2)}) collective-permute-start(f32[56,128]{1,0:T(8,128)S(1)} %reduce_sum.28.own_ref), channel_id=1, source_target_pairs={{0,1},{1,0},{2,3},{3,2},{4,5},{5,4},{6,7},{7,6},{8,9},{9,8},{10,11... | collective-permute-start | bytes 86024 | tf_op jit(solution)/shard_map/ppermute | solution.py:390
  80.5 0.9 collective-permute-done.9.other_ref
  81.3 0.6 copy-done.15
  81.9 5.5 %shard_map.75.p0 = f32[112,128]{1,0:T(8,128)} custom-call(f32[56,128]{1,0:T(8,128)} %copy-done.9, f32[56,128]{1,0:T(8,128)} %copy-done.15, s32[5,128,64]{2,1,0:T(8,128)} %copy.20.signs_ref), custom_call_target="tpu_custom_call" | custom-call | tf_op jit(solution)/shard_map/pallas_call | solution.py:375
  87.5 1.0 collective-permute-start.11
  88.4 0.8 collective-permute-start.10
  89.2 1.5 collective-permute-done.12.p3
  90.7 1.5 collective-permute-done.11.p2
  92.2 1.9 %collective-permute-done.10.p1 = f32[112,128]{1,0:T(8,128)S(1)} collective-permute-done((f32[112,128]{1,0:T(8,128)}, f32[112,128]{1,0:T(8,128)S(1)}, u32[]{:S(2)}, u32[]{:S(2)}) %collective-permute-start.10) | collective-permute-done | bytes 57376 | tf_op jit(solution)/shard_map/ppermute | solution.py:390
  94.1 0.6 copy-done.13
  94.7 12.1 %shard_map.76.r0 = f32[288,128]{1,0:T(8,128)} custom-call(f32[112,128]{1,0:T(8,128)} %shard_map.75.p0, f32[112,128]{1,0:T(8,128)} %copy-done.13, f32[112,128]{1,0:T(8,128)} %copy-done.12, f32[112,128]{1,0:T(8,128)} %copy-done.11, f32[4,4,64,128]{3,2,1,0:T(8,128)} %get-tuple-element.23.all_ref, s32[5,128,64]{2,1,0:T(8,128)} %copy.20.signs_ref), custom_call_target="tpu_custom_call" | custom-call | tf_op jit(solution)/shard_map/pallas_call | solution.py:375
  106.9 2.5 %collective-permute-start.15 = (f32[288,128]{1,0:T(8,128)}, f32[288,128]{1,0:T(8,128)S(1)}, u32[]{:S(2)}, u32[]{:S(2)}) collective-permute-start(f32[288,128]{1,0:T(8,128)} %shard_map.76.r0), channel_id=1, source_target_pairs={{0,192},{64,0},{128,64},{192,128},{1,193},{65,1},{129,65},{193,129... | collective-permute-start | bytes 442376 | tf_op jit(solution)/shard_map/ppermute | solution.py:390
  109.3 0.5 collective-permute-start.14
  109.9 0.6 collective-permute-start.13
  110.5 2.4 %collective-permute-done.15.r3 = f32[288,128]{1,0:T(8,128)S(1)} collective-permute-done((f32[288,128]{1,0:T(8,128)}, f32[288,128]{1,0:T(8,128)S(1)}, u32[]{:S(2)}, u32[]{:S(2)}) %collective-permute-start.15) | collective-permute-done | bytes 147488 | tf_op jit(solution)/shard_map/ppermute | solution.py:390
  112.9 2.2 %collective-permute-done.14.r2 = f32[288,128]{1,0:T(8,128)S(1)} collective-permute-done((f32[288,128]{1,0:T(8,128)}, f32[288,128]{1,0:T(8,128)S(1)}, u32[]{:S(2)}, u32[]{:S(2)}) %collective-permute-start.14) | collective-permute-done | bytes 147488 | tf_op jit(solution)/shard_map/ppermute | solution.py:390
  115.2 4.6 %collective-permute-done.13.r1 = f32[288,128]{1,0:T(8,128)S(1)} collective-permute-done((f32[288,128]{1,0:T(8,128)}, f32[288,128]{1,0:T(8,128)S(1)}, u32[]{:S(2)}, u32[]{:S(2)}) %collective-permute-start.13) | collective-permute-done | bytes 147488 | tf_op jit(solution)/shard_map/ppermute | solution.py:390
  119.8 0.7 copy-done.2
  120.4 3.1 %shard_map.77 = (f32[2,4,64,128]{3,2,1,0:T(8,128)}, f32[48,128]{1,0:T(8,128)}, f32[48,128]{1,0:T(8,128)}) custom-call(f32[288,128]{1,0:T(8,128)} %shard_map.76.r0, f32[288,128]{1,0:T(8,128)} %copy-done.2, f32[288,128]{1,0:T(8,128)} %copy-done.1, f32[288,128]{1,0:T(8,128)} %copy-done, s32[5,128,64]{2,1,0:T(8,128)} %copy.20.signs_ref), custom_call_target="tpu_custom_call" | custom-call | tf_op jit(solution)/shard_map/pallas_call | solution.py:375
  123.5 0.7 collective-permute-start.16
  124.2 1.1 collective-permute-done.16
  125.3 0.7 add.28
  126.0 0.7 collective-permute-start.19
  126.8 0.6 collective-permute-start.18
  127.4 0.1 collective-permute-start.17
  127.5 1.2 collective-permute-done.19
  128.7 2.2 %collective-permute-done.18 = f32[48,128]{1,0:T(8,128)S(1)} collective-permute-done((f32[48,128]{1,0:T(8,128)S(1)}, f32[48,128]{1,0:T(8,128)S(1)}, u32[]{:S(2)}, u32[]{:S(2)}) %collective-permute-start.18) | collective-permute-done | bytes 24608 | tf_op jit(solution)/shard_map/ppermute | solution.py:390
  131.0 0.3 collective-permute-done.17
  131.3 11.1 %all_to_all.11 = f32[8,48,128]{2,1,0:T(8,128)S(1)} all-to-all(f32[8,48,128]{2,1,0:T(8,128)S(1)} %broadcast_in_dim.46), channel_id=1, replica_groups=mesh['x'=4,'y'=4,'z'=8,'core'=2] {'z'}, dimensions={0} | all-to-all | bytes 393216 | tf_op jit(solution)/shard_map/all_to_all | solution.py:404
  142.4 3.2 %collective-permute-start.20 = (f32[48,128]{1,0:T(8,128)S(1)}, f32[48,128]{1,0:T(8,128)S(1)}, u32[]{:S(2)}, u32[]{:S(2)}) collective-permute-start(f32[48,128]{1,0:T(8,128)S(1)} %reduce_sum.29.own_ref), channel_id=1, source_target_pairs={{0,1},{1,0},{2,3},{3,2},{4,5},{5,4},{6,7},{7,6},{8,9},{9,8},{10,11... | collective-permute-start | bytes 73736 | tf_op jit(solution)/shard_map/ppermute | solution.py:390
  145.7 0.8 collective-permute-done.20.other_ref
  146.5 0.6 copy-done.16
  147.1 11.2 %shard_map.78 = f32[64,128]{1,0:T(8,128)} custom-call(f32[48,128]{1,0:T(8,128)} %copy-done.10, f32[48,128]{1,0:T(8,128)} %copy-done.16, f32[288,128]{1,0:T(8,128)} %shard_map.76.r0, f32[288,128]{1,0:T(8,128)} %copy-done.2, f32[288,128]{1,0:T(8,128)} %copy-done.1, f32[288,128]{1,0:T(8,128)} %copy-done, f32[2,4,64,128]{3,2,1,0:T(8,128)} %get-tuple-element.26.s_ref, ...), custom_call_target="tpu_custom_call" | custom-call | tf_op jit(solution)/shard_map/pallas_call | solution.py:375
  158.3 1.5 copy.25
  (45 shorter events, 0.2 us)
Async XLA Ops:
  0.0 0.7 copy-start.14
  2.0 11.1 %collective-permute-start = (f32[130,8,128]{2,1,0:T(8,128)S(1)}, f32[130,8,128]{2,1,0:T(8,128)S(1)}, u32[]{:S(2)}, u32[]{:S(2)}) collective-permute-start(f32[130,8,128]{2,1,0:T(8,128)S(1)} %pad_maximum_fusion), channel_id=1, source_target_pairs={{0,1},{1,2},{2,3},{3,4},{4,5},{5,6},{6,7},{7,8},{8,9},{9,10},{10,1... | collective-permute-start | bytes 1597448 | tf_op jit(solution)/shard_map/ppermute | solution.py:421
  7.0 2.8 %copy-start.5 = (s32[5,128,64]{1,2,0:T(8,128)S(1)}, s32[5,128,64]{1,2,0:T(8,128)}, u32[]{:S(2)}) copy-start(s32[5,128,64]{1,2,0:T(8,128)} %param.13) | copy-start | bytes 491524
  7.0 10.7 %collective-permute-start.1 = (f32[130,8,128]{2,1,0:T(8,128)S(1)}, f32[130,8,128]{2,1,0:T(8,128)S(1)}, u32[]{:S(2)}, u32[]{:S(2)}) collective-permute-start(f32[130,8,128]{2,1,0:T(8,128)S(1)} %pad_maximum_fusion.1), channel_id=1, source_target_pairs={{1,0},{2,1},{3,2},{4,3},{5,4},{6,5},{7,6},{8,7},{9,8},{10,9},{11,1... | collective-permute-start | bytes 1597448 | tf_op jit(solution)/shard_map/ppermute | solution.py:422
  10.6 0.7 copy-start.17
  10.6 0.7 copy-start.18
  13.2 5.4 %copy-start.3 = (f32[130,8,128]{2,1,0:T(8,128)}, f32[130,8,128]{2,1,0:T(8,128)S(1)}, u32[]{:S(2)}) copy-start(f32[130,8,128]{2,1,0:T(8,128)S(1)} %collective-permute-done) | copy-start | bytes 1597444
  17.8 0.8 copy-start.4
  36.2 5.3 %collective-permute-start.2 = (f32[4,64,128]{2,1,0:T(8,128)}, f32[4,64,128]{2,1,0:T(8,128)S(1)}, u32[]{:S(2)}, u32[]{:S(2)}) collective-permute-start(f32[4,64,128]{2,1,0:T(8,128)} %get-tuple-element.18), channel_id=1, source_target_pairs={{0,16},{16,32},{32,48},{48,0},{1,17},{17,33},{33,49},{49,1},{2,18}... | collective-permute-start | bytes 393224 | tf_op jit(solution)/shard_map/ppermute | solution.py:390
  37.5 6.6 %collective-permute-start.3 = (f32[4,64,128]{2,1,0:T(8,128)}, f32[4,64,128]{2,1,0:T(8,128)S(1)}, u32[]{:S(2)}, u32[]{:S(2)}) collective-permute-start(f32[4,64,128]{2,1,0:T(8,128)} %get-tuple-element.19), channel_id=1, source_target_pairs={{0,32},{16,48},{32,0},{48,16},{1,33},{17,49},{33,1},{49,17},{2,34}... | collective-permute-start | bytes 393224 | tf_op jit(solution)/shard_map/ppermute | solution.py:390
  40.1 4.0 %collective-permute-start.4 = (f32[4,64,128]{2,1,0:T(8,128)}, f32[4,64,128]{2,1,0:T(8,128)S(1)}, u32[]{:S(2)}, u32[]{:S(2)}) collective-permute-start(f32[4,64,128]{2,1,0:T(8,128)} %get-tuple-element.20), channel_id=1, source_target_pairs={{0,48},{16,0},{32,16},{48,32},{1,49},{17,1},{33,17},{49,33},{2,50}... | collective-permute-start | bytes 393224 | tf_op jit(solution)/shard_map/ppermute | solution.py:390
  41.5 2.7 %copy-start.6 = (f32[4,64,128]{2,1,0:T(8,128)}, f32[4,64,128]{2,1,0:T(8,128)S(1)}, u32[]{:S(2)}) copy-start(f32[4,64,128]{2,1,0:T(8,128)S(1)} %collective-permute-done.2.r1) | copy-start | bytes 393220
  44.1 0.7 copy-start.7
  44.1 0.7 copy-start.8
  48.6 1.5 collective-permute-start.5
  50.9 3.2 %collective-permute-start.8 = (f32[24,128]{1,0:T(8,128)S(1)}, f32[24,128]{1,0:T(8,128)S(1)}, u32[]{:S(2)}, u32[]{:S(2)}) collective-permute-start(f32[24,128]{1,0:T(8,128)S(1)} %get-tuple-element.29), channel_id=1, source_target_pairs={{0,48},{16,0},{32,16},{48,32},{1,49},{17,1},{33,17},{49,33},{2,50}... | collective-permute-start | bytes 36872 | tf_op jit(solution)/shard_map/ppermute | solution.py:390
  53.3 4.0 %collective-permute-start.7 = (f32[24,128]{1,0:T(8,128)S(1)}, f32[24,128]{1,0:T(8,128)S(1)}, u32[]{:S(2)}, u32[]{:S(2)}) collective-permute-start(f32[24,128]{1,0:T(8,128)S(1)} %get-tuple-element.30), channel_id=1, source_target_pairs={{0,32},{16,48},{32,0},{48,16},{1,33},{17,49},{33,1},{49,17},{2,34}... | collective-permute-start | bytes 36872 | tf_op jit(solution)/shard_map/ppermute | solution.py:390
  53.7 3.8 %collective-permute-start.6 = (f32[24,128]{1,0:T(8,128)S(1)}, f32[24,128]{1,0:T(8,128)S(1)}, u32[]{:S(2)}, u32[]{:S(2)}) collective-permute-start(f32[24,128]{1,0:T(8,128)S(1)} %get-tuple-element.31), channel_id=1, source_target_pairs={{0,16},{16,32},{32,48},{48,0},{1,17},{17,33},{33,49},{49,1},{2,18}... | collective-permute-start | bytes 36872 | tf_op jit(solution)/shard_map/ppermute | solution.py:390
  76.7 4.6 %copy-start.9 = (f32[56,128]{1,0:T(8,128)}, f32[56,128]{1,0:T(8,128)S(1)}, u32[]{:S(2)}) copy-start(f32[56,128]{1,0:T(8,128)S(1)} %reduce_sum.28.own_ref) | copy-start | bytes 86020
  76.7 4.6 %collective-permute-start.9 = (f32[56,128]{1,0:T(8,128)S(1)}, f32[56,128]{1,0:T(8,128)S(1)}, u32[]{:S(2)}, u32[]{:S(2)}) collective-permute-start(f32[56,128]{1,0:T(8,128)S(1)} %reduce_sum.28.own_ref), channel_id=1, source_target_pairs={{0,1},{1,0},{2,3},{3,2},{4,5},{5,4},{6,7},{7,6},{8,9},{9,8},{10,11... | collective-permute-start | bytes 86024 | tf_op jit(solution)/shard_map/ppermute | solution.py:390
  81.3 0.6 copy-start.15
  87.4 3.2 %collective-permute-start.12 = (f32[112,128]{1,0:T(8,128)}, f32[112,128]{1,0:T(8,128)S(1)}, u32[]{:S(2)}, u32[]{:S(2)}) collective-permute-start(f32[112,128]{1,0:T(8,128)} %shard_map.75.p0), channel_id=1, source_target_pairs={{0,48},{16,0},{32,16},{48,32},{1,49},{17,1},{33,17},{49,33},{2,50}... | collective-permute-start | bytes 172040 | tf_op jit(solution)/shard_map/ppermute | solution.py:390
  87.5 4.7 %collective-permute-start.11 = (f32[112,128]{1,0:T(8,128)}, f32[112,128]{1,0:T(8,128)S(1)}, u32[]{:S(2)}, u32[]{:S(2)}) collective-permute-start(f32[112,128]{1,0:T(8,128)} %shard_map.75.p0), channel_id=1, source_target_pairs={{0,32},{16,48},{32,0},{48,16},{1,33},{17,49},{33,1},{49,17},{2,34}... | collective-permute-start | bytes 172040 | tf_op jit(solution)/shard_map/ppermute | solution.py:390
  88.4 5.7 %collective-permute-start.10 = (f32[112,128]{1,0:T(8,128)}, f32[112,128]{1,0:T(8,128)S(1)}, u32[]{:S(2)}, u32[]{:S(2)}) collective-permute-start(f32[112,128]{1,0:T(8,128)} %shard_map.75.p0), channel_id=1, source_target_pairs={{0,16},{16,32},{32,48},{48,0},{1,17},{17,33},{33,49},{49,1},{2,18}... | collective-permute-start | bytes 172040 | tf_op jit(solution)/shard_map/ppermute | solution.py:390
  90.7 3.4 %copy-start.11 = (f32[112,128]{1,0:T(8,128)}, f32[112,128]{1,0:T(8,128)S(1)}, u32[]{:S(2)}) copy-start(f32[112,128]{1,0:T(8,128)S(1)} %collective-permute-done.12.p3) | copy-start | bytes 172036
  92.2 1.9 %copy-start.12 = (f32[112,128]{1,0:T(8,128)}, f32[112,128]{1,0:T(8,128)S(1)}, u32[]{:S(2)}) copy-start(f32[112,128]{1,0:T(8,128)S(1)} %collective-permute-done.11.p2) | copy-start | bytes 172036
  94.1 0.6 copy-start.13
  106.9 6.0 %collective-permute-start.15 = (f32[288,128]{1,0:T(8,128)}, f32[288,128]{1,0:T(8,128)S(1)}, u32[]{:S(2)}, u32[]{:S(2)}) collective-permute-start(f32[288,128]{1,0:T(8,128)} %shard_map.76.r0), channel_id=1, source_target_pairs={{0,192},{64,0},{128,64},{192,128},{1,193},{65,1},{129,65},{193,129... | collective-permute-start | bytes 442376 | tf_op jit(solution)/shard_map/ppermute | solution.py:390
  109.3 5.8 %collective-permute-start.14 = (f32[288,128]{1,0:T(8,128)}, f32[288,128]{1,0:T(8,128)S(1)}, u32[]{:S(2)}, u32[]{:S(2)}) collective-permute-start(f32[288,128]{1,0:T(8,128)} %shard_map.76.r0), channel_id=1, source_target_pairs={{0,128},{64,192},{128,0},{192,64},{1,129},{65,193},{129,1},{193,65... | collective-permute-start | bytes 442376 | tf_op jit(solution)/shard_map/ppermute | solution.py:390
  109.9 9.9 %collective-permute-start.13 = (f32[288,128]{1,0:T(8,128)}, f32[288,128]{1,0:T(8,128)S(1)}, u32[]{:S(2)}, u32[]{:S(2)}) collective-permute-start(f32[288,128]{1,0:T(8,128)} %shard_map.76.r0), channel_id=1, source_target_pairs={{0,64},{64,128},{128,192},{192,0},{1,65},{65,129},{129,193},{193,1... | collective-permute-start | bytes 442376 | tf_op jit(solution)/shard_map/ppermute | solution.py:390
  112.9 6.8 %copy-start = (f32[288,128]{1,0:T(8,128)}, f32[288,128]{1,0:T(8,128)S(1)}, u32[]{:S(2)}) copy-start(f32[288,128]{1,0:T(8,128)S(1)} %collective-permute-done.15.r3) | copy-start | bytes 442372
  115.2 4.6 %copy-start.1 = (f32[288,128]{1,0:T(8,128)}, f32[288,128]{1,0:T(8,128)S(1)}, u32[]{:S(2)}) copy-start(f32[288,128]{1,0:T(8,128)S(1)} %collective-permute-done.14.r2) | copy-start | bytes 442372
  119.8 0.7 copy-start.2
  123.5 1.8 %collective-permute-start.16 = (f32[48,128]{1,0:T(8,128)}, f32[48,128]{1,0:T(8,128)S(1)}, u32[]{:S(2)}, u32[]{:S(2)}) collective-permute-start(f32[48,128]{1,0:T(8,128)} %get-tuple-element.25), channel_id=1, source_target_pairs={{0,1},{1,0},{2,3},{3,2},{4,5},{5,4},{6,7},{7,6},{8,9},{9,8},{10,11... | collective-permute-start | bytes 73736 | tf_op jit(solution)/shard_map/ppermute | solution.py:390
  126.0 2.7 %collective-permute-start.19 = (f32[48,128]{1,0:T(8,128)S(1)}, f32[48,128]{1,0:T(8,128)S(1)}, u32[]{:S(2)}, u32[]{:S(2)}) collective-permute-start(f32[48,128]{1,0:T(8,128)S(1)} %add.28), channel_id=1, source_target_pairs={{0,48},{16,0},{32,16},{48,32},{1,49},{17,1},{33,17},{49,33},{2,50}... | collective-permute-start | bytes 73736 | tf_op jit(solution)/shard_map/ppermute | solution.py:390
  126.8 4.2 %collective-permute-start.18 = (f32[48,128]{1,0:T(8,128)S(1)}, f32[48,128]{1,0:T(8,128)S(1)}, u32[]{:S(2)}, u32[]{:S(2)}) collective-permute-start(f32[48,128]{1,0:T(8,128)S(1)} %add.28), channel_id=1, source_target_pairs={{0,32},{16,48},{32,0},{48,16},{1,33},{17,49},{33,1},{49,17},{2,34}... | collective-permute-start | bytes 73736 | tf_op jit(solution)/shard_map/ppermute | solution.py:390
  127.4 3.9 %collective-permute-start.17 = (f32[48,128]{1,0:T(8,128)S(1)}, f32[48,128]{1,0:T(8,128)S(1)}, u32[]{:S(2)}, u32[]{:S(2)}) collective-permute-start(f32[48,128]{1,0:T(8,128)S(1)} %add.28), channel_id=1, source_target_pairs={{0,16},{16,32},{32,48},{48,0},{1,17},{17,33},{33,49},{49,1},{2,18}... | collective-permute-start | bytes 73736 | tf_op jit(solution)/shard_map/ppermute | solution.py:390
  142.4 4.1 %copy-start.10 = (f32[48,128]{1,0:T(8,128)}, f32[48,128]{1,0:T(8,128)S(1)}, u32[]{:S(2)}) copy-start(f32[48,128]{1,0:T(8,128)S(1)} %reduce_sum.29.own_ref) | copy-start | bytes 73732
  142.4 4.1 %collective-permute-start.20 = (f32[48,128]{1,0:T(8,128)S(1)}, f32[48,128]{1,0:T(8,128)S(1)}, u32[]{:S(2)}, u32[]{:S(2)}) collective-permute-start(f32[48,128]{1,0:T(8,128)S(1)} %reduce_sum.29.own_ref), channel_id=1, source_target_pairs={{0,1},{1,0},{2,3},{3,2},{4,5},{5,4},{6,7},{7,6},{8,9},{9,8},{10,11... | collective-permute-start | bytes 73736 | tf_op jit(solution)/shard_map/ppermute | solution.py:390
  146.5 0.6 copy-start.16
where the time goes:
time: 160 us
  Pallas kernels  53.3 us (33%)
  waiting for transfers between devices  34.8 us (22%)
  blocking collectives  30.3 us (19%)
  starting transfers between devices  29.7 us (19%)
  local copies, waits for them, and re-layouts  9.1 us (6%)
  other arithmetic  1.82 us (1%)
    pallas_call x6, Pallas kernels, call(): pl.pallas_call(kernel, out_shape=out_shapes, in_specs=specs, out_specs=ja...  53.3 us
    all_to_all x2, blocking collectives, sum_over(): return lax.all_to_all(sent, axis, 0, 0, tiled=True).sum(axis=0)  30.3 us
    ppermute x19, waiting for transfers between devices, shift(): return lax.ppermute(value, axis, [(i, (i + by) % n) for i in range(n)])  28.5 us
    ppermute x19, starting transfers between devices, shift(): return lax.ppermute(value, axis, [(i, (i + by) % n) for i in range(n)])  22.7 us
    ppermute x1, starting transfers between devices, per_device(): bef = lax.ppermute(tail, slabs, up)  4.92 us
    unnamed x39, local copies, waits for them, and re-layouts  4.75 us
    ppermute x1, waiting for transfers between devices, per_device(): aft = lax.ppermute(head, slabs, down)  4.58 us
  transfers between devices with their start and end apart: 21, of which 20 were waited for; matrix products, arithmetic and copies ran while one was open for 1% of the time, Pallas kernels for 0%

commit v1 on v0

--- a/solution.py
+++ b/solution.py
@@ -142,9 +142,8 @@
     return 0.5 * signs_mm(signs_t, jnp.concatenate([top, bottom], axis=0))
 
 
-def signs_of(signs_ref, level):
-    signs = 2.0 * signs_ref[level].astype(F32) - 1.0
-    return signs.astype(jnp.bfloat16), signs.T.astype(jnp.bfloat16)
+def signs_of(signs_refs, level):
+    return signs_refs[0][level], signs_refs[1][level]
 
 
 def both_halves(own_ref, other_ref):
@@ -171,8 +170,64 @@
     return out
 
 
+def advance(mid, above, below, rate, bend_rate, force, live):
+    lane = lax.broadcasted_iota(jnp.int32, mid.shape, 1)
+    left = jnp.where(lane != 0, pltpu.roll(mid, 1, 1), 0.0)
+    right = jnp.where(lane != 127, pltpu.roll(mid, 127, 1), 0.0)
+    lap = (below + above) + (right + left) - 4.0 * mid
+    bend = jnp.tanh(mid)
+    return jnp.where(live, mid + (rate + bend_rate * (bend * bend)) * lap + force, mid)
+
+
+def spread_rows(at, rate, src, c_s, h_s, src_s):
+    at = slice(8 * at, 8 * at + 8)
+    c_s[at, :] = jnp.broadcast_to(rate, (8, 128))
+    h_s[at, :] = jnp.broadcast_to(0.5 * rate, (8, 128))
+    src_s[at, :] = jnp.broadcast_to(src, (8, 128))
+
+
+def inner_kernel(
+    count_ref, pick_ref, table_ref, x_ref, rate_ref, src_ref, bits_ref,
+    last_ref, prev_ref, amp_ref, sg_ref, sgt_ref, c_s, h_s, src_s, f_s,
+):
+    for level in range(5):
+        signs = 2.0 * bits_ref[level].astype(F32) - 1.0
+        sg_ref[level] = signs.astype(jnp.bfloat16)
+        sgt_ref[level] = signs.T.astype(jnp.bfloat16)
+    for r in range(16):
+        spread_rows(r, rate_ref[r : r + 1, :], src_ref[r : r + 1, :], c_s, h_s, src_s)
+    count = count_ref[0]
+    sub = lax.broadcasted_iota(jnp.int32, (8, 128), 0)
+
+    def block(b, carry):
+        rows = pl.ds(pl.multiple_of(b * 8, 8), 8)
+        amp = jnp.zeros((8, 128), F32)
+        for i in range(8):
+            amp = jnp.where(sub == i, 0.1 * table_ref[pick_ref[0, 8 * b + i]], amp)
+        amp_ref[rows, :] = amp
+        old = [x_ref[pl.ds(b * 128 + r, 8, stride=16), :] for r in range(16)]
+        for r in range(1, 15):
+            f_s[8 * r : 8 * r + 8, :] = amp * src_s[8 * r : 8 * r + 8, :]
+        for r in (0, 15):
+            last_ref[r, rows, :] = old[r]
+        for t in range(7):
+            new = list(old)
+            for r in range(t + 1, 15 - t):
+                at = slice(8 * r, 8 * r + 8)
+                new[r] = advance(
+                    old[r], old[r - 1], old[r + 1], c_s[at, :], h_s[at, :], f_s[at, :], t < count
+                )
+            for r in (t + 1, 14 - t):
+                prev_ref[r, rows, :] = old[r]
+                last_ref[r, rows, :] = new[r]
+            old = new
+        return carry
+
+    lax.fori_loop(0, 16, block, 0)
+
+
 def flow_kernel(
-    count_ref, x_ref, bef_ref, aft_ref, rate_ref, src_ref, amp_ref, signs_ref,
+    count_ref, last_ref, prev_ref, bef_ref, aft_ref, rate_ref, src_ref, amp_ref, sgt_ref,
     yt_ref, d0, d1, d2, d3, c_s, h_s, src_s, f_s, field_s, s_s,
 ):
     for r in range(32):
@@ -182,45 +237,38 @@
             rate, src = rate_ref[r - 8 : r - 7, :], src_ref[r - 8 : r - 7, :]
         else:
             rate, src = aft_ref[1000 + r : 1001 + r, :], aft_ref[1008 + r : 1009 + r, :]
-        at = slice(8 * r, 8 * r + 8)
-        c_s[at, :] = jnp.broadcast_to(rate, (8, 128))
-        h_s[at, :] = jnp.broadcast_to(0.5 * rate, (8, 128))
-        src_s[at, :] = jnp.broadcast_to(src, (8, 128))
+        spread_rows(r, rate, src, c_s, h_s, src_s)
     count = count_ref[0]
-    lane = lax.broadcasted_iota(jnp.int32, (8, 128), 1)
-    not_first = lane != 0
-    not_last = lane != 127
 
     def block(b, carry):
-        amp = amp_ref[pl.ds(pl.multiple_of(b * 8, 8), 8), :]
-        old = []
-        for r in range(32):
-            if r < 8:
-                old.append(bef_ref[pl.ds(b * 64 + r, 8, stride=8), :])
-            elif r < 24:
-                old.append(x_ref[pl.ds(b * 128 + (r - 8), 8, stride=16), :])
-            else:
-                old.append(aft_ref[pl.ds(b * 64 + (r - 24), 8, stride=8), :])
+        rows = pl.ds(pl.multiple_of(b * 8, 8), 8)
+        amp = amp_ref[rows, :]
+        for r in range(1, 31):
             f_s[8 * r : 8 * r + 8, :] = amp * src_s[8 * r : 8 * r + 8, :]
+        low = {r - 8: bef_ref[pl.ds(b * 64 + r, 8, stride=8), :] for r in range(8)}
+        high = {r + 16: aft_ref[pl.ds(b * 64 + r, 8, stride=8), :] for r in range(8)}
         for t in range(STEPS):
-            live = t < count
-            new = list(old)
-            for r in range(t + 1, 31 - t):
-                at = slice(8 * r, 8 * r + 8)
-                mid = old[r]
-                left = jnp.where(not_first, pltpu.roll(mid, 1, 1), 0.0)
-                right = jnp.where(not_last, pltpu.roll(mid, 127, 1), 0.0)
-                lap = (old[r + 1] + old[r - 1]) + (right + left) - 4.0 * mid
-                bend = jnp.tanh(mid)
-                val = mid + (c_s[at, :] + h_s[at, :] * (bend * bend)) * lap + f_s[at, :]
-                new[r] = jnp.where(live, val, mid)
-            old = new
-        for r in range(16):
-            field_s[r, pl.ds(pl.multiple_of(b * 8, 8), 8), :] = old[8 + r]
+            low[t] = last_ref[t, rows, :]
+            high[15 - t] = last_ref[15 - t, rows, :]
+            low[t + 1] = last_ref[8, rows, :] if t == 7 else prev_ref[t + 1, rows, :]
+            high[14 - t] = last_ref[7, rows, :] if t == 7 else prev_ref[14 - t, rows, :]
+            sides = []
+            for old, first in ((low, t - 7), (high, 15 - t)):
+                new = {}
+                for r in range(first, first + 8):
+                    at = slice(8 * r + 64, 8 * r + 72)
+                    new[r] = advance(
+                        old[r], old[r - 1], old[r + 1], c_s[at, :], h_s[at, :], f_s[at, :], t < count
+                    )
+                sides.append(new)
+            low, high = sides
+        for r in range(8):
+            field_s[r, rows, :] = low[r]
+            field_s[8 + r, rows, :] = high[8 + r]
         return carry
 
     lax.fori_loop(0, 16, block, 0)
-    _, signs_t = signs_of(signs_ref, 0)
+    signs_t = sgt_ref[0]
     yt = jnp.zeros((64, 128), F32)
     for q in range(4):
         parts = []
@@ -262,16 +310,16 @@
     send_ref[...] = pay_s[1 - core]
 
 
-def leaf_kernel(own_ref, other_ref, signs_ref, out_ref):
+def leaf_kernel(own_ref, other_ref, sg_ref, sgt_ref, out_ref):
     low, high = both_halves(own_ref, other_ref)
-    signs, _ = signs_of(signs_ref, 0)
+    signs, _ = signs_of((sg_ref, sgt_ref), 0)
     (b,), (moment,) = compress([jnp.concatenate([low[:32], high[:32]], axis=0)], signs)
     out_ref[0:64] = jnp.concatenate([b, gram_of(b, moment)], axis=1)
     out_ref[64:88] = low[32:]
     out_ref[88:112] = high[32:]
 
 
-def middle_kernel(p0, p1, p2, p3, all_ref, signs_ref, out_ref, pay_s, z_s):
+def middle_kernel(p0, p1, p2, p3, all_ref, sg_ref, sgt_ref, out_ref, pay_s, z_s):
     place = lax.axis_index("y")
     for d, ref in enumerate((p0, p1, p2, p3)):
         pay_s[rest_of(place, -d)] = ref[...]
@@ -281,7 +329,7 @@
     grams = [pay_s[g, 0:64][:, 64:] for g in range(4)]
     inside = z_s[0:64]
     crosses = [mm_nt(mm(bs[0], inside[:, :64]), bs[1]), mm_nt(mm(bs[2], inside[:, 64:]), bs[3])]
-    signs, signs_t = signs_of(signs_ref, 1)
+    signs, signs_t = signs_of((sg_ref, sgt_ref), 1)
     yts = [
         sketch_of_pair(grams[2 * n], crosses[n], grams[2 * n + 1], signs_t) for n in range(2)
     ]
@@ -293,7 +341,7 @@
         high = signs_mm(signs_t[:, 64:], bs[2 * n + 1])
         ws.append(mm(ups[n], jnp.concatenate([low, high], axis=1)) * half)
     cross = mm_nt(mm(ws[0], z_s[64:192]), ws[1])
-    signs, signs_t = signs_of(signs_ref, 2)
+    signs, signs_t = signs_of((sg_ref, sgt_ref), 2)
     first, second = (gram_of(u, m) for u, m in zip(ups, moments))
     (b,), (moment,) = compress([sketch_of_pair(first, cross, second, signs_t)], signs)
     low = signs_mm(signs_t[:, :64], ws[0])
@@ -307,11 +355,11 @@
     out_ref[256:288] = jnp.concatenate([gram[:32], gram[32:]], axis=1)
 
 
-def upper_kernel(r0, r1, r2, r3, signs_ref, s_ref, keep_ref, send_ref, all_s, pay_s):
+def upper_kernel(r0, r1, r2, r3, sg_ref, sgt_ref, s_ref, keep_ref, send_ref, all_s, pay_s):
     place = lax.axis_index("x")
     for d, ref in enumerate((r0, r1, r2, r3)):
         all_s[rest_of(place, -d)] = ref[0:256]
-    _, signs_t = signs_of(signs_ref, 3)
+    _, signs_t = signs_of((sg_ref, sgt_ref), 3)
     slabs = [jnp.zeros((64, 64), F32)] * 3
     for q in range(4):
         at = slice(64 * q, 64 * q + 64)
@@ -334,7 +382,7 @@
     send_ref[...] = pay_s[1 - core]
 
 
-def last_kernel(own_ref, other_ref, r0, r1, r2, r3, s_ref, signs_ref, out_ref, gram_s):
+def last_kernel(own_ref, other_ref, r0, r1, r2, r3, s_ref, sg_ref, sgt_ref, out_ref, gram_s):
     place = lax.axis_index("x")
     for d, ref in enumerate((r0, r1, r2, r3)):
         gram_s[rest_of(place, -d)] = ref[256:288]
@@ -347,7 +395,7 @@
     inside = jnp.concatenate(
         [low[32:, :64], low[32:, 64:], high[32:, :64], high[32:, 64:]], axis=0
     )
-    signs, signs_t = signs_of(signs_ref, 3)
+    signs, signs_t = signs_of((sg_ref, sgt_ref), 3)
     yts = [
         sketch_of_pair(grams[2 * n], pairs[:, 64 * n : 64 * n + 64], grams[2 * n + 1], signs_t)
         for n in range(2)
@@ -355,7 +403,7 @@
     bs, moments = compress(yts, signs)
     cross = mm_nt(mm(bs[0], inside), bs[1])
     first, second = (gram_of(u, m) for u, m in zip(bs, moments))
-    signs, signs_t = signs_of(signs_ref, 4)
+    signs, signs_t = signs_of((sg_ref, sgt_ref), 4)
     (b,), _ = compress([sketch_of_pair(first, cross, second, signs_t)], signs)
     lower = signs_mm(signs_t[:, :64], bs[0])
     upper = signs_mm(signs_t[:, 64:], bs[1])
@@ -370,7 +418,7 @@
     out_ref[...] = mm(w, mine)
 
 
-def call(kernel, out_shapes, smem, *args, scratch=()):
+def call(kernel, out_shapes, smem, *args, scratch=(), limit=16, cost=None):
     specs = [SMEM] * smem + [VMEM] * (len(args) - smem)
     return pl.pallas_call(
         kernel,
@@ -378,6 +426,8 @@
         in_specs=specs,
         out_specs=jax.tree.map(lambda _: VMEM, out_shapes),
         scratch_shapes=list(scratch),
+        cost_estimate=cost,
+        compiler_params=pltpu.CompilerParams(vmem_limit_bytes=limit << 20),
     )(*args)
 
 
@@ -407,11 +457,6 @@
 def per_device(init_state, coef, source, amplitudes, sample_idx, step_counts, sketch_signs):
     field = init_state[0]
     rate = coef[0]
-    table = amplitudes.shape[0]
-    picks = sample_idx[0][:, None] == jnp.arange(table, dtype=jnp.int32)[None, :]
-    amp = 0.1 * jnp.sum(jnp.where(picks, amplitudes[None, :], 0.0), axis=1)
-    amp = jnp.broadcast_to(amp[:, None], (128, 128))
-
     slabs = ("z", "core")
     n = lax.axis_size(slabs)
     up = [(i, i + 1) for i in range(n - 1)]
@@ -421,18 +466,39 @@
     bef = lax.ppermute(tail, slabs, up)
     aft = lax.ppermute(head, slabs, down)
 
+    last, prev, amp, signs, signs_t = call(
+        inner_kernel,
+        (
+            shape(16, 128, 128),
+            shape(16, 128, 128),
+            shape(128, 128),
+            jax.ShapeDtypeStruct((5, 128, 64), jnp.bfloat16),
+            jax.ShapeDtypeStruct((5, 64, 128), jnp.bfloat16),
+        ),
+        3,
+        step_counts,
+        sample_idx,
+        amplitudes,
+        field.reshape(2048, 128),
+        rate,
+        source,
+        sketch_signs,
+        scratch=[pltpu.VMEM((128, 128), F32)] * 4,
+        cost=pl.CostEstimate(flops=4_000_000_000, bytes_accessed=4_000_000, transcendentals=0),
+    )
     yt, *chunks = call(
         flow_kernel,
         (shape(64, 128),) + (shape(4, 64, 128),) * 4,
         1,
         step_counts,
-        field.reshape(2048, 128),
+        last,
+        prev,
         bef.reshape(1040, 128),
         aft.reshape(1040, 128),
         rate,
         source,
         amp,
-        sketch_signs,
+        signs_t,
         scratch=[pltpu.VMEM((256, 128), F32)] * 4
         + [pltpu.VMEM((16, 128, 128), F32), pltpu.VMEM((4, 4, 64, 128), F32)],
     )
@@ -448,14 +514,15 @@
     half = keep + shift(send, "core", 1)
     quarters = [half[32:56]] + [shift(half[32 + 24 * d : 56 + 24 * d], "y", d) for d in (1, 2, 3)]
     own = sum_over(jnp.concatenate([half[:32], total(quarters)], axis=0), "z")
-    leaf = call(leaf_kernel, shape(112, 128), 0, own, shift(own, "core", 1), sketch_signs)
+    leaf = call(leaf_kernel, shape(112, 128), 0, own, shift(own, "core", 1), signs, signs_t)
     piece = call(
         middle_kernel,
         shape(288, 128),
         0,
         *from_ring(leaf, "y"),
         sketches,
-        sketch_signs,
+        signs,
+        signs_t,
         scratch=[pltpu.VMEM((4, 112, 128), F32), pltpu.VMEM((192, 128), F32)],
     )
     pieces = from_ring(piece, "x")
@@ -464,7 +531,8 @@
         (shape(2, 4, 64, 128), shape(48, 128), shape(48, 128)),
         0,
         *pieces,
-        sketch_signs,
+        signs,
+        signs_t,
         scratch=[pltpu.VMEM((4, 256, 128), F32), pltpu.VMEM((2, 48, 128), F32)],
     )
     half = keep + shift(send, "core", 1)
@@ -477,7 +545,8 @@
         shift(own, "core", 1),
         *pieces,
         s,
-        sketch_signs,
+        signs,
+        signs_t,
         scratch=[pltpu.VMEM((4, 32, 128), F32)],
     )
     return out.reshape(64, 16, 8)

time: 160 us -> 144 us (0.900)
  waiting for transfers between devices: 34.8 us -> 29 us
  local copies, waits for them, and re-layouts: 9.1 us -> 3.61 us
  Pallas kernels: 53.3 us -> 50 us
  blocking collectives: 30.3 us -> 28.6 us
    ppermute x1, waiting for transfers between devices: 4.58 us -> 0.01 us  [per_device(): aft = lax.ppermute(head, slabs, down)]
    unnamed x39 -> x13, local copies, waits for them, and re-layouts: 4.75 us -> 0.84 us
    pallas_call x6 -> x7, Pallas kernels: 53.3 us -> 50 us  [call(): pl.pallas_call(kernel, out_shape=out_shapes, in_specs=specs, out_specs=ja...]
    ppermute x1, waiting for transfers between devices: 1.75 us -> 0.01 us  [per_device(): bef = lax.ppermute(tail, slabs, up)]
    all_to_all x2, blocking collectives: 30.3 us -> 28.6 us  [sum_over(): return lax.all_to_all(sent, axis, 0, 0, tiled=True).sum(axis=0)]
  transfers between devices with their start and end apart: 21 -> 21, of which waited for: 20 -> 18; matrix products, arithmetic and copies ran while one was open for 1% -> 1% of each run, Pallas kernels for 0% -> 6%
where the time goes in v1:
time: 144 us
  Pallas kernels  50 us (35%)
  starting transfers between devices  30.7 us (21%)
  waiting for transfers between devices  29 us (20%)
  blocking collectives  28.6 us (20%)
  local copies, waits for them, and re-layouts  3.61 us (3%)
    pallas_call x7, Pallas kernels, call(): pl.pallas_call(kernel, out_shape=out_shapes, in_specs=specs, out_specs=ja...  50 us
    ppermute x19, waiting for transfers between devices, shift(): return lax.ppermute(value, axis, [(i, (i + by) % n) for i in range(n)])  29 us
    all_to_all x2, blocking collectives, sum_over(): return lax.all_to_all(sent, axis, 0, 0, tiled=True).sum(axis=0)  28.6 us
    ppermute x19, starting transfers between devices, shift(): return lax.ppermute(value, axis, [(i, (i + by) % n) for i in range(n)])  23.8 us
    ppermute x1, starting transfers between devices, per_device(): bef = lax.ppermute(tail, slabs, up)  5.06 us
  transfers between devices with their start and end apart: 21, of which 18 were waited for; matrix products, arithmetic and copies ran while one was open for 1% of the time, Pallas kernels for 6%

profile of v1, /device:TPU:1, one launch (start us, length us, event | category | flops | bytes accessed | tf_op | source)
XLA Modules:
  0.0 143.8 jit_solution(18180351850361003970)
XLA Ops:
  0.0 0.7 fusion.3
  0.7 1.3 fusion.1
  2.0 0.0 copy-start.5
  2.1 0.0 copy-start
  2.1 5.1 %collective-permute-start = (f32[130,8,128]{2,1,0:T(8,128)S(1)}, f32[130,8,128]{2,1,0:T(8,128)S(1)}, u32[]{:S(2)}, u32[]{:S(2)}) collective-permute-start(f32[130,8,128]{2,1,0:T(8,128)S(1)} %pad_maximum_fusion), channel_id=1, source_target_pairs={{0,1},{1,2},{2,3},{3,4},{4,5},{5,6},{6,7},{7,8},{8,9},{9,10},{10,1... | collective-permute-start | bytes 1597448 | tf_op jit(solution)/shard_map/ppermute | solution.py:466
  7.1 0.8 pad_maximum_fusion.1
  8.0 1.9 %collective-permute-start.1 = (f32[130,8,128]{2,1,0:T(8,128)}, f32[130,8,128]{2,1,0:T(8,128)S(1)}, u32[]{:S(2)}, u32[]{:S(2)}) collective-permute-start(f32[130,8,128]{2,1,0:T(8,128)} %pad_maximum_fusion.1), channel_id=1, source_target_pairs={{1,0},{2,1},{3,2},{4,3},{5,4},{6,5},{7,6},{8,7},{9,8},{10,9},{11,1... | collective-permute-start | bytes 1597448 | tf_op jit(solution)/shard_map/ppermute | solution.py:467
  10.5 0.0 copy-start.1
  10.6 0.2 copy.12.bits_ref
  10.7 0.0 copy-start.3
  10.7 0.0 copy-start.4
  10.8 0.5 copy-done.1
  11.2 0.1 copy-done.3
  11.4 0.0 copy-done.4
  11.4 9.2 %shard_map.73 = (f32[16,128,128]{2,1,0:T(8,128)S(1)}, f32[16,128,128]{2,1,0:T(8,128)S(1)}, f32[128,128]{1,0:T(8,128)S(1)}, bf16[5,128,64]{2,1,0:T(8,128)(2,1)S(1)}, bf16[5,64,128]{2,1,0:T(8,128)(2,1)S(1)}) custom-call(s32[1]{0:T(128)S(6)} %copy.14.count_ref, s32[1,128]{1,0:T(1,128)S(1)} %copy-done.3, f32[64]{0:T(128)S(1)} %copy-done.4, ...), custom_call_target="tpu_custom_call" | custom-call | flops 4000000000 | bytes 4000000 | tf_op jit(solution)/shard_map/pallas_call | solution.py:423
  20.6 0.0 collective-permute-done
  20.6 0.0 collective-permute-done.1
  20.6 14.5 %shard_map.74 = (f32[64,128]{1,0:T(8,128)S(1)}, f32[4,64,128]{2,1,0:T(8,128)S(1)}, f32[4,64,128]{2,1,0:T(8,128)S(1)}, f32[4,64,128]{2,1,0:T(8,128)S(1)}, f32[4,64,128]{2,1,0:T(8,128)S(1)}) custom-call(s32[1]{0:T(128)S(6)} %copy.14.count_ref, f32[16,128,128]{2,1,0:T(8,128)S(1)} %get-tuple-element.21.last_ref, f32[16,128,128]{2,1,0:T(8,128)S(1)} %get-tuple-element.22.prev_ref, ...), custom_call_target="tpu_custom_call" | custom-call | tf_op jit(solution)/shard_map/pallas_call | solution.py:423
  35.1 1.4 collective-permute-start.2
  36.5 2.6 %collective-permute-start.3 = (f32[4,64,128]{2,1,0:T(8,128)S(1)}, f32[4,64,128]{2,1,0:T(8,128)S(1)}, u32[]{:S(2)}, u32[]{:S(2)}) collective-permute-start(f32[4,64,128]{2,1,0:T(8,128)S(1)} %get-tuple-element.28), channel_id=1, source_target_pairs={{0,32},{16,48},{32,0},{48,16},{1,33},{17,49},{33,1},{49,17},{2,34}... | collective-permute-start | bytes 393224 | tf_op jit(solution)/shard_map/ppermute | solution.py:440
  39.1 1.1 collective-permute-start.4
  40.2 3.7 %collective-permute-done.2.r1 = f32[4,64,128]{2,1,0:T(8,128)S(1)} collective-permute-done((f32[4,64,128]{2,1,0:T(8,128)S(1)}, f32[4,64,128]{2,1,0:T(8,128)S(1)}, u32[]{:S(2)}, u32[]{:S(2)}) %collective-permute-start.2) | collective-permute-done | bytes 131104 | tf_op jit(solution)/shard_map/ppermute | solution.py:440
  43.9 0.0 collective-permute-done.3.r2
  43.9 0.9 collective-permute-done.4.r3
  44.7 1.9 %shard_map.75 = (f32[128,128]{1,0:T(8,128)S(1)}, f32[128,128]{1,0:T(8,128)S(1)}, f32[4,4,64,128]{3,2,1,0:T(8,128)S(1)}) custom-call(f32[64,128]{1,0:T(8,128)S(1)} %get-tuple-element.25.yt_ref, f32[4,64,128]{2,1,0:T(8,128)S(1)} %get-tuple-element.26.r0, f32[4,64,128]{2,1,0:T(8,128)S(1)} %collective-permute-done.2.r1, ...), custom_call_target="tpu_custom_call" | custom-call | tf_op jit(solution)/shard_map/pallas_call | solution.py:423
  46.6 0.3 collective-permute-start.5
  46.9 1.0 collective-permute-done.5
  48.0 2.7 %collective-permute-start.8 = (f32[24,128]{1,0:T(8,128)S(1)}, f32[24,128]{1,0:T(8,128)S(1)}, u32[]{:S(2)}, u32[]{:S(2)}) collective-permute-start(f32[24,128]{1,0:T(8,128)S(1)} %get-tuple-element.39), channel_id=1, source_target_pairs={{0,48},{16,0},{32,16},{48,32},{1,49},{17,1},{33,17},{49,33},{2,50}... | collective-permute-start | bytes 36872 | tf_op jit(solution)/shard_map/ppermute | solution.py:440
  50.7 0.5 collective-permute-start.7
  51.2 0.1 collective-permute-start.6
  51.4 0.2 collective-permute-done.8
  51.5 3.2 %collective-permute-done.7 = f32[24,128]{1,0:T(8,128)S(1)} collective-permute-done((f32[24,128]{1,0:T(8,128)S(1)}, f32[24,128]{1,0:T(8,128)S(1)}, u32[]{:S(2)}, u32[]{:S(2)}) %collective-permute-start.7) | collective-permute-done | bytes 12320 | tf_op jit(solution)/shard_map/ppermute | solution.py:440
  54.7 0.2 collective-permute-done.6
  55.0 17.6 %all_to_all.10 = f32[8,56,128]{2,1,0:T(8,128)S(1)} all-to-all(f32[8,56,128]{2,1,0:T(8,128)S(1)} %broadcast_in_dim.10), channel_id=1, replica_groups=mesh['x'=4,'y'=4,'z'=8,'core'=2] {'z'}, dimensions={0} | all-to-all | bytes 458752 | tf_op jit(solution)/shard_map/all_to_all | solution.py:454
  72.6 3.5 %collective-permute-start.9 = (f32[56,128]{1,0:T(8,128)S(1)}, f32[56,128]{1,0:T(8,128)S(1)}, u32[]{:S(2)}, u32[]{:S(2)}) collective-permute-start(f32[56,128]{1,0:T(8,128)S(1)} %reduce_sum.18.own_ref), channel_id=1, source_target_pairs={{0,1},{1,0},{2,3},{3,2},{4,5},{5,4},{6,7},{7,6},{8,9},{9,8},{10,11... | collective-permute-start | bytes 86024 | tf_op jit(solution)/shard_map/ppermute | solution.py:440
  76.1 0.9 collective-permute-done.9.other_ref
  77.0 3.9 %shard_map.76.p0 = f32[112,128]{1,0:T(8,128)S(1)} custom-call(f32[56,128]{1,0:T(8,128)S(1)} %reduce_sum.18.own_ref, f32[56,128]{1,0:T(8,128)S(1)} %collective-permute-done.9.other_ref, bf16[5,128,64]{2,1,0:T(8,128)(2,1)S(1)} %get-tuple-element.32.sg_ref, bf16[5,64,128]{2,1,0:T(8,128)(2,1)S(1)} %get-tuple-element.24.sgt_ref), custom_call_target="tpu_custom_call" | custom-call | tf_op jit(solution)/shard_map/pallas_call | solution.py:423
  80.8 0.5 collective-permute-start.12
  81.3 1.2 collective-permute-start.11
  82.5 0.8 collective-permute-start.10
  83.3 0.7 collective-permute-done.12.p3
  83.9 1.9 %collective-permute-done.11.p2 = f32[112,128]{1,0:T(8,128)S(1)} collective-permute-done((f32[112,128]{1,0:T(8,128)S(1)}, f32[112,128]{1,0:T(8,128)S(1)}, u32[]{:S(2)}, u32[]{:S(2)}) %collective-permute-start.11) | collective-permute-done | bytes 57376 | tf_op jit(solution)/shard_map/ppermute | solution.py:440
  85.9 1.9 %collective-permute-done.10.p1 = f32[112,128]{1,0:T(8,128)S(1)} collective-permute-done((f32[112,128]{1,0:T(8,128)S(1)}, f32[112,128]{1,0:T(8,128)S(1)}, u32[]{:S(2)}, u32[]{:S(2)}) %collective-permute-start.10) | collective-permute-done | bytes 57376 | tf_op jit(solution)/shard_map/ppermute | solution.py:440
  87.8 10.2 %shard_map.77.r0 = f32[288,128]{1,0:T(8,128)S(1)} custom-call(f32[112,128]{1,0:T(8,128)S(1)} %shard_map.76.p0, f32[112,128]{1,0:T(8,128)S(1)} %collective-permute-done.10.p1, f32[112,128]{1,0:T(8,128)S(1)} %collective-permute-done.11.p2, f32[112,128]{1,0:T(8,128)S(1)} %collective-permute-done.12.p3, f32[4,4,64,128]{3,2,1,0:T(8,128)S(1)} %get-tuple-element.33.all_ref, ...), custom_call_target="tpu_custom_call" | custom-call | tf_op jit(solution)/shard_map/pallas_call | solution.py:423
  98.0 2.8 %collective-permute-start.15 = (f32[288,128]{1,0:T(8,128)S(1)}, f32[288,128]{1,0:T(8,128)S(1)}, u32[]{:S(2)}, u32[]{:S(2)}) collective-permute-start(f32[288,128]{1,0:T(8,128)S(1)} %shard_map.77.r0), channel_id=1, source_target_pairs={{0,192},{64,0},{128,64},{192,128},{1,193},{65,1},{129,65},{193,129... | collective-permute-start | bytes 442376 | tf_op jit(solution)/shard_map/ppermute | solution.py:440
  100.8 0.5 collective-permute-start.14
  101.3 0.6 collective-permute-start.13
  101.9 2.2 %collective-permute-done.15.r3 = f32[288,128]{1,0:T(8,128)S(1)} collective-permute-done((f32[288,128]{1,0:T(8,128)S(1)}, f32[288,128]{1,0:T(8,128)S(1)}, u32[]{:S(2)}, u32[]{:S(2)}) %collective-permute-start.15) | collective-permute-done | bytes 147488 | tf_op jit(solution)/shard_map/ppermute | solution.py:440
  104.1 2.3 %collective-permute-done.14.r2 = f32[288,128]{1,0:T(8,128)S(1)} collective-permute-done((f32[288,128]{1,0:T(8,128)S(1)}, f32[288,128]{1,0:T(8,128)S(1)}, u32[]{:S(2)}, u32[]{:S(2)}) %collective-permute-start.14) | collective-permute-done | bytes 147488 | tf_op jit(solution)/shard_map/ppermute | solution.py:440
  106.4 4.7 %collective-permute-done.13.r1 = f32[288,128]{1,0:T(8,128)S(1)} collective-permute-done((f32[288,128]{1,0:T(8,128)S(1)}, f32[288,128]{1,0:T(8,128)S(1)}, u32[]{:S(2)}, u32[]{:S(2)}) %collective-permute-start.13) | collective-permute-done | bytes 147488 | tf_op jit(solution)/shard_map/ppermute | solution.py:440
  111.0 1.1 shard_map.78
  112.1 0.7 collective-permute-start.16
  112.9 0.8 collective-permute-done.16
  113.7 0.4 collective-permute-start.19
  114.1 0.5 collective-permute-start.18
  114.6 0.6 collective-permute-start.17
  115.2 1.2 collective-permute-done.19
  116.4 1.9 %collective-permute-done.18 = f32[48,128]{1,0:T(8,128)S(1)} collective-permute-done((f32[48,128]{1,0:T(8,128)S(1)}, f32[48,128]{1,0:T(8,128)S(1)}, u32[]{:S(2)}, u32[]{:S(2)}) %collective-permute-start.18) | collective-permute-done | bytes 24608 | tf_op jit(solution)/shard_map/ppermute | solution.py:440
  118.3 0.5 collective-permute-done.17
  118.8 11.1 %all_to_all.11 = f32[8,48,128]{2,1,0:T(8,128)S(1)} all-to-all(f32[8,48,128]{2,1,0:T(8,128)S(1)} %broadcast_in_dim.11), channel_id=1, replica_groups=mesh['x'=4,'y'=4,'z'=8,'core'=2] {'z'}, dimensions={0} | all-to-all | bytes 393216 | tf_op jit(solution)/shard_map/all_to_all | solution.py:454
  129.9 3.0 %collective-permute-start.20 = (f32[48,128]{1,0:T(8,128)S(1)}, f32[48,128]{1,0:T(8,128)S(1)}, u32[]{:S(2)}, u32[]{:S(2)}) collective-permute-start(f32[48,128]{1,0:T(8,128)S(1)} %reduce_sum.19.own_ref), channel_id=1, source_target_pairs={{0,1},{1,0},{2,3},{3,2},{4,5},{5,4},{6,7},{7,6},{8,9},{9,8},{10,11... | collective-permute-start | bytes 73736 | tf_op jit(solution)/shard_map/ppermute | solution.py:440
  132.9 0.8 collective-permute-done.20.other_ref
  133.8 9.3 %shard_map.79 = f32[64,128]{1,0:T(8,128)S(1)} custom-call(f32[48,128]{1,0:T(8,128)S(1)} %reduce_sum.19.own_ref, f32[48,128]{1,0:T(8,128)S(1)} %collective-permute-done.20.other_ref, f32[288,128]{1,0:T(8,128)S(1)} %shard_map.77.r0, f32[288,128]{1,0:T(8,128)S(1)} %collective-permute-done.13.r1, f32[288,128]{1,0:T(8,128)S(1)} %collective-permute-done.14.r2, ...), custom_call_target="tpu_custom_call" | custom-call | tf_op jit(solution)/shard_map/pallas_call | solution.py:423
  143.0 0.7 copy.13
  (17 shorter events, 0.2 us)
Async XLA Ops:
  0.0 0.7 copy-start.2
  2.0 8.5 %copy-start.5 = (s32[5,128,64]{1,2,0:T(8,128)S(1)}, s32[5,128,64]{1,2,0:T(8,128)}, u32[]{:S(2)}) copy-start(s32[5,128,64]{1,2,0:T(8,128)} %param.13) | copy-start | bytes 491524
  2.1 8.7 %copy-start = (f32[1,128,16,128]{3,2,1,0:T(8,128)S(1)}, f32[1,128,16,128]{3,2,1,0:T(8,128)}, u32[]{:S(2)}) copy-start(f32[1,128,16,128]{3,2,1,0:T(8,128)} %param.7) | copy-start | bytes 3145732
  2.1 18.5 %collective-permute-start = (f32[130,8,128]{2,1,0:T(8,128)S(1)}, f32[130,8,128]{2,1,0:T(8,128)S(1)}, u32[]{:S(2)}, u32[]{:S(2)}) collective-permute-start(f32[130,8,128]{2,1,0:T(8,128)S(1)} %pad_maximum_fusion), channel_id=1, source_target_pairs={{0,1},{1,2},{2,3},{3,4},{4,5},{5,6},{6,7},{7,8},{8,9},{9,10},{10,1... | collective-permute-start | bytes 1597448 | tf_op jit(solution)/shard_map/ppermute | solution.py:466
  8.0 12.6 %collective-permute-start.1 = (f32[130,8,128]{2,1,0:T(8,128)}, f32[130,8,128]{2,1,0:T(8,128)S(1)}, u32[]{:S(2)}, u32[]{:S(2)}) collective-permute-start(f32[130,8,128]{2,1,0:T(8,128)} %pad_maximum_fusion.1), channel_id=1, source_target_pairs={{1,0},{2,1},{3,2},{4,3},{5,4},{6,5},{7,6},{8,7},{9,8},{10,9},{11,1... | collective-permute-start | bytes 1597448 | tf_op jit(solution)/shard_map/ppermute | solution.py:467
  10.5 0.7 copy-start.1
  10.7 0.7 copy-start.3
  10.7 0.7 copy-start.4
  35.1 8.7 %collective-permute-start.2 = (f32[4,64,128]{2,1,0:T(8,128)S(1)}, f32[4,64,128]{2,1,0:T(8,128)S(1)}, u32[]{:S(2)}, u32[]{:S(2)}) collective-permute-start(f32[4,64,128]{2,1,0:T(8,128)S(1)} %get-tuple-element.27), channel_id=1, source_target_pairs={{0,16},{16,32},{32,48},{48,0},{1,17},{17,33},{33,49},{49,1},{2,18}... | collective-permute-start | bytes 393224 | tf_op jit(solution)/shard_map/ppermute | solution.py:440
  36.5 7.4 %collective-permute-start.3 = (f32[4,64,128]{2,1,0:T(8,128)S(1)}, f32[4,64,128]{2,1,0:T(8,128)S(1)}, u32[]{:S(2)}, u32[]{:S(2)}) collective-permute-start(f32[4,64,128]{2,1,0:T(8,128)S(1)} %get-tuple-element.28), channel_id=1, source_target_pairs={{0,32},{16,48},{32,0},{48,16},{1,33},{17,49},{33,1},{49,17},{2,34}... | collective-permute-start | bytes 393224 | tf_op jit(solution)/shard_map/ppermute | solution.py:440
  39.1 5.6 %collective-permute-start.4 = (f32[4,64,128]{2,1,0:T(8,128)S(1)}, f32[4,64,128]{2,1,0:T(8,128)S(1)}, u32[]{:S(2)}, u32[]{:S(2)}) collective-permute-start(f32[4,64,128]{2,1,0:T(8,128)S(1)} %get-tuple-element.29), channel_id=1, source_target_pairs={{0,48},{16,0},{32,16},{48,32},{1,49},{17,1},{33,17},{49,33},{2,50}... | collective-permute-start | bytes 393224 | tf_op jit(solution)/shard_map/ppermute | solution.py:440
  46.6 1.3 collective-permute-start.5
  48.0 3.5 %collective-permute-start.8 = (f32[24,128]{1,0:T(8,128)S(1)}, f32[24,128]{1,0:T(8,128)S(1)}, u32[]{:S(2)}, u32[]{:S(2)}) collective-permute-start(f32[24,128]{1,0:T(8,128)S(1)} %get-tuple-element.39), channel_id=1, source_target_pairs={{0,48},{16,0},{32,16},{48,32},{1,49},{17,1},{33,17},{49,33},{2,50}... | collective-permute-start | bytes 36872 | tf_op jit(solution)/shard_map/ppermute | solution.py:440
  50.7 4.0 %collective-permute-start.7 = (f32[24,128]{1,0:T(8,128)S(1)}, f32[24,128]{1,0:T(8,128)S(1)}, u32[]{:S(2)}, u32[]{:S(2)}) collective-permute-start(f32[24,128]{1,0:T(8,128)S(1)} %get-tuple-element.40), channel_id=1, source_target_pairs={{0,32},{16,48},{32,0},{48,16},{1,33},{17,49},{33,1},{49,17},{2,34}... | collective-permute-start | bytes 36872 | tf_op jit(solution)/shard_map/ppermute | solution.py:440
  51.2 3.8 %collective-permute-start.6 = (f32[24,128]{1,0:T(8,128)S(1)}, f32[24,128]{1,0:T(8,128)S(1)}, u32[]{:S(2)}, u32[]{:S(2)}) collective-permute-start(f32[24,128]{1,0:T(8,128)S(1)} %get-tuple-element.41), channel_id=1, source_target_pairs={{0,16},{16,32},{32,48},{48,0},{1,17},{17,33},{33,49},{49,1},{2,18}... | collective-permute-start | bytes 36872 | tf_op jit(solution)/shard_map/ppermute | solution.py:440
  72.6 4.4 %collective-permute-start.9 = (f32[56,128]{1,0:T(8,128)S(1)}, f32[56,128]{1,0:T(8,128)S(1)}, u32[]{:S(2)}, u32[]{:S(2)}) collective-permute-start(f32[56,128]{1,0:T(8,128)S(1)} %reduce_sum.18.own_ref), channel_id=1, source_target_pairs={{0,1},{1,0},{2,3},{3,2},{4,5},{5,4},{6,7},{7,6},{8,9},{9,8},{10,11... | collective-permute-start | bytes 86024 | tf_op jit(solution)/shard_map/ppermute | solution.py:440
  80.8 3.1 %collective-permute-start.12 = (f32[112,128]{1,0:T(8,128)S(1)}, f32[112,128]{1,0:T(8,128)S(1)}, u32[]{:S(2)}, u32[]{:S(2)}) collective-permute-start(f32[112,128]{1,0:T(8,128)S(1)} %shard_map.76.p0), channel_id=1, source_target_pairs={{0,48},{16,0},{32,16},{48,32},{1,49},{17,1},{33,17},{49,33},{2,50}... | collective-permute-start | bytes 172040 | tf_op jit(solution)/shard_map/ppermute | solution.py:440
  81.3 4.5 %collective-permute-start.11 = (f32[112,128]{1,0:T(8,128)S(1)}, f32[112,128]{1,0:T(8,128)S(1)}, u32[]{:S(2)}, u32[]{:S(2)}) collective-permute-start(f32[112,128]{1,0:T(8,128)S(1)} %shard_map.76.p0), channel_id=1, source_target_pairs={{0,32},{16,48},{32,0},{48,16},{1,33},{17,49},{33,1},{49,17},{2,34}... | collective-permute-start | bytes 172040 | tf_op jit(solution)/shard_map/ppermute | solution.py:440
  82.5 5.3 %collective-permute-start.10 = (f32[112,128]{1,0:T(8,128)S(1)}, f32[112,128]{1,0:T(8,128)S(1)}, u32[]{:S(2)}, u32[]{:S(2)}) collective-permute-start(f32[112,128]{1,0:T(8,128)S(1)} %shard_map.76.p0), channel_id=1, source_target_pairs={{0,16},{16,32},{32,48},{48,0},{1,17},{17,33},{33,49},{49,1},{2,18}... | collective-permute-start | bytes 172040 | tf_op jit(solution)/shard_map/ppermute | solution.py:440
  98.0 6.1 %collective-permute-start.15 = (f32[288,128]{1,0:T(8,128)S(1)}, f32[288,128]{1,0:T(8,128)S(1)}, u32[]{:S(2)}, u32[]{:S(2)}) collective-permute-start(f32[288,128]{1,0:T(8,128)S(1)} %shard_map.77.r0), channel_id=1, source_target_pairs={{0,192},{64,0},{128,64},{192,128},{1,193},{65,1},{129,65},{193,129... | collective-permute-start | bytes 442376 | tf_op jit(solution)/shard_map/ppermute | solution.py:440
  100.8 5.6 %collective-permute-start.14 = (f32[288,128]{1,0:T(8,128)S(1)}, f32[288,128]{1,0:T(8,128)S(1)}, u32[]{:S(2)}, u32[]{:S(2)}) collective-permute-start(f32[288,128]{1,0:T(8,128)S(1)} %shard_map.77.r0), channel_id=1, source_target_pairs={{0,128},{64,192},{128,0},{192,64},{1,129},{65,193},{129,1},{193,65... | collective-permute-start | bytes 442376 | tf_op jit(solution)/shard_map/ppermute | solution.py:440
  101.3 9.7 %collective-permute-start.13 = (f32[288,128]{1,0:T(8,128)S(1)}, f32[288,128]{1,0:T(8,128)S(1)}, u32[]{:S(2)}, u32[]{:S(2)}) collective-permute-start(f32[288,128]{1,0:T(8,128)S(1)} %shard_map.77.r0), channel_id=1, source_target_pairs={{0,64},{64,128},{128,192},{192,0},{1,65},{65,129},{129,193},{193,1... | collective-permute-start | bytes 442376 | tf_op jit(solution)/shard_map/ppermute | solution.py:440
  112.1 1.6 %collective-permute-start.16 = (f32[48,128]{1,0:T(8,128)S(1)}, f32[48,128]{1,0:T(8,128)S(1)}, u32[]{:S(2)}, u32[]{:S(2)}) collective-permute-start(f32[48,128]{1,0:T(8,128)S(1)} %get-tuple-element.35), channel_id=1, source_target_pairs={{0,1},{1,0},{2,3},{3,2},{4,5},{5,4},{6,7},{7,6},{8,9},{9,8},{10,11... | collective-permute-start | bytes 73736 | tf_op jit(solution)/shard_map/ppermute | solution.py:440
  113.7 2.7 %collective-permute-start.19 = (f32[48,128]{1,0:T(8,128)S(1)}, f32[48,128]{1,0:T(8,128)S(1)}, u32[]{:S(2)}, u32[]{:S(2)}) collective-permute-start(f32[48,128]{1,0:T(8,128)S(1)} %add.28), channel_id=1, source_target_pairs={{0,48},{16,0},{32,16},{48,32},{1,49},{17,1},{33,17},{49,33},{2,50}... | collective-permute-start | bytes 73736 | tf_op jit(solution)/shard_map/ppermute | solution.py:440
  114.1 4.2 %collective-permute-start.18 = (f32[48,128]{1,0:T(8,128)S(1)}, f32[48,128]{1,0:T(8,128)S(1)}, u32[]{:S(2)}, u32[]{:S(2)}) collective-permute-start(f32[48,128]{1,0:T(8,128)S(1)} %add.28), channel_id=1, source_target_pairs={{0,32},{16,48},{32,0},{48,16},{1,33},{17,49},{33,1},{49,17},{2,34}... | collective-permute-start | bytes 73736 | tf_op jit(solution)/shard_map/ppermute | solution.py:440
  114.6 4.2 %collective-permute-start.17 = (f32[48,128]{1,0:T(8,128)S(1)}, f32[48,128]{1,0:T(8,128)S(1)}, u32[]{:S(2)}, u32[]{:S(2)}) collective-permute-start(f32[48,128]{1,0:T(8,128)S(1)} %add.28), channel_id=1, source_target_pairs={{0,16},{16,32},{32,48},{48,0},{1,17},{17,33},{33,49},{49,1},{2,18}... | collective-permute-start | bytes 73736 | tf_op jit(solution)/shard_map/ppermute | solution.py:440
  129.9 3.8 %collective-permute-start.20 = (f32[48,128]{1,0:T(8,128)S(1)}, f32[48,128]{1,0:T(8,128)S(1)}, u32[]{:S(2)}, u32[]{:S(2)}) collective-permute-start(f32[48,128]{1,0:T(8,128)S(1)} %reduce_sum.19.own_ref), channel_id=1, source_target_pairs={{0,1},{1,0},{2,3},{3,2},{4,5},{5,4},{6,7},{7,6},{8,9},{9,8},{10,11... | collective-permute-start | bytes 73736 | tf_op jit(solution)/shard_map/ppermute | solution.py:440

commit v2 on v1

--- a/solution.py
+++ b/solution.py
@@ -186,8 +186,57 @@
     src_s[at, :] = jnp.broadcast_to(src, (8, 128))
 
 
+def turned(vals):
+    sub = lax.broadcasted_iota(jnp.int32, vals[0].shape, 0)
+    out = list(vals)
+    for bit in (1, 2, 4):
+        low = (sub & bit) == 0
+        for i in range(8):
+            if i & bit:
+                continue
+            a, b = out[i], out[i | bit]
+            out[i] = jnp.where(low, a, pltpu.roll(b, bit, 0))
+            out[i | bit] = jnp.where(low, pltpu.roll(a, 8 - bit, 0), b)
+    return out
+
+
+def pack_kernel(x_ref, rate_ref, src_ref, head_ref, tail_ref, x_s, sems):
+    parts = [
+        pltpu.make_async_copy(
+            x_ref.at[pl.ds(512 * n, 512)], x_s.at[pl.ds(512 * n, 512)], sems.at[n]
+        )
+        for n in range(4)
+    ]
+    edges = []
+    for half, out in enumerate((head_ref, tail_ref)):
+        for n, ref in enumerate((rate_ref, src_ref)):
+            edges.append(
+                pltpu.make_async_copy(
+                    ref.at[pl.ds(8 * half, 8)],
+                    out.at[pl.ds(1024 + 8 * n, 8)],
+                    sems.at[4 + len(edges)],
+                )
+            )
+    for copy in parts + edges:
+        copy.start()
+
+    def block(b, carry):
+        for half, out in enumerate((head_ref, tail_ref)):
+            start = pl.multiple_of(b * 128, 8) + 8 * half
+            vals = turned([x_s[pl.ds(start + 16 * i, 8), :] for i in range(8)])
+            for r in range(8):
+                out[pl.ds(pl.multiple_of(b * 8, 8) + 128 * r, 8), :] = vals[r]
+        return carry
+
+    for n in range(4):
+        parts[n].wait()
+        lax.fori_loop(4 * n, 4 * n + 4, block, 0)
+    for copy in edges:
+        copy.wait()
+
+
 def inner_kernel(
-    count_ref, pick_ref, table_ref, x_ref, rate_ref, src_ref, bits_ref,
+    count_ref, pick_ref, table_ref, head_ref, tail_ref, bits_ref,
     last_ref, prev_ref, amp_ref, sg_ref, sgt_ref, c_s, h_s, src_s, f_s,
 ):
     for level in range(5):
@@ -195,95 +244,118 @@
         sg_ref[level] = signs.astype(jnp.bfloat16)
         sgt_ref[level] = signs.T.astype(jnp.bfloat16)
     for r in range(16):
-        spread_rows(r, rate_ref[r : r + 1, :], src_ref[r : r + 1, :], c_s, h_s, src_s)
+        ref, at = (head_ref, 1024 + r) if r < 8 else (tail_ref, 1016 + r)
+        spread_rows(r, ref[at : at + 1, :], ref[at + 8 : at + 9, :], c_s, h_s, src_s)
     count = count_ref[0]
     sub = lax.broadcasted_iota(jnp.int32, (8, 128), 0)
 
-    def block(b, carry):
-        rows = pl.ds(pl.multiple_of(b * 8, 8), 8)
-        amp = jnp.zeros((8, 128), F32)
-        for i in range(8):
-            amp = jnp.where(sub == i, 0.1 * table_ref[pick_ref[0, 8 * b + i]], amp)
-        amp_ref[rows, :] = amp
-        old = [x_ref[pl.ds(b * 128 + r, 8, stride=16), :] for r in range(16)]
-        for r in range(1, 15):
-            f_s[8 * r : 8 * r + 8, :] = amp * src_s[8 * r : 8 * r + 8, :]
-        for r in (0, 15):
-            last_ref[r, rows, :] = old[r]
+    def block(pair, carry):
+        state = []
+        for u in range(2):
+            b = 2 * pair + u
+            rows = pl.ds(pl.multiple_of(b * 8, 8), 8)
+            amp = jnp.zeros((8, 128), F32)
+            for i in range(8):
+                amp = jnp.where(sub == i, 0.1 * table_ref[pick_ref[0, 8 * b + i]], amp)
+            amp_ref[rows, :] = amp
+            old = [
+                ref[pl.ds(pl.multiple_of(b * 8, 8) + 128 * r, 8), :]
+                for ref in (head_ref, tail_ref)
+                for r in range(8)
+            ]
+            for r in range(1, 15):
+                f_s[u, 8 * r : 8 * r + 8, :] = amp * src_s[8 * r : 8 * r + 8, :]
+            for r in (0, 15):
+                last_ref[r, rows, :] = old[r]
+            state.append((rows, old))
         for t in range(7):
-            new = list(old)
-            for r in range(t + 1, 15 - t):
-                at = slice(8 * r, 8 * r + 8)
-                new[r] = advance(
-                    old[r], old[r - 1], old[r + 1], c_s[at, :], h_s[at, :], f_s[at, :], t < count
-                )
-            for r in (t + 1, 14 - t):
-                prev_ref[r, rows, :] = old[r]
-                last_ref[r, rows, :] = new[r]
-            old = new
+            stepped = []
+            for u, (rows, old) in enumerate(state):
+                new = list(old)
+                for r in range(t + 1, 15 - t):
+                    at = slice(8 * r, 8 * r + 8)
+                    new[r] = advance(
+                        old[r], old[r - 1], old[r + 1],
+                        c_s[at, :], h_s[at, :], f_s[u, at, :], t < count,
+                    )
+                for r in (t + 1, 14 - t):
+                    prev_ref[r, rows, :] = old[r]
+                    last_ref[r, rows, :] = new[r]
+                stepped.append((rows, new))
+            state = stepped
         return carry
 
-    lax.fori_loop(0, 16, block, 0)
+    lax.fori_loop(0, 8, block, 0)
 
 
 def flow_kernel(
-    count_ref, last_ref, prev_ref, bef_ref, aft_ref, rate_ref, src_ref, amp_ref, sgt_ref,
-    yt_ref, d0, d1, d2, d3, c_s, h_s, src_s, f_s, field_s, s_s,
+    count_ref, last_ref, prev_ref, bef_ref, aft_ref, head_ref, tail_ref, amp_ref, sgt_ref,
+    field_ref, sk_ref, d0, d1, d2, d3, c_s, h_s, src_s, f_s, s_s,
 ):
     for r in range(32):
-        if r < 8:
-            rate, src = bef_ref[1024 + r : 1025 + r, :], bef_ref[1032 + r : 1033 + r, :]
-        elif r < 24:
-            rate, src = rate_ref[r - 8 : r - 7, :], src_ref[r - 8 : r - 7, :]
-        else:
-            rate, src = aft_ref[1000 + r : 1001 + r, :], aft_ref[1008 + r : 1009 + r, :]
+        ref = (bef_ref, head_ref, tail_ref, aft_ref)[r // 8]
+        at = 1024 + r % 8
+        rate, src = ref[at : at + 1, :], ref[at + 8 : at + 9, :]
         spread_rows(r, rate, src, c_s, h_s, src_s)
     count = count_ref[0]
 
-    def block(b, carry):
-        rows = pl.ds(pl.multiple_of(b * 8, 8), 8)
-        amp = amp_ref[rows, :]
-        for r in range(1, 31):
-            f_s[8 * r : 8 * r + 8, :] = amp * src_s[8 * r : 8 * r + 8, :]
-        low = {r - 8: bef_ref[pl.ds(b * 64 + r, 8, stride=8), :] for r in range(8)}
-        high = {r + 16: aft_ref[pl.ds(b * 64 + r, 8, stride=8), :] for r in range(8)}
+    def block(pair, carry):
+        state = []
+        for u in range(2):
+            start = pl.multiple_of(pair * 16 + 8 * u, 8)
+            rows = pl.ds(start, 8)
+            amp = amp_ref[rows, :]
+            for r in range(1, 31):
+                f_s[u, 8 * r : 8 * r + 8, :] = amp * src_s[8 * r : 8 * r + 8, :]
+            low = {r - 8: bef_ref[pl.ds(start + 128 * r, 8), :] for r in range(8)}
+            high = {r + 16: aft_ref[pl.ds(start + 128 * r, 8), :] for r in range(8)}
+            state.append((rows, low, high))
         for t in range(STEPS):
-            low[t] = last_ref[t, rows, :]
-            high[15 - t] = last_ref[15 - t, rows, :]
-            low[t + 1] = last_ref[8, rows, :] if t == 7 else prev_ref[t + 1, rows, :]
-            high[14 - t] = last_ref[7, rows, :] if t == 7 else prev_ref[14 - t, rows, :]
-            sides = []
-            for old, first in ((low, t - 7), (high, 15 - t)):
-                new = {}
-                for r in range(first, first + 8):
-                    at = slice(8 * r + 64, 8 * r + 72)
-                    new[r] = advance(
-                        old[r], old[r - 1], old[r + 1], c_s[at, :], h_s[at, :], f_s[at, :], t < count
-                    )
-                sides.append(new)
-            low, high = sides
-        for r in range(8):
-            field_s[r, rows, :] = low[r]
-            field_s[8 + r, rows, :] = high[8 + r]
+            stepped = []
+            for u, (rows, low, high) in enumerate(state):
+                low[t] = last_ref[t, rows, :]
+                high[15 - t] = last_ref[15 - t, rows, :]
+                low[t + 1] = last_ref[8, rows, :] if t == 7 else prev_ref[t + 1, rows, :]
+                high[14 - t] = last_ref[7, rows, :] if t == 7 else prev_ref[14 - t, rows, :]
+                sides = []
+                for old, first in ((low, t - 7), (high, 15 - t)):
+                    new = {}
+                    for r in range(first, first + 8):
+                        at = slice(8 * r + 64, 8 * r + 72)
+                        new[r] = advance(
+                            old[r], old[r - 1], old[r + 1],
+                            c_s[at, :], h_s[at, :], f_s[u, at, :], t < count,
+                        )
+                    sides.append(new)
+                stepped.append((rows, *sides))
+            state = stepped
+        for rows, low, high in state:
+            for r in range(8):
+                field_ref[r, rows, :] = low[r]
+                field_ref[8 + r, rows, :] = high[8 + r]
         return carry
 
-    lax.fori_loop(0, 16, block, 0)
+    lax.fori_loop(0, 8, block, 0)
     signs_t = sgt_ref[0]
-    yt = jnp.zeros((64, 128), F32)
     for q in range(4):
         parts = []
         for i in range(4):
-            own = field_s[4 * q + i]
-            sk = signs_mm(signs_t, own)
-            yt = yt + mm_nt(sk, own)
+            sk = signs_mm(signs_t, field_ref[4 * q + i])
+            sk_ref[4 * q + i] = sk
             parts.append(sk)
         parts = exchange_blocks(exchange_blocks(parts, 1, 8), 2, 16)
         for j in range(4):
             s_s[j, q] = parts[j]
-    yt_ref[...] = yt
     place = lax.axis_index("y")
     for d, out in enumerate((d0, d1, d2, d3)):
         out[...] = s_s[rest_of(place, d)]
+
+
+def leaf_sum_kernel(field_ref, sk_ref, yt_ref):
+    yt = jnp.zeros((64, 128), F32)
+    for r in range(16):
+        yt = yt + mm_nt(sk_ref[r], field_ref[r])
+    yt_ref[...] = yt
 
 
 def cross_kernel(yt_ref, r0, r1, r2, r3, keep_ref, send_ref, all_s, z_s, pay_s):
@@ -431,6 +503,10 @@
     )(*args)
 
 
+def in_hbm(value):
+    return pltpu.with_memory_space_constraint(value, pltpu.HBM)
+
+
 def shape(*dims):
     return jax.ShapeDtypeStruct(dims, F32)
 
@@ -461,11 +537,16 @@
     n = lax.axis_size(slabs)
     up = [(i, i + 1) for i in range(n - 1)]
     down = [(i + 1, i) for i in range(n - 1)]
-    tail = jnp.concatenate([field[:, 8:], rate[None, 8:], source[None, 8:]], axis=0)
-    head = jnp.concatenate([field[:, :8], rate[None, :8], source[None, :8]], axis=0)
+    head, tail = pl.pallas_call(
+        pack_kernel,
+        out_shape=(shape(1040, 128),) * 2,
+        in_specs=[pl.BlockSpec(memory_space=pltpu.HBM)] * 3,
+        out_specs=(VMEM, VMEM),
+        scratch_shapes=[pltpu.VMEM((2048, 128), F32), pltpu.SemaphoreType.DMA((8,))],
+        compiler_params=pltpu.CompilerParams(vmem_limit_bytes=16 << 20),
+    )(*(in_hbm(v) for v in (field.reshape(2048, 128), rate, source)))
     bef = lax.ppermute(tail, slabs, up)
     aft = lax.ppermute(head, slabs, down)
-
     last, prev, amp, signs, signs_t = call(
         inner_kernel,
         (
@@ -479,28 +560,35 @@
         step_counts,
         sample_idx,
         amplitudes,
-        field.reshape(2048, 128),
-        rate,
-        source,
+        head,
+        tail,
         sketch_signs,
-        scratch=[pltpu.VMEM((128, 128), F32)] * 4,
+        scratch=[pltpu.VMEM((128, 128), F32)] * 3 + [pltpu.VMEM((2, 128, 128), F32)],
         cost=pl.CostEstimate(flops=4_000_000_000, bytes_accessed=4_000_000, transcendentals=0),
     )
-    yt, *chunks = call(
+    final, sks, *chunks = call(
         flow_kernel,
-        (shape(64, 128),) + (shape(4, 64, 128),) * 4,
+        (shape(16, 128, 128), shape(16, 64, 128)) + (shape(4, 64, 128),) * 4,
         1,
         step_counts,
         last,
         prev,
-        bef.reshape(1040, 128),
-        aft.reshape(1040, 128),
-        rate,
-        source,
+        bef,
+        aft,
+        head,
+        tail,
         amp,
         signs_t,
-        scratch=[pltpu.VMEM((256, 128), F32)] * 4
-        + [pltpu.VMEM((16, 128, 128), F32), pltpu.VMEM((4, 4, 64, 128), F32)],
+        scratch=[pltpu.VMEM((256, 128), F32)] * 3
+        + [pltpu.VMEM((2, 256, 128), F32), pltpu.VMEM((4, 4, 64, 128), F32)],
+    )
+    yt = call(
+        leaf_sum_kernel,
+        shape(64, 128),
+        0,
+        final,
+        sks,
+        cost=pl.CostEstimate(flops=2_000_000_000, bytes_accessed=2_000_000, transcendentals=0),
     )
     got = [chunks[0]] + [shift(chunks[d], "y", d) for d in (1, 2, 3)]
     keep, send, sketches = call(

time: 144 us -> 131 us (0.910)
  Pallas kernels: 50 us -> 41.5 us
  local copies, waits for them, and re-layouts: 3.61 us -> 1.45 us
  waiting for transfers between devices: 29 us -> 27.3 us
    pallas_call x7 -> x8, Pallas kernels: 50 us -> 40.1 us  [call(): pl.pallas_call(kernel, out_shape=out_shapes, in_specs=specs, out_specs=ja...]
    ppermute x1, starting transfers between devices: 1.91 us -> 5.11 us  [per_device(): aft = lax.ppermute(head, slabs, down)]
    ppermute x1, starting transfers between devices: 5.06 us -> 1.92 us  [per_device(): bef = lax.ppermute(tail, slabs, up)]
    slice x2 -> x0, local copies, waits for them, and re-layouts: 1.99 us -> none  [the longest x1 1.27 us: per_device(): field[:, :8]]
    ppermute x19, waiting for transfers between devices: 29 us -> 27.3 us  [shift(): return lax.ppermute(value, axis, [(i, (i + by) % n) for i in range(n)])]
  transfers between devices with their start and end apart: 21 -> 21, of which waited for: 18 -> 16; matrix products, arithmetic and copies ran while one was open for 1% -> 0% of each run, Pallas kernels for 6% -> 6%
where the time goes in v2:
time: 131 us; the launch traced here: 130 us
  Pallas kernels  41.5 us (32%)
  starting transfers between devices  31.1 us (24%)
  blocking collectives  28.2 us (22%)
  waiting for transfers between devices  27.3 us (21%)
  local copies, waits for them, and re-layouts  1.45 us (1%)
    pallas_call x8, Pallas kernels, call(): pl.pallas_call(kernel, out_shape=out_shapes, in_specs=specs, out_specs=ja...  40.1 us
    all_to_all x2, blocking collectives, sum_over(): return lax.all_to_all(sent, axis, 0, 0, tiled=True).sum(axis=0)  28.2 us
    ppermute x19, waiting for transfers between devices, shift(): return lax.ppermute(value, axis, [(i, (i + by) % n) for i in range(n)])  27.3 us
    ppermute x19, starting transfers between devices, shift(): return lax.ppermute(value, axis, [(i, (i + by) % n) for i in range(n)])  24 us
    ppermute x1, starting transfers between devices, per_device(): aft = lax.ppermute(head, slabs, down)  5.11 us
  transfers between devices with their start and end apart: 21, of which 16 were waited for; matrix products, arithmetic and copies ran while one was open for 0% of the time, Pallas kernels for 6%

profile of v2, /device:TPU:1, one launch (start us, length us, event | category | flops | bytes accessed | tf_op | source)
XLA Modules:
  0.0 130.4 jit_solution(4322341659727141037)
XLA Ops:
  0.0 0.0 copy-start.2
  0.0 1.4 %shard_map.73 = (f32[1040,128]{1,0:T(8,128)S(1)}, f32[1040,128]{1,0:T(8,128)S(1)}) custom-call(f32[2048,128]{1,0:T(8,128)} %bitcast.3, f32[16,128]{1,0:T(8,128)} %bitcast.4, f32[16,128]{1,0:T(8,128)} %src_ref.1), custom_call_target="tpu_custom_call" | custom-call | tf_op jit(solution)/shard_map/pallas_call | solution.py:540
  1.4 5.1 %collective-permute-start.1 = (f32[1040,128]{1,0:T(8,128)S(1)}, f32[1040,128]{1,0:T(8,128)S(1)}, u32[]{:S(2)}, u32[]{:S(2)}) collective-permute-start(f32[1040,128]{1,0:T(8,128)S(1)} %get-tuple-element.24.head_ref), channel_id=1, source_target_pairs={{1,0},{2,1},{3,2},{4,3},{5,4},{6,5},{7,6},{8,7},{9,8},{10,9},{11,1... | collective-permute-start | bytes 1597448 | tf_op jit(solution)/shard_map/ppermute | solution.py:549
  6.5 1.9 %collective-permute-start = (f32[1040,128]{1,0:T(8,128)S(1)}, f32[1040,128]{1,0:T(8,128)S(1)}, u32[]{:S(2)}, u32[]{:S(2)}) collective-permute-start(f32[1040,128]{1,0:T(8,128)S(1)} %get-tuple-element.25.tail_ref), channel_id=1, source_target_pairs={{0,1},{1,2},{2,3},{3,4},{4,5},{5,6},{6,7},{7,8},{8,9},{9,10},{10,1... | collective-permute-start | bytes 1597448 | tf_op jit(solution)/shard_map/ppermute | solution.py:548
  9.1 0.0 copy-done.2
  9.1 0.0 copy-start
  9.1 0.0 copy-start.1
  9.1 0.2 copy.12.bits_ref
  9.3 0.5 copy-done
  9.7 0.0 copy-done.1
  9.8 5.1 %shard_map.74 = (f32[16,128,128]{2,1,0:T(8,128)S(1)}, f32[16,128,128]{2,1,0:T(8,128)S(1)}, f32[128,128]{1,0:T(8,128)S(1)}, bf16[5,128,64]{2,1,0:T(8,128)(2,1)S(1)}, bf16[5,64,128]{2,1,0:T(8,128)(2,1)S(1)}) custom-call(s32[1]{0:T(128)S(6)} %copy.14.count_ref, s32[1,128]{1,0:T(1,128)S(1)} %copy-done, f32[64]{0:T(128)S(1)} %copy-done.1, ...), custom_call_target="tpu_custom_call" | custom-call | flops 4000000000 | bytes 4000000 | tf_op jit(solution)/shard_map/pallas_call | solution.py:495
  14.8 0.0 collective-permute-done.1.aft_ref
  14.9 0.0 collective-permute-done.bef_ref
  14.9 6.6 %shard_map.75 = (f32[16,128,128]{2,1,0:T(8,128)S(1)}, f32[16,64,128]{2,1,0:T(8,128)S(1)}, f32[4,64,128]{2,1,0:T(8,128)S(1)}, f32[4,64,128]{2,1,0:T(8,128)S(1)}, ...) custom-call(s32[1]{0:T(128)S(6)} %copy.14.count_ref, f32[16,128,128]{2,1,0:T(8,128)S(1)} %get-tuple-element.26.last_ref, ...), custom_call_target="tpu_custom_call" | custom-call | tf_op jit(solution)/shard_map/pallas_call | solution.py:495
  21.5 1.2 collective-permute-start.2
  22.7 2.6 %collective-permute-start.3 = (f32[4,64,128]{2,1,0:T(8,128)S(1)}, f32[4,64,128]{2,1,0:T(8,128)S(1)}, u32[]{:S(2)}, u32[]{:S(2)}) collective-permute-start(f32[4,64,128]{2,1,0:T(8,128)S(1)} %get-tuple-element.34), channel_id=1, source_target_pairs={{0,32},{16,48},{32,0},{48,16},{1,33},{17,49},{33,1},{49,17},{2,34}... | collective-permute-start | bytes 393224 | tf_op jit(solution)/shard_map/ppermute | solution.py:516
  25.3 1.1 collective-permute-start.4
  26.3 2.1 %shard_map.76.yt_ref = f32[64,128]{1,0:T(8,128)S(1)} custom-call(f32[16,128,128]{2,1,0:T(8,128)S(1)} %get-tuple-element.30.field_ref, f32[16,64,128]{2,1,0:T(8,128)S(1)} %get-tuple-element.31.sk_ref), custom_call_target="tpu_custom_call" | custom-call | flops 2000000000 | bytes 2000000 | tf_op jit(solution)/shard_map/pallas_call | solution.py:495
  28.4 0.0 collective-permute-done.2.r1
  28.4 2.9 %collective-permute-done.3.r2 = f32[4,64,128]{2,1,0:T(8,128)S(1)} collective-permute-done((f32[4,64,128]{2,1,0:T(8,128)S(1)}, f32[4,64,128]{2,1,0:T(8,128)S(1)}, u32[]{:S(2)}, u32[]{:S(2)}) %collective-permute-start.3) | collective-permute-done | bytes 131104 | tf_op jit(solution)/shard_map/ppermute | solution.py:516
  31.3 0.0 collective-permute-done.4.r3
  31.3 1.9 %shard_map.77 = (f32[128,128]{1,0:T(8,128)S(1)}, f32[128,128]{1,0:T(8,128)S(1)}, f32[4,4,64,128]{3,2,1,0:T(8,128)S(1)}) custom-call(f32[64,128]{1,0:T(8,128)S(1)} %shard_map.76.yt_ref, f32[4,64,128]{2,1,0:T(8,128)S(1)} %get-tuple-element.32.r0, f32[4,64,128]{2,1,0:T(8,128)S(1)} %collective-permute-done.2.r1, f32[4,64,128]{2,1,0:T(8,128)S(1)} %collective-permute-done.3.r2, ...), custom_call_target="tpu_custom_call" | custom-call | tf_op jit(solution)/shard_map/pallas_call | solution.py:495
  33.2 0.8 collective-permute-start.5
  34.0 0.9 collective-permute-done.5
  34.9 2.5 %collective-permute-start.8 = (f32[24,128]{1,0:T(8,128)S(1)}, f32[24,128]{1,0:T(8,128)S(1)}, u32[]{:S(2)}, u32[]{:S(2)}) collective-permute-start(f32[24,128]{1,0:T(8,128)S(1)} %get-tuple-element.43), channel_id=1, source_target_pairs={{0,48},{16,0},{32,16},{48,32},{1,49},{17,1},{33,17},{49,33},{2,50}... | collective-permute-start | bytes 36872 | tf_op jit(solution)/shard_map/ppermute | solution.py:516
  37.4 0.9 collective-permute-start.7
  38.3 0.0 collective-permute-start.6
  38.3 0.0 collective-permute-done.8
  38.3 3.2 %collective-permute-done.7 = f32[24,128]{1,0:T(8,128)S(1)} collective-permute-done((f32[24,128]{1,0:T(8,128)S(1)}, f32[24,128]{1,0:T(8,128)S(1)}, u32[]{:S(2)}, u32[]{:S(2)}) %collective-permute-start.7) | collective-permute-done | bytes 12320 | tf_op jit(solution)/shard_map/ppermute | solution.py:516
  41.5 0.6 collective-permute-done.6
  42.1 17.1 %all_to_all.10 = f32[8,56,128]{2,1,0:T(8,128)S(1)} all-to-all(f32[8,56,128]{2,1,0:T(8,128)S(1)} %broadcast_in_dim.4), channel_id=1, replica_groups=mesh['x'=4,'y'=4,'z'=8,'core'=2] {'z'}, dimensions={0} | all-to-all | bytes 458752 | tf_op jit(solution)/shard_map/all_to_all | solution.py:530
  59.2 3.5 %collective-permute-start.9 = (f32[56,128]{1,0:T(8,128)S(1)}, f32[56,128]{1,0:T(8,128)S(1)}, u32[]{:S(2)}, u32[]{:S(2)}) collective-permute-start(f32[56,128]{1,0:T(8,128)S(1)} %reduce_sum.18.own_ref), channel_id=1, source_target_pairs={{0,1},{1,0},{2,3},{3,2},{4,5},{5,4},{6,7},{7,6},{8,9},{9,8},{10,11... | collective-permute-start | bytes 86024 | tf_op jit(solution)/shard_map/ppermute | solution.py:516
  62.7 0.9 collective-permute-done.9.other_ref
  63.6 3.9 %shard_map.78.p0 = f32[112,128]{1,0:T(8,128)S(1)} custom-call(f32[56,128]{1,0:T(8,128)S(1)} %reduce_sum.18.own_ref, f32[56,128]{1,0:T(8,128)S(1)} %collective-permute-done.9.other_ref, bf16[5,128,64]{2,1,0:T(8,128)(2,1)S(1)} %get-tuple-element.38.sg_ref, bf16[5,64,128]{2,1,0:T(8,128)(2,1)S(1)} %get-tuple-element.29.sgt_ref), custom_call_target="tpu_custom_call" | custom-call | tf_op jit(solution)/shard_map/pallas_call | solution.py:495
  67.5 0.5 collective-permute-start.12
  68.0 1.2 collective-permute-start.11
  69.2 0.8 collective-permute-start.10
  69.9 0.7 collective-permute-done.12.p3
  70.6 1.9 %collective-permute-done.11.p2 = f32[112,128]{1,0:T(8,128)S(1)} collective-permute-done((f32[112,128]{1,0:T(8,128)S(1)}, f32[112,128]{1,0:T(8,128)S(1)}, u32[]{:S(2)}, u32[]{:S(2)}) %collective-permute-start.11) | collective-permute-done | bytes 57376 | tf_op jit(solution)/shard_map/ppermute | solution.py:516
  72.5 1.9 %collective-permute-done.10.p1 = f32[112,128]{1,0:T(8,128)S(1)} collective-permute-done((f32[112,128]{1,0:T(8,128)S(1)}, f32[112,128]{1,0:T(8,128)S(1)}, u32[]{:S(2)}, u32[]{:S(2)}) %collective-permute-start.10) | collective-permute-done | bytes 57376 | tf_op jit(solution)/shard_map/ppermute | solution.py:516
  74.4 10.2 %shard_map.79.r0 = f32[288,128]{1,0:T(8,128)S(1)} custom-call(f32[112,128]{1,0:T(8,128)S(1)} %shard_map.78.p0, f32[112,128]{1,0:T(8,128)S(1)} %collective-permute-done.10.p1, f32[112,128]{1,0:T(8,128)S(1)} %collective-permute-done.11.p2, f32[112,128]{1,0:T(8,128)S(1)} %collective-permute-done.12.p3, f32[4,4,64,128]{3,2,1,0:T(8,128)S(1)} %get-tuple-element.39.all_ref, ...), custom_call_target="tpu_custom_call" | custom-call | tf_op jit(solution)/shard_map/pallas_call | solution.py:495
  84.6 2.8 %collective-permute-start.15 = (f32[288,128]{1,0:T(8,128)S(1)}, f32[288,128]{1,0:T(8,128)S(1)}, u32[]{:S(2)}, u32[]{:S(2)}) collective-permute-start(f32[288,128]{1,0:T(8,128)S(1)} %shard_map.79.r0), channel_id=1, source_target_pairs={{0,192},{64,0},{128,64},{192,128},{1,193},{65,1},{129,65},{193,129... | collective-permute-start | bytes 442376 | tf_op jit(solution)/shard_map/ppermute | solution.py:516
  87.4 0.5 collective-permute-start.14
  87.9 0.6 collective-permute-start.13
  88.5 2.2 %collective-permute-done.15.r3 = f32[288,128]{1,0:T(8,128)S(1)} collective-permute-done((f32[288,128]{1,0:T(8,128)S(1)}, f32[288,128]{1,0:T(8,128)S(1)}, u32[]{:S(2)}, u32[]{:S(2)}) %collective-permute-start.15) | collective-permute-done | bytes 147488 | tf_op jit(solution)/shard_map/ppermute | solution.py:516
  90.8 2.3 %collective-permute-done.14.r2 = f32[288,128]{1,0:T(8,128)S(1)} collective-permute-done((f32[288,128]{1,0:T(8,128)S(1)}, f32[288,128]{1,0:T(8,128)S(1)}, u32[]{:S(2)}, u32[]{:S(2)}) %collective-permute-start.14) | collective-permute-done | bytes 147488 | tf_op jit(solution)/shard_map/ppermute | solution.py:516
  93.0 4.7 %collective-permute-done.13.r1 = f32[288,128]{1,0:T(8,128)S(1)} collective-permute-done((f32[288,128]{1,0:T(8,128)S(1)}, f32[288,128]{1,0:T(8,128)S(1)}, u32[]{:S(2)}, u32[]{:S(2)}) %collective-permute-start.13) | collective-permute-done | bytes 147488 | tf_op jit(solution)/shard_map/ppermute | solution.py:516
  97.7 1.1 shard_map.80
  98.8 0.7 collective-permute-start.16
  99.5 0.8 collective-permute-done.16
  100.4 0.3 collective-permute-start.19
  100.7 0.5 collective-permute-start.18
  101.3 0.6 collective-permute-start.17
  101.9 1.2 collective-permute-done.19
  103.1 1.9 %collective-permute-done.18 = f32[48,128]{1,0:T(8,128)S(1)} collective-permute-done((f32[48,128]{1,0:T(8,128)S(1)}, f32[48,128]{1,0:T(8,128)S(1)}, u32[]{:S(2)}, u32[]{:S(2)}) %collective-permute-start.18) | collective-permute-done | bytes 24608 | tf_op jit(solution)/shard_map/ppermute | solution.py:516
  104.9 0.5 collective-permute-done.17
  105.5 11.1 %all_to_all.11 = f32[8,48,128]{2,1,0:T(8,128)S(1)} all-to-all(f32[8,48,128]{2,1,0:T(8,128)S(1)} %broadcast_in_dim.5), channel_id=1, replica_groups=mesh['x'=4,'y'=4,'z'=8,'core'=2] {'z'}, dimensions={0} | all-to-all | bytes 393216 | tf_op jit(solution)/shard_map/all_to_all | solution.py:530
  116.6 3.0 %collective-permute-start.20 = (f32[48,128]{1,0:T(8,128)S(1)}, f32[48,128]{1,0:T(8,128)S(1)}, u32[]{:S(2)}, u32[]{:S(2)}) collective-permute-start(f32[48,128]{1,0:T(8,128)S(1)} %reduce_sum.19.own_ref), channel_id=1, source_target_pairs={{0,1},{1,0},{2,3},{3,2},{4,5},{5,4},{6,7},{7,6},{8,9},{9,8},{10,11... | collective-permute-start | bytes 73736 | tf_op jit(solution)/shard_map/ppermute | solution.py:516
  119.5 0.8 collective-permute-done.20.other_ref
  120.4 9.3 %shard_map.81 = f32[64,128]{1,0:T(8,128)S(1)} custom-call(f32[48,128]{1,0:T(8,128)S(1)} %reduce_sum.19.own_ref, f32[48,128]{1,0:T(8,128)S(1)} %collective-permute-done.20.other_ref, f32[288,128]{1,0:T(8,128)S(1)} %shard_map.79.r0, f32[288,128]{1,0:T(8,128)S(1)} %collective-permute-done.13.r1, f32[288,128]{1,0:T(8,128)S(1)} %collective-permute-done.14.r2, ...), custom_call_target="tpu_custom_call" | custom-call | tf_op jit(solution)/shard_map/pallas_call | solution.py:495
  129.7 0.7 copy.13
  (11 shorter events, 0.1 us)
Async XLA Ops:
  0.0 9.1 %copy-start.2 = (s32[5,128,64]{1,2,0:T(8,128)S(1)}, s32[5,128,64]{1,2,0:T(8,128)}, u32[]{:S(2)}) copy-start(s32[5,128,64]{1,2,0:T(8,128)} %param.13) | copy-start | bytes 491524
  1.4 13.5 %collective-permute-start.1 = (f32[1040,128]{1,0:T(8,128)S(1)}, f32[1040,128]{1,0:T(8,128)S(1)}, u32[]{:S(2)}, u32[]{:S(2)}) collective-permute-start(f32[1040,128]{1,0:T(8,128)S(1)} %get-tuple-element.24.head_ref), channel_id=1, source_target_pairs={{1,0},{2,1},{3,2},{4,3},{5,4},{6,5},{7,6},{8,7},{9,8},{10,9},{11,1... | collective-permute-start | bytes 1597448 | tf_op jit(solution)/shard_map/ppermute | solution.py:549
  6.5 8.4 %collective-permute-start = (f32[1040,128]{1,0:T(8,128)S(1)}, f32[1040,128]{1,0:T(8,128)S(1)}, u32[]{:S(2)}, u32[]{:S(2)}) collective-permute-start(f32[1040,128]{1,0:T(8,128)S(1)} %get-tuple-element.25.tail_ref), channel_id=1, source_target_pairs={{0,1},{1,2},{2,3},{3,4},{4,5},{5,6},{6,7},{7,8},{8,9},{9,10},{10,1... | collective-permute-start | bytes 1597448 | tf_op jit(solution)/shard_map/ppermute | solution.py:548
  9.1 0.7 copy-start
  9.1 0.7 copy-start.1
  21.5 7.0 %collective-permute-start.2 = (f32[4,64,128]{2,1,0:T(8,128)S(1)}, f32[4,64,128]{2,1,0:T(8,128)S(1)}, u32[]{:S(2)}, u32[]{:S(2)}) collective-permute-start(f32[4,64,128]{2,1,0:T(8,128)S(1)} %get-tuple-element.33), channel_id=1, source_target_pairs={{0,16},{16,32},{32,48},{48,0},{1,17},{17,33},{33,49},{49,1},{2,18}... | collective-permute-start | bytes 393224 | tf_op jit(solution)/shard_map/ppermute | solution.py:516
  22.7 8.7 %collective-permute-start.3 = (f32[4,64,128]{2,1,0:T(8,128)S(1)}, f32[4,64,128]{2,1,0:T(8,128)S(1)}, u32[]{:S(2)}, u32[]{:S(2)}) collective-permute-start(f32[4,64,128]{2,1,0:T(8,128)S(1)} %get-tuple-element.34), channel_id=1, source_target_pairs={{0,32},{16,48},{32,0},{48,16},{1,33},{17,49},{33,1},{49,17},{2,34}... | collective-permute-start | bytes 393224 | tf_op jit(solution)/shard_map/ppermute | solution.py:516
  25.3 6.0 %collective-permute-start.4 = (f32[4,64,128]{2,1,0:T(8,128)S(1)}, f32[4,64,128]{2,1,0:T(8,128)S(1)}, u32[]{:S(2)}, u32[]{:S(2)}) collective-permute-start(f32[4,64,128]{2,1,0:T(8,128)S(1)} %get-tuple-element.35), channel_id=1, source_target_pairs={{0,48},{16,0},{32,16},{48,32},{1,49},{17,1},{33,17},{49,33},{2,50}... | collective-permute-start | bytes 393224 | tf_op jit(solution)/shard_map/ppermute | solution.py:516
  33.2 1.7 %collective-permute-start.5 = (f32[128,128]{1,0:T(8,128)S(1)}, f32[128,128]{1,0:T(8,128)S(1)}, u32[]{:S(2)}, u32[]{:S(2)}) collective-permute-start(f32[128,128]{1,0:T(8,128)S(1)} %get-tuple-element.37), channel_id=1, source_target_pairs={{0,1},{1,0},{2,3},{3,2},{4,5},{5,4},{6,7},{7,6},{8,9},{9,8},{10,11... | collective-permute-start | bytes 196616 | tf_op jit(solution)/shard_map/ppermute | solution.py:516
  34.9 3.3 %collective-permute-start.8 = (f32[24,128]{1,0:T(8,128)S(1)}, f32[24,128]{1,0:T(8,128)S(1)}, u32[]{:S(2)}, u32[]{:S(2)}) collective-permute-start(f32[24,128]{1,0:T(8,128)S(1)} %get-tuple-element.43), channel_id=1, source_target_pairs={{0,48},{16,0},{32,16},{48,32},{1,49},{17,1},{33,17},{49,33},{2,50}... | collective-permute-start | bytes 36872 | tf_op jit(solution)/shard_map/ppermute | solution.py:516
  37.4 4.0 %collective-permute-start.7 = (f32[24,128]{1,0:T(8,128)S(1)}, f32[24,128]{1,0:T(8,128)S(1)}, u32[]{:S(2)}, u32[]{:S(2)}) collective-permute-start(f32[24,128]{1,0:T(8,128)S(1)} %get-tuple-element.44), channel_id=1, source_target_pairs={{0,32},{16,48},{32,0},{48,16},{1,33},{17,49},{33,1},{49,17},{2,34}... | collective-permute-start | bytes 36872 | tf_op jit(solution)/shard_map/ppermute | solution.py:516
  38.3 3.8 %collective-permute-start.6 = (f32[24,128]{1,0:T(8,128)S(1)}, f32[24,128]{1,0:T(8,128)S(1)}, u32[]{:S(2)}, u32[]{:S(2)}) collective-permute-start(f32[24,128]{1,0:T(8,128)S(1)} %get-tuple-element.45), channel_id=1, source_target_pairs={{0,16},{16,32},{32,48},{48,0},{1,17},{17,33},{33,49},{49,1},{2,18}... | collective-permute-start | bytes 36872 | tf_op jit(solution)/shard_map/ppermute | solution.py:516
  59.2 4.4 %collective-permute-start.9 = (f32[56,128]{1,0:T(8,128)S(1)}, f32[56,128]{1,0:T(8,128)S(1)}, u32[]{:S(2)}, u32[]{:S(2)}) collective-permute-start(f32[56,128]{1,0:T(8,128)S(1)} %reduce_sum.18.own_ref), channel_id=1, source_target_pairs={{0,1},{1,0},{2,3},{3,2},{4,5},{5,4},{6,7},{7,6},{8,9},{9,8},{10,11... | collective-permute-start | bytes 86024 | tf_op jit(solution)/shard_map/ppermute | solution.py:516
  67.5 3.1 %collective-permute-start.12 = (f32[112,128]{1,0:T(8,128)S(1)}, f32[112,128]{1,0:T(8,128)S(1)}, u32[]{:S(2)}, u32[]{:S(2)}) collective-permute-start(f32[112,128]{1,0:T(8,128)S(1)} %shard_map.78.p0), channel_id=1, source_target_pairs={{0,48},{16,0},{32,16},{48,32},{1,49},{17,1},{33,17},{49,33},{2,50}... | collective-permute-start | bytes 172040 | tf_op jit(solution)/shard_map/ppermute | solution.py:516
  68.0 4.5 %collective-permute-start.11 = (f32[112,128]{1,0:T(8,128)S(1)}, f32[112,128]{1,0:T(8,128)S(1)}, u32[]{:S(2)}, u32[]{:S(2)}) collective-permute-start(f32[112,128]{1,0:T(8,128)S(1)} %shard_map.78.p0), channel_id=1, source_target_pairs={{0,32},{16,48},{32,0},{48,16},{1,33},{17,49},{33,1},{49,17},{2,34}... | collective-permute-start | bytes 172040 | tf_op jit(solution)/shard_map/ppermute | solution.py:516
  69.2 5.3 %collective-permute-start.10 = (f32[112,128]{1,0:T(8,128)S(1)}, f32[112,128]{1,0:T(8,128)S(1)}, u32[]{:S(2)}, u32[]{:S(2)}) collective-permute-start(f32[112,128]{1,0:T(8,128)S(1)} %shard_map.78.p0), channel_id=1, source_target_pairs={{0,16},{16,32},{32,48},{48,0},{1,17},{17,33},{33,49},{49,1},{2,18}... | collective-permute-start | bytes 172040 | tf_op jit(solution)/shard_map/ppermute | solution.py:516
  84.6 6.1 %collective-permute-start.15 = (f32[288,128]{1,0:T(8,128)S(1)}, f32[288,128]{1,0:T(8,128)S(1)}, u32[]{:S(2)}, u32[]{:S(2)}) collective-permute-start(f32[288,128]{1,0:T(8,128)S(1)} %shard_map.79.r0), channel_id=1, source_target_pairs={{0,192},{64,0},{128,64},{192,128},{1,193},{65,1},{129,65},{193,129... | collective-permute-start | bytes 442376 | tf_op jit(solution)/shard_map/ppermute | solution.py:516
  87.4 5.6 %collective-permute-start.14 = (f32[288,128]{1,0:T(8,128)S(1)}, f32[288,128]{1,0:T(8,128)S(1)}, u32[]{:S(2)}, u32[]{:S(2)}) collective-permute-start(f32[288,128]{1,0:T(8,128)S(1)} %shard_map.79.r0), channel_id=1, source_target_pairs={{0,128},{64,192},{128,0},{192,64},{1,129},{65,193},{129,1},{193,65... | collective-permute-start | bytes 442376 | tf_op jit(solution)/shard_map/ppermute | solution.py:516
  87.9 9.7 %collective-permute-start.13 = (f32[288,128]{1,0:T(8,128)S(1)}, f32[288,128]{1,0:T(8,128)S(1)}, u32[]{:S(2)}, u32[]{:S(2)}) collective-permute-start(f32[288,128]{1,0:T(8,128)S(1)} %shard_map.79.r0), channel_id=1, source_target_pairs={{0,64},{64,128},{128,192},{192,0},{1,65},{65,129},{129,193},{193,1... | collective-permute-start | bytes 442376 | tf_op jit(solution)/shard_map/ppermute | solution.py:516
  98.8 1.6 %collective-permute-start.16 = (f32[48,128]{1,0:T(8,128)S(1)}, f32[48,128]{1,0:T(8,128)S(1)}, u32[]{:S(2)}, u32[]{:S(2)}) collective-permute-start(f32[48,128]{1,0:T(8,128)S(1)} %get-tuple-element.41), channel_id=1, source_target_pairs={{0,1},{1,0},{2,3},{3,2},{4,5},{5,4},{6,7},{7,6},{8,9},{9,8},{10,11... | collective-permute-start | bytes 73736 | tf_op jit(solution)/shard_map/ppermute | solution.py:516
  100.4 2.7 %collective-permute-start.19 = (f32[48,128]{1,0:T(8,128)S(1)}, f32[48,128]{1,0:T(8,128)S(1)}, u32[]{:S(2)}, u32[]{:S(2)}) collective-permute-start(f32[48,128]{1,0:T(8,128)S(1)} %add.28), channel_id=1, source_target_pairs={{0,48},{16,0},{32,16},{48,32},{1,49},{17,1},{33,17},{49,33},{2,50}... | collective-permute-start | bytes 73736 | tf_op jit(solution)/shard_map/ppermute | solution.py:516
  100.7 4.2 %collective-permute-start.18 = (f32[48,128]{1,0:T(8,128)S(1)}, f32[48,128]{1,0:T(8,128)S(1)}, u32[]{:S(2)}, u32[]{:S(2)}) collective-permute-start(f32[48,128]{1,0:T(8,128)S(1)} %add.28), channel_id=1, source_target_pairs={{0,32},{16,48},{32,0},{48,16},{1,33},{17,49},{33,1},{49,17},{2,34}... | collective-permute-start | bytes 73736 | tf_op jit(solution)/shard_map/ppermute | solution.py:516
  101.3 4.2 %collective-permute-start.17 = (f32[48,128]{1,0:T(8,128)S(1)}, f32[48,128]{1,0:T(8,128)S(1)}, u32[]{:S(2)}, u32[]{:S(2)}) collective-permute-start(f32[48,128]{1,0:T(8,128)S(1)} %add.28), channel_id=1, source_target_pairs={{0,16},{16,32},{32,48},{48,0},{1,17},{17,33},{33,49},{49,1},{2,18}... | collective-permute-start | bytes 73736 | tf_op jit(solution)/shard_map/ppermute | solution.py:516
  116.6 3.8 %collective-permute-start.20 = (f32[48,128]{1,0:T(8,128)S(1)}, f32[48,128]{1,0:T(8,128)S(1)}, u32[]{:S(2)}, u32[]{:S(2)}) collective-permute-start(f32[48,128]{1,0:T(8,128)S(1)} %reduce_sum.19.own_ref), channel_id=1, source_target_pairs={{0,1},{1,0},{2,3},{3,2},{4,5},{5,4},{6,7},{7,6},{8,9},{9,8},{10,11... | collective-permute-start | bytes 73736 | tf_op jit(solution)/shard_map/ppermute | solution.py:516

commit v3 on v2

--- a/solution.py
+++ b/solution.py
@@ -200,7 +200,10 @@
     return out
 
 
-def pack_kernel(x_ref, rate_ref, src_ref, head_ref, tail_ref, x_s, sems):
+def pack_kernel(
+    x_ref, rate_ref, src_ref, pick_ref, table_ref,
+    head_ref, tail_ref, amp_ref, x_s, pick_s, table_s, sems,
+):
     parts = [
         pltpu.make_async_copy(
             x_ref.at[pl.ds(512 * n, 512)], x_s.at[pl.ds(512 * n, 512)], sems.at[n]
@@ -217,8 +220,24 @@
                     sems.at[4 + len(edges)],
                 )
             )
-    for copy in parts + edges:
+    tables = [
+        pltpu.make_async_copy(pick_ref, pick_s, sems.at[8]),
+        pltpu.make_async_copy(table_ref, table_s, sems.at[9]),
+    ]
+    for copy in parts + tables + edges:
         copy.start()
+    for copy in tables:
+        copy.wait()
+    sub = lax.broadcasted_iota(jnp.int32, (8, 128), 0)
+
+    def amplitude(b, carry):
+        amp = jnp.zeros((8, 128), F32)
+        for i in range(8):
+            amp = jnp.where(sub == i, 0.1 * table_s[pick_s[0, 8 * b + i]], amp)
+        amp_ref[pl.ds(pl.multiple_of(b * 8, 8), 8), :] = amp
+        return carry
+
+    lax.fori_loop(0, 16, amplitude, 0)
 
     def block(b, carry):
         for half, out in enumerate((head_ref, tail_ref)):
@@ -236,28 +255,21 @@
 
 
 def inner_kernel(
-    count_ref, pick_ref, table_ref, head_ref, tail_ref, bits_ref,
-    last_ref, prev_ref, amp_ref, sg_ref, sgt_ref, c_s, h_s, src_s, f_s,
+    count_ref, head_ref, tail_ref, amp_ref, bits_ref,
+    last_ref, prev_ref, sgt_ref, c_s, h_s, src_s, f_s,
 ):
-    for level in range(5):
-        signs = 2.0 * bits_ref[level].astype(F32) - 1.0
-        sg_ref[level] = signs.astype(jnp.bfloat16)
-        sgt_ref[level] = signs.T.astype(jnp.bfloat16)
+    sgt_ref[...] = (2.0 * bits_ref[0].astype(F32) - 1.0).astype(jnp.bfloat16)
     for r in range(16):
         ref, at = (head_ref, 1024 + r) if r < 8 else (tail_ref, 1016 + r)
         spread_rows(r, ref[at : at + 1, :], ref[at + 8 : at + 9, :], c_s, h_s, src_s)
     count = count_ref[0]
-    sub = lax.broadcasted_iota(jnp.int32, (8, 128), 0)
 
     def block(pair, carry):
         state = []
         for u in range(2):
             b = 2 * pair + u
             rows = pl.ds(pl.multiple_of(b * 8, 8), 8)
-            amp = jnp.zeros((8, 128), F32)
-            for i in range(8):
-                amp = jnp.where(sub == i, 0.1 * table_ref[pick_ref[0, 8 * b + i]], amp)
-            amp_ref[rows, :] = amp
+            amp = amp_ref[rows, :]
             old = [
                 ref[pl.ds(pl.multiple_of(b * 8, 8) + 128 * r, 8), :]
                 for ref in (head_ref, tail_ref)
@@ -336,7 +348,7 @@
         return carry
 
     lax.fori_loop(0, 8, block, 0)
-    signs_t = sgt_ref[0]
+    signs_t = sgt_ref[...]
     for q in range(4):
         parts = []
         for i in range(4):
@@ -351,7 +363,11 @@
         out[...] = s_s[rest_of(place, d)]
 
 
-def leaf_sum_kernel(field_ref, sk_ref, yt_ref):
+def leaf_sum_kernel(field_ref, sk_ref, bits_ref, yt_ref, sg_ref, sgt_ref):
+    for level in range(5):
+        signs = 2.0 * bits_ref[level].astype(F32) - 1.0
+        sg_ref[level] = signs.T.astype(jnp.bfloat16)
+        sgt_ref[level] = signs.astype(jnp.bfloat16)
     yt = jnp.zeros((64, 128), F32)
     for r in range(16):
         yt = yt + mm_nt(sk_ref[r], field_ref[r])
@@ -537,32 +553,40 @@
     n = lax.axis_size(slabs)
     up = [(i, i + 1) for i in range(n - 1)]
     down = [(i + 1, i) for i in range(n - 1)]
-    head, tail = pl.pallas_call(
+    head, tail, amp = pl.pallas_call(
         pack_kernel,
-        out_shape=(shape(1040, 128),) * 2,
-        in_specs=[pl.BlockSpec(memory_space=pltpu.HBM)] * 3,
-        out_specs=(VMEM, VMEM),
-        scratch_shapes=[pltpu.VMEM((2048, 128), F32), pltpu.SemaphoreType.DMA((8,))],
+        out_shape=(shape(1040, 128), shape(1040, 128), shape(128, 128)),
+        in_specs=[pl.BlockSpec(memory_space=pltpu.HBM)] * 5,
+        out_specs=(VMEM,) * 3,
+        scratch_shapes=[
+            pltpu.VMEM((2048, 128), F32),
+            pltpu.SMEM((1, 128), jnp.int32),
+            pltpu.SMEM((64,), F32),
+            pltpu.SemaphoreType.DMA((10,)),
+        ],
         compiler_params=pltpu.CompilerParams(vmem_limit_bytes=16 << 20),
-    )(*(in_hbm(v) for v in (field.reshape(2048, 128), rate, source)))
+    )(
+        *(
+            in_hbm(v)
+            for v in (field.reshape(2048, 128), rate, source, sample_idx, amplitudes)
+        )
+    )
+    bits = jnp.swapaxes(sketch_signs, 1, 2)
     bef = lax.ppermute(tail, slabs, up)
     aft = lax.ppermute(head, slabs, down)
-    last, prev, amp, signs, signs_t = call(
+    last, prev, first_signs = call(
         inner_kernel,
         (
             shape(16, 128, 128),
             shape(16, 128, 128),
-            shape(128, 128),
-            jax.ShapeDtypeStruct((5, 128, 64), jnp.bfloat16),
-            jax.ShapeDtypeStruct((5, 64, 128), jnp.bfloat16),
+            jax.ShapeDtypeStruct((64, 128), jnp.bfloat16),
         ),
-        3,
+        1,
         step_counts,
-        sample_idx,
-        amplitudes,
         head,
         tail,
-        sketch_signs,
+        amp,
+        bits,
         scratch=[pltpu.VMEM((128, 128), F32)] * 3 + [pltpu.VMEM((2, 128, 128), F32)],
         cost=pl.CostEstimate(flops=4_000_000_000, bytes_accessed=4_000_000, transcendentals=0),
     )
@@ -578,16 +602,21 @@
         head,
         tail,
         amp,
-        signs_t,
+        first_signs,
         scratch=[pltpu.VMEM((256, 128), F32)] * 3
         + [pltpu.VMEM((2, 256, 128), F32), pltpu.VMEM((4, 4, 64, 128), F32)],
     )
-    yt = call(
+    yt, signs, signs_t = call(
         leaf_sum_kernel,
-        shape(64, 128),
+        (
+            shape(64, 128),
+            jax.ShapeDtypeStruct((5, 128, 64), jnp.bfloat16),
+            jax.ShapeDtypeStruct((5, 64, 128), jnp.bfloat16),
+        ),
         0,
         final,
         sks,
+        bits,
         cost=pl.CostEstimate(flops=2_000_000_000, bytes_accessed=2_000_000, transcendentals=0),
     )
     got = [chunks[0]] + [shift(chunks[d], "y", d) for d in (1, 2, 3)]

time: 131 us -> 131 us (level)
  transfers between devices with their start and end apart: 21 -> 21, of which waited for: 16 -> 18; matrix products, arithmetic and copies ran while one was open for 0% -> 0% of each run, Pallas kernels for 6% -> 5%
where the time goes in v3:
time: 131 us; the launch traced here: 130 us
  Pallas kernels  40.8 us (31%)
  starting transfers between devices  30.6 us (23%)
  blocking collectives  29 us (22%)
  waiting for transfers between devices  28.4 us (22%)
    pallas_call x8, Pallas kernels, call(): pl.pallas_call(kernel, out_shape=out_shapes, in_specs=specs, out_specs=ja...  39.4 us
    all_to_all x2, blocking collectives, sum_over(): return lax.all_to_all(sent, axis, 0, 0, tiled=True).sum(axis=0)  29 us
    ppermute x19, waiting for transfers between devices, shift(): return lax.ppermute(value, axis, [(i, (i + by) % n) for i in range(n)])  27.3 us
    ppermute x19, starting transfers between devices, shift(): return lax.ppermute(value, axis, [(i, (i + by) % n) for i in range(n)])  23.6 us
    ppermute x1, starting transfers between devices, per_device(): aft = lax.ppermute(head, slabs, down)  5.11 us
  transfers between devices with their start and end apart: 21, of which 18 were waited for; matrix products, arithmetic and copies ran while one was open for 0% of the time, Pallas kernels for 5%

profile of v3, /device:TPU:1, one launch (start us, length us, event | category | flops | bytes accessed | tf_op | source)
XLA Modules:
  0.0 130.4 jit_solution(2709525348300020575)
XLA Ops:
  0.0 0.0 copy-start
  0.0 1.4 %shard_map.73 = (f32[1040,128]{1,0:T(8,128)S(1)}, f32[1040,128]{1,0:T(8,128)S(1)}, f32[128,128]{1,0:T(8,128)S(1)}) custom-call(f32[2048,128]{1,0:T(8,128)} %bitcast.6, f32[16,128]{1,0:T(8,128)} %bitcast.7, f32[16,128]{1,0:T(8,128)} %src_ref.1, s32[1,128]{1,0:T(1,128)} %pick_ref.1, f32[64]{0:T(128)} %table_ref.1), custom_call_target="tpu_custom_call" | custom-call | tf_op jit(solution)/shard_map/pallas_call | solution.py:556
  1.4 5.1 %collective-permute-start.1 = (f32[1040,128]{1,0:T(8,128)S(1)}, f32[1040,128]{1,0:T(8,128)S(1)}, u32[]{:S(2)}, u32[]{:S(2)}) collective-permute-start(f32[1040,128]{1,0:T(8,128)S(1)} %get-tuple-element.26.head_ref), channel_id=1, source_target_pairs={{1,0},{2,1},{3,2},{4,3},{5,4},{6,5},{7,6},{8,7},{9,8},{10,9},{11,1... | collective-permute-start | bytes 1597448 | tf_op jit(solution)/shard_map/ppermute | solution.py:576
  6.5 1.9 %collective-permute-start = (f32[1040,128]{1,0:T(8,128)S(1)}, f32[1040,128]{1,0:T(8,128)S(1)}, u32[]{:S(2)}, u32[]{:S(2)}) collective-permute-start(f32[1040,128]{1,0:T(8,128)S(1)} %get-tuple-element.27.tail_ref), channel_id=1, source_target_pairs={{0,1},{1,2},{2,3},{3,4},{4,5},{5,6},{6,7},{7,8},{8,9},{9,10},{10,1... | collective-permute-start | bytes 1597448 | tf_op jit(solution)/shard_map/ppermute | solution.py:575
  9.1 0.0 copy-done
  9.1 4.4 %shard_map.74 = (f32[16,128,128]{2,1,0:T(8,128)S(1)}, f32[16,128,128]{2,1,0:T(8,128)S(1)}, bf16[64,128]{1,0:T(8,128)(2,1)S(1)}) custom-call(s32[1]{0:T(128)S(6)} %copy.11.count_ref, f32[1040,128]{1,0:T(8,128)S(1)} %get-tuple-element.26.head_ref, f32[1040,128]{1,0:T(8,128)S(1)} %get-tuple-element.27.tail_ref, f32[128,128]{1,0:T(8,128)S(1)} %get-tuple-element.28.amp_ref, ...), custom_call_target="tpu_custom_call" | custom-call | flops 4000000000 | bytes 4000000 | tf_op jit(solution)/shard_map/pallas_call | solution.py:511
  13.6 0.0 collective-permute-done.1.aft_ref
  13.6 1.1 collective-permute-done.bef_ref
  14.7 6.6 %shard_map.75 = (f32[16,128,128]{2,1,0:T(8,128)S(1)}, f32[16,64,128]{2,1,0:T(8,128)S(1)}, f32[4,64,128]{2,1,0:T(8,128)S(1)}, f32[4,64,128]{2,1,0:T(8,128)S(1)}, ...) custom-call(s32[1]{0:T(128)S(6)} %copy.11.count_ref, f32[16,128,128]{2,1,0:T(8,128)S(1)} %get-tuple-element.29.last_ref, ...), custom_call_target="tpu_custom_call" | custom-call | tf_op jit(solution)/shard_map/pallas_call | solution.py:511
  21.2 1.2 collective-permute-start.2
  22.4 2.6 %collective-permute-start.3 = (f32[4,64,128]{2,1,0:T(8,128)S(1)}, f32[4,64,128]{2,1,0:T(8,128)S(1)}, u32[]{:S(2)}, u32[]{:S(2)}) collective-permute-start(f32[4,64,128]{2,1,0:T(8,128)S(1)} %get-tuple-element.37), channel_id=1, source_target_pairs={{0,32},{16,48},{32,0},{48,16},{1,33},{17,49},{33,1},{49,17},{2,34}... | collective-permute-start | bytes 393224 | tf_op jit(solution)/shard_map/ppermute | solution.py:532
  25.1 1.1 collective-permute-start.4
  26.1 2.1 %shard_map.76 = (f32[64,128]{1,0:T(8,128)S(1)}, bf16[5,128,64]{2,1,0:T(8,128)(2,1)S(1)}, bf16[5,64,128]{2,1,0:T(8,128)(2,1)S(1)}) custom-call(f32[16,128,128]{2,1,0:T(8,128)S(1)} %get-tuple-element.32.field_ref, f32[16,64,128]{2,1,0:T(8,128)S(1)} %get-tuple-element.33.sk_ref, s32[5,64,128]{2,1,0:T(8,128)S(1)} %bitcast.5), custom_call_target="tpu_custom_call" | custom-call | flops 2000000000 | bytes 2000000 | tf_op jit(solution)/shard_map/pallas_call | solution.py:511
  28.2 2.5 %collective-permute-done.2.r1 = f32[4,64,128]{2,1,0:T(8,128)S(1)} collective-permute-done((f32[4,64,128]{2,1,0:T(8,128)S(1)}, f32[4,64,128]{2,1,0:T(8,128)S(1)}, u32[]{:S(2)}, u32[]{:S(2)}) %collective-permute-start.2) | collective-permute-done | bytes 131104 | tf_op jit(solution)/shard_map/ppermute | solution.py:532
  30.7 0.0 collective-permute-done.3.r2
  30.7 0.6 collective-permute-done.4.r3
  31.3 1.9 %shard_map.77 = (f32[128,128]{1,0:T(8,128)S(1)}, f32[128,128]{1,0:T(8,128)S(1)}, f32[4,4,64,128]{3,2,1,0:T(8,128)S(1)}) custom-call(f32[64,128]{1,0:T(8,128)S(1)} %get-tuple-element.34.yt_ref, f32[4,64,128]{2,1,0:T(8,128)S(1)} %get-tuple-element.35.r0, f32[4,64,128]{2,1,0:T(8,128)S(1)} %collective-permute-done.2.r1, ...), custom_call_target="tpu_custom_call" | custom-call | tf_op jit(solution)/shard_map/pallas_call | solution.py:511
  33.2 0.7 collective-permute-start.5
  33.8 0.9 collective-permute-done.5
  34.8 2.3 %collective-permute-start.8 = (f32[24,128]{1,0:T(8,128)S(1)}, f32[24,128]{1,0:T(8,128)S(1)}, u32[]{:S(2)}, u32[]{:S(2)}) collective-permute-start(f32[24,128]{1,0:T(8,128)S(1)} %get-tuple-element.47), channel_id=1, source_target_pairs={{0,48},{16,0},{32,16},{48,32},{1,49},{17,1},{33,17},{49,33},{2,50}... | collective-permute-start | bytes 36872 | tf_op jit(solution)/shard_map/ppermute | solution.py:532
  37.1 0.3 collective-permute-start.7
  37.4 0.4 collective-permute-start.6
  37.8 0.2 collective-permute-done.8
  37.9 3.3 %collective-permute-done.7 = f32[24,128]{1,0:T(8,128)S(1)} collective-permute-done((f32[24,128]{1,0:T(8,128)S(1)}, f32[24,128]{1,0:T(8,128)S(1)}, u32[]{:S(2)}, u32[]{:S(2)}) %collective-permute-start.7) | collective-permute-done | bytes 12320 | tf_op jit(solution)/shard_map/ppermute | solution.py:532
  41.2 0.0 collective-permute-done.6
  41.3 17.9 %all_to_all.10 = f32[8,56,128]{2,1,0:T(8,128)S(1)} all-to-all(f32[8,56,128]{2,1,0:T(8,128)S(1)} %broadcast_in_dim.4), channel_id=1, replica_groups=mesh['x'=4,'y'=4,'z'=8,'core'=2] {'z'}, dimensions={0} | all-to-all | bytes 458752 | tf_op jit(solution)/shard_map/all_to_all | solution.py:546
  59.3 3.5 %collective-permute-start.9 = (f32[56,128]{1,0:T(8,128)S(1)}, f32[56,128]{1,0:T(8,128)S(1)}, u32[]{:S(2)}, u32[]{:S(2)}) collective-permute-start(f32[56,128]{1,0:T(8,128)S(1)} %reduce_sum.18.own_ref), channel_id=1, source_target_pairs={{0,1},{1,0},{2,3},{3,2},{4,5},{5,4},{6,7},{7,6},{8,9},{9,8},{10,11... | collective-permute-start | bytes 86024 | tf_op jit(solution)/shard_map/ppermute | solution.py:532
  62.8 0.9 collective-permute-done.9.other_ref
  63.6 3.9 %shard_map.78.p0 = f32[112,128]{1,0:T(8,128)S(1)} custom-call(f32[56,128]{1,0:T(8,128)S(1)} %reduce_sum.18.own_ref, f32[56,128]{1,0:T(8,128)S(1)} %collective-permute-done.9.other_ref, bf16[5,128,64]{2,1,0:T(8,128)(2,1)S(1)} %get-tuple-element.41.sg_ref, bf16[5,64,128]{2,1,0:T(8,128)(2,1)S(1)} %get-tuple-element.42.sgt_ref), custom_call_target="tpu_custom_call" | custom-call | tf_op jit(solution)/shard_map/pallas_call | solution.py:511
  67.5 0.5 collective-permute-start.12
  68.0 1.2 collective-permute-start.11
  69.2 0.8 collective-permute-start.10
  70.0 0.7 collective-permute-done.12.p3
  70.6 1.9 %collective-permute-done.11.p2 = f32[112,128]{1,0:T(8,128)S(1)} collective-permute-done((f32[112,128]{1,0:T(8,128)S(1)}, f32[112,128]{1,0:T(8,128)S(1)}, u32[]{:S(2)}, u32[]{:S(2)}) %collective-permute-start.11) | collective-permute-done | bytes 57376 | tf_op jit(solution)/shard_map/ppermute | solution.py:532
  72.6 1.9 %collective-permute-done.10.p1 = f32[112,128]{1,0:T(8,128)S(1)} collective-permute-done((f32[112,128]{1,0:T(8,128)S(1)}, f32[112,128]{1,0:T(8,128)S(1)}, u32[]{:S(2)}, u32[]{:S(2)}) %collective-permute-start.10) | collective-permute-done | bytes 57376 | tf_op jit(solution)/shard_map/ppermute | solution.py:532
  74.5 10.2 %shard_map.79.r0 = f32[288,128]{1,0:T(8,128)S(1)} custom-call(f32[112,128]{1,0:T(8,128)S(1)} %shard_map.78.p0, f32[112,128]{1,0:T(8,128)S(1)} %collective-permute-done.10.p1, f32[112,128]{1,0:T(8,128)S(1)} %collective-permute-done.11.p2, f32[112,128]{1,0:T(8,128)S(1)} %collective-permute-done.12.p3, f32[4,4,64,128]{3,2,1,0:T(8,128)S(1)} %get-tuple-element.43.all_ref, ...), custom_call_target="tpu_custom_call" | custom-call | tf_op jit(solution)/shard_map/pallas_call | solution.py:511
  84.7 2.8 %collective-permute-start.15 = (f32[288,128]{1,0:T(8,128)S(1)}, f32[288,128]{1,0:T(8,128)S(1)}, u32[]{:S(2)}, u32[]{:S(2)}) collective-permute-start(f32[288,128]{1,0:T(8,128)S(1)} %shard_map.79.r0), channel_id=1, source_target_pairs={{0,192},{64,0},{128,64},{192,128},{1,193},{65,1},{129,65},{193,129... | collective-permute-start | bytes 442376 | tf_op jit(solution)/shard_map/ppermute | solution.py:532
  87.5 0.5 collective-permute-start.14
  88.0 0.6 collective-permute-start.13
  88.6 2.2 %collective-permute-done.15.r3 = f32[288,128]{1,0:T(8,128)S(1)} collective-permute-done((f32[288,128]{1,0:T(8,128)S(1)}, f32[288,128]{1,0:T(8,128)S(1)}, u32[]{:S(2)}, u32[]{:S(2)}) %collective-permute-start.15) | collective-permute-done | bytes 147488 | tf_op jit(solution)/shard_map/ppermute | solution.py:532
  90.8 2.3 %collective-permute-done.14.r2 = f32[288,128]{1,0:T(8,128)S(1)} collective-permute-done((f32[288,128]{1,0:T(8,128)S(1)}, f32[288,128]{1,0:T(8,128)S(1)}, u32[]{:S(2)}, u32[]{:S(2)}) %collective-permute-start.14) | collective-permute-done | bytes 147488 | tf_op jit(solution)/shard_map/ppermute | solution.py:532
  93.1 4.7 %collective-permute-done.13.r1 = f32[288,128]{1,0:T(8,128)S(1)} collective-permute-done((f32[288,128]{1,0:T(8,128)S(1)}, f32[288,128]{1,0:T(8,128)S(1)}, u32[]{:S(2)}, u32[]{:S(2)}) %collective-permute-start.13) | collective-permute-done | bytes 147488 | tf_op jit(solution)/shard_map/ppermute | solution.py:532
  97.7 1.1 shard_map.80
  98.8 0.7 collective-permute-start.16
  99.6 0.8 collective-permute-done.16
  100.4 0.3 collective-permute-start.19
  100.8 0.5 collective-permute-start.18
  101.3 0.6 collective-permute-start.17
  101.9 1.2 collective-permute-done.19
  103.1 1.9 %collective-permute-done.18 = f32[48,128]{1,0:T(8,128)S(1)} collective-permute-done((f32[48,128]{1,0:T(8,128)S(1)}, f32[48,128]{1,0:T(8,128)S(1)}, u32[]{:S(2)}, u32[]{:S(2)}) %collective-permute-start.18) | collective-permute-done | bytes 24608 | tf_op jit(solution)/shard_map/ppermute | solution.py:532
  105.0 0.5 collective-permute-done.17
  105.5 11.1 %all_to_all.11 = f32[8,48,128]{2,1,0:T(8,128)S(1)} all-to-all(f32[8,48,128]{2,1,0:T(8,128)S(1)} %broadcast_in_dim.5), channel_id=1, replica_groups=mesh['x'=4,'y'=4,'z'=8,'core'=2] {'z'}, dimensions={0} | all-to-all | bytes 393216 | tf_op jit(solution)/shard_map/all_to_all | solution.py:546
  116.6 3.0 %collective-permute-start.20 = (f32[48,128]{1,0:T(8,128)S(1)}, f32[48,128]{1,0:T(8,128)S(1)}, u32[]{:S(2)}, u32[]{:S(2)}) collective-permute-start(f32[48,128]{1,0:T(8,128)S(1)} %reduce_sum.19.own_ref), channel_id=1, source_target_pairs={{0,1},{1,0},{2,3},{3,2},{4,5},{5,4},{6,7},{7,6},{8,9},{9,8},{10,11... | collective-permute-start | bytes 73736 | tf_op jit(solution)/shard_map/ppermute | solution.py:532
  119.6 0.8 collective-permute-done.20.other_ref
  120.4 9.3 %shard_map.81 = f32[64,128]{1,0:T(8,128)S(1)} custom-call(f32[48,128]{1,0:T(8,128)S(1)} %reduce_sum.19.own_ref, f32[48,128]{1,0:T(8,128)S(1)} %collective-permute-done.20.other_ref, f32[288,128]{1,0:T(8,128)S(1)} %shard_map.79.r0, f32[288,128]{1,0:T(8,128)S(1)} %collective-permute-done.13.r1, f32[288,128]{1,0:T(8,128)S(1)} %collective-permute-done.14.r2, ...), custom_call_target="tpu_custom_call" | custom-call | tf_op jit(solution)/shard_map/pallas_call | solution.py:511
  129.7 0.7 copy.10
  (11 shorter events, 0.1 us)
Async XLA Ops:
  0.0 9.1 %copy-start = (s32[5,128,64]{1,2,0:T(8,128)S(1)}, s32[5,128,64]{1,2,0:T(8,128)}, u32[]{:S(2)}) copy-start(s32[5,128,64]{1,2,0:T(8,128)} %param.13) | copy-start | bytes 491524
  1.4 12.1 %collective-permute-start.1 = (f32[1040,128]{1,0:T(8,128)S(1)}, f32[1040,128]{1,0:T(8,128)S(1)}, u32[]{:S(2)}, u32[]{:S(2)}) collective-permute-start(f32[1040,128]{1,0:T(8,128)S(1)} %get-tuple-element.26.head_ref), channel_id=1, source_target_pairs={{1,0},{2,1},{3,2},{4,3},{5,4},{6,5},{7,6},{8,7},{9,8},{10,9},{11,1... | collective-permute-start | bytes 1597448 | tf_op jit(solution)/shard_map/ppermute | solution.py:576
  6.5 8.1 %collective-permute-start = (f32[1040,128]{1,0:T(8,128)S(1)}, f32[1040,128]{1,0:T(8,128)S(1)}, u32[]{:S(2)}, u32[]{:S(2)}) collective-permute-start(f32[1040,128]{1,0:T(8,128)S(1)} %get-tuple-element.27.tail_ref), channel_id=1, source_target_pairs={{0,1},{1,2},{2,3},{3,4},{4,5},{5,6},{6,7},{7,8},{8,9},{9,10},{10,1... | collective-permute-start | bytes 1597448 | tf_op jit(solution)/shard_map/ppermute | solution.py:575
  21.2 9.4 %collective-permute-start.2 = (f32[4,64,128]{2,1,0:T(8,128)S(1)}, f32[4,64,128]{2,1,0:T(8,128)S(1)}, u32[]{:S(2)}, u32[]{:S(2)}) collective-permute-start(f32[4,64,128]{2,1,0:T(8,128)S(1)} %get-tuple-element.36), channel_id=1, source_target_pairs={{0,16},{16,32},{32,48},{48,0},{1,17},{17,33},{33,49},{49,1},{2,18}... | collective-permute-start | bytes 393224 | tf_op jit(solution)/shard_map/ppermute | solution.py:532
  22.4 8.2 %collective-permute-start.3 = (f32[4,64,128]{2,1,0:T(8,128)S(1)}, f32[4,64,128]{2,1,0:T(8,128)S(1)}, u32[]{:S(2)}, u32[]{:S(2)}) collective-permute-start(f32[4,64,128]{2,1,0:T(8,128)S(1)} %get-tuple-element.37), channel_id=1, source_target_pairs={{0,32},{16,48},{32,0},{48,16},{1,33},{17,49},{33,1},{49,17},{2,34}... | collective-permute-start | bytes 393224 | tf_op jit(solution)/shard_map/ppermute | solution.py:532
  25.1 6.2 %collective-permute-start.4 = (f32[4,64,128]{2,1,0:T(8,128)S(1)}, f32[4,64,128]{2,1,0:T(8,128)S(1)}, u32[]{:S(2)}, u32[]{:S(2)}) collective-permute-start(f32[4,64,128]{2,1,0:T(8,128)S(1)} %get-tuple-element.38), channel_id=1, source_target_pairs={{0,48},{16,0},{32,16},{48,32},{1,49},{17,1},{33,17},{49,33},{2,50}... | collective-permute-start | bytes 393224 | tf_op jit(solution)/shard_map/ppermute | solution.py:532
  33.2 1.6 %collective-permute-start.5 = (f32[128,128]{1,0:T(8,128)S(1)}, f32[128,128]{1,0:T(8,128)S(1)}, u32[]{:S(2)}, u32[]{:S(2)}) collective-permute-start(f32[128,128]{1,0:T(8,128)S(1)} %get-tuple-element.40), channel_id=1, source_target_pairs={{0,1},{1,0},{2,3},{3,2},{4,5},{5,4},{6,7},{7,6},{8,9},{9,8},{10,11... | collective-permute-start | bytes 196616 | tf_op jit(solution)/shard_map/ppermute | solution.py:532
  34.8 3.2 %collective-permute-start.8 = (f32[24,128]{1,0:T(8,128)S(1)}, f32[24,128]{1,0:T(8,128)S(1)}, u32[]{:S(2)}, u32[]{:S(2)}) collective-permute-start(f32[24,128]{1,0:T(8,128)S(1)} %get-tuple-element.47), channel_id=1, source_target_pairs={{0,48},{16,0},{32,16},{48,32},{1,49},{17,1},{33,17},{49,33},{2,50}... | collective-permute-start | bytes 36872 | tf_op jit(solution)/shard_map/ppermute | solution.py:532
  37.1 4.2 %collective-permute-start.7 = (f32[24,128]{1,0:T(8,128)S(1)}, f32[24,128]{1,0:T(8,128)S(1)}, u32[]{:S(2)}, u32[]{:S(2)}) collective-permute-start(f32[24,128]{1,0:T(8,128)S(1)} %get-tuple-element.48), channel_id=1, source_target_pairs={{0,32},{16,48},{32,0},{48,16},{1,33},{17,49},{33,1},{49,17},{2,34}... | collective-permute-start | bytes 36872 | tf_op jit(solution)/shard_map/ppermute | solution.py:532
  37.4 3.9 %collective-permute-start.6 = (f32[24,128]{1,0:T(8,128)S(1)}, f32[24,128]{1,0:T(8,128)S(1)}, u32[]{:S(2)}, u32[]{:S(2)}) collective-permute-start(f32[24,128]{1,0:T(8,128)S(1)} %get-tuple-element.49), channel_id=1, source_target_pairs={{0,16},{16,32},{32,48},{48,0},{1,17},{17,33},{33,49},{49,1},{2,18}... | collective-permute-start | bytes 36872 | tf_op jit(solution)/shard_map/ppermute | solution.py:532
  59.3 4.4 %collective-permute-start.9 = (f32[56,128]{1,0:T(8,128)S(1)}, f32[56,128]{1,0:T(8,128)S(1)}, u32[]{:S(2)}, u32[]{:S(2)}) collective-permute-start(f32[56,128]{1,0:T(8,128)S(1)} %reduce_sum.18.own_ref), channel_id=1, source_target_pairs={{0,1},{1,0},{2,3},{3,2},{4,5},{5,4},{6,7},{7,6},{8,9},{9,8},{10,11... | collective-permute-start | bytes 86024 | tf_op jit(solution)/shard_map/ppermute | solution.py:532
  67.5 3.1 %collective-permute-start.12 = (f32[112,128]{1,0:T(8,128)S(1)}, f32[112,128]{1,0:T(8,128)S(1)}, u32[]{:S(2)}, u32[]{:S(2)}) collective-permute-start(f32[112,128]{1,0:T(8,128)S(1)} %shard_map.78.p0), channel_id=1, source_target_pairs={{0,48},{16,0},{32,16},{48,32},{1,49},{17,1},{33,17},{49,33},{2,50}... | collective-permute-start | bytes 172040 | tf_op jit(solution)/shard_map/ppermute | solution.py:532
  68.0 4.5 %collective-permute-start.11 = (f32[112,128]{1,0:T(8,128)S(1)}, f32[112,128]{1,0:T(8,128)S(1)}, u32[]{:S(2)}, u32[]{:S(2)}) collective-permute-start(f32[112,128]{1,0:T(8,128)S(1)} %shard_map.78.p0), channel_id=1, source_target_pairs={{0,32},{16,48},{32,0},{48,16},{1,33},{17,49},{33,1},{49,17},{2,34}... | collective-permute-start | bytes 172040 | tf_op jit(solution)/shard_map/ppermute | solution.py:532
  69.2 5.3 %collective-permute-start.10 = (f32[112,128]{1,0:T(8,128)S(1)}, f32[112,128]{1,0:T(8,128)S(1)}, u32[]{:S(2)}, u32[]{:S(2)}) collective-permute-start(f32[112,128]{1,0:T(8,128)S(1)} %shard_map.78.p0), channel_id=1, source_target_pairs={{0,16},{16,32},{32,48},{48,0},{1,17},{17,33},{33,49},{49,1},{2,18}... | collective-permute-start | bytes 172040 | tf_op jit(solution)/shard_map/ppermute | solution.py:532
  84.7 6.1 %collective-permute-start.15 = (f32[288,128]{1,0:T(8,128)S(1)}, f32[288,128]{1,0:T(8,128)S(1)}, u32[]{:S(2)}, u32[]{:S(2)}) collective-permute-start(f32[288,128]{1,0:T(8,128)S(1)} %shard_map.79.r0), channel_id=1, source_target_pairs={{0,192},{64,0},{128,64},{192,128},{1,193},{65,1},{129,65},{193,129... | collective-permute-start | bytes 442376 | tf_op jit(solution)/shard_map/ppermute | solution.py:532
  87.5 5.6 %collective-permute-start.14 = (f32[288,128]{1,0:T(8,128)S(1)}, f32[288,128]{1,0:T(8,128)S(1)}, u32[]{:S(2)}, u32[]{:S(2)}) collective-permute-start(f32[288,128]{1,0:T(8,128)S(1)} %shard_map.79.r0), channel_id=1, source_target_pairs={{0,128},{64,192},{128,0},{192,64},{1,129},{65,193},{129,1},{193,65... | collective-permute-start | bytes 442376 | tf_op jit(solution)/shard_map/ppermute | solution.py:532
  88.0 9.7 %collective-permute-start.13 = (f32[288,128]{1,0:T(8,128)S(1)}, f32[288,128]{1,0:T(8,128)S(1)}, u32[]{:S(2)}, u32[]{:S(2)}) collective-permute-start(f32[288,128]{1,0:T(8,128)S(1)} %shard_map.79.r0), channel_id=1, source_target_pairs={{0,64},{64,128},{128,192},{192,0},{1,65},{65,129},{129,193},{193,1... | collective-permute-start | bytes 442376 | tf_op jit(solution)/shard_map/ppermute | solution.py:532
  98.8 1.6 %collective-permute-start.16 = (f32[48,128]{1,0:T(8,128)S(1)}, f32[48,128]{1,0:T(8,128)S(1)}, u32[]{:S(2)}, u32[]{:S(2)}) collective-permute-start(f32[48,128]{1,0:T(8,128)S(1)} %get-tuple-element.45), channel_id=1, source_target_pairs={{0,1},{1,0},{2,3},{3,2},{4,5},{5,4},{6,7},{7,6},{8,9},{9,8},{10,11... | collective-permute-start | bytes 73736 | tf_op jit(solution)/shard_map/ppermute | solution.py:532
  100.4 2.7 %collective-permute-start.19 = (f32[48,128]{1,0:T(8,128)S(1)}, f32[48,128]{1,0:T(8,128)S(1)}, u32[]{:S(2)}, u32[]{:S(2)}) collective-permute-start(f32[48,128]{1,0:T(8,128)S(1)} %add.28), channel_id=1, source_target_pairs={{0,48},{16,0},{32,16},{48,32},{1,49},{17,1},{33,17},{49,33},{2,50}... | collective-permute-start | bytes 73736 | tf_op jit(solution)/shard_map/ppermute | solution.py:532
  100.8 4.2 %collective-permute-start.18 = (f32[48,128]{1,0:T(8,128)S(1)}, f32[48,128]{1,0:T(8,128)S(1)}, u32[]{:S(2)}, u32[]{:S(2)}) collective-permute-start(f32[48,128]{1,0:T(8,128)S(1)} %add.28), channel_id=1, source_target_pairs={{0,32},{16,48},{32,0},{48,16},{1,33},{17,49},{33,1},{49,17},{2,34}... | collective-permute-start | bytes 73736 | tf_op jit(solution)/shard_map/ppermute | solution.py:532
  101.3 4.2 %collective-permute-start.17 = (f32[48,128]{1,0:T(8,128)S(1)}, f32[48,128]{1,0:T(8,128)S(1)}, u32[]{:S(2)}, u32[]{:S(2)}) collective-permute-start(f32[48,128]{1,0:T(8,128)S(1)} %add.28), channel_id=1, source_target_pairs={{0,16},{16,32},{32,48},{48,0},{1,17},{17,33},{33,49},{49,1},{2,18}... | collective-permute-start | bytes 73736 | tf_op jit(solution)/shard_map/ppermute | solution.py:532
  116.6 3.8 %collective-permute-start.20 = (f32[48,128]{1,0:T(8,128)S(1)}, f32[48,128]{1,0:T(8,128)S(1)}, u32[]{:S(2)}, u32[]{:S(2)}) collective-permute-start(f32[48,128]{1,0:T(8,128)S(1)} %reduce_sum.19.own_ref), channel_id=1, source_target_pairs={{0,1},{1,0},{2,3},{3,2},{4,5},{5,4},{6,7},{7,6},{8,9},{9,8},{10,11... | collective-permute-start | bytes 73736 | tf_op jit(solution)/shard_map/ppermute | solution.py:532

commit v4 on v3

--- a/solution.py
+++ b/solution.py
@@ -202,7 +202,7 @@
 
 def pack_kernel(
     x_ref, rate_ref, src_ref, pick_ref, table_ref,
-    head_ref, tail_ref, amp_ref, x_s, pick_s, table_s, sems,
+    ends_ref, cross_ref, chip_ref, amp_ref, x_s, pick_s, table_s, sems,
 ):
     parts = [
         pltpu.make_async_copy(
@@ -211,7 +211,7 @@
         for n in range(4)
     ]
     edges = []
-    for half, out in enumerate((head_ref, tail_ref)):
+    for half, out in enumerate((ends_ref.at[0], ends_ref.at[1])):
         for n, ref in enumerate((rate_ref, src_ref)):
             edges.append(
                 pltpu.make_async_copy(
@@ -240,7 +240,7 @@
     lax.fori_loop(0, 16, amplitude, 0)
 
     def block(b, carry):
-        for half, out in enumerate((head_ref, tail_ref)):
+        for half, out in enumerate((ends_ref.at[0], ends_ref.at[1])):
             start = pl.multiple_of(b * 128, 8) + 8 * half
             vals = turned([x_s[pl.ds(start + 16 * i, 8), :] for i in range(8)])
             for r in range(8):
@@ -252,12 +252,16 @@
         lax.fori_loop(4 * n, 4 * n + 4, block, 0)
     for copy in edges:
         copy.wait()
+    core = lax.axis_index("core")
+    cross_ref[...] = ends_ref[core]
+    chip_ref[...] = ends_ref[1 - core]
 
 
 def inner_kernel(
-    count_ref, head_ref, tail_ref, amp_ref, bits_ref,
+    count_ref, ends_ref, amp_ref, bits_ref,
     last_ref, prev_ref, sgt_ref, c_s, h_s, src_s, f_s,
 ):
+    head_ref, tail_ref = ends_ref.at[0], ends_ref.at[1]
     sgt_ref[...] = (2.0 * bits_ref[0].astype(F32) - 1.0).astype(jnp.bfloat16)
     for r in range(16):
         ref, at = (head_ref, 1024 + r) if r < 8 else (tail_ref, 1016 + r)
@@ -301,9 +305,14 @@
 
 
 def flow_kernel(
-    count_ref, last_ref, prev_ref, bef_ref, aft_ref, head_ref, tail_ref, amp_ref, sgt_ref,
-    field_ref, sk_ref, d0, d1, d2, d3, c_s, h_s, src_s, f_s, s_s,
+    count_ref, last_ref, prev_ref, cross_ref, chip_ref, ends_ref, amp_ref, sgt_ref,
+    field_ref, sk_ref, d0, d1, d2, d3, c_s, h_s, src_s, f_s, s_s, halo_s,
 ):
+    core = lax.axis_index("core")
+    halo_s[core] = cross_ref[...]
+    halo_s[1 - core] = chip_ref[...]
+    bef_ref, aft_ref = halo_s.at[0], halo_s.at[1]
+    head_ref, tail_ref = ends_ref.at[0], ends_ref.at[1]
     for r in range(32):
         ref = (bef_ref, head_ref, tail_ref, aft_ref)[r // 8]
         at = 1024 + r % 8
@@ -551,13 +560,12 @@
     rate = coef[0]
     slabs = ("z", "core")
     n = lax.axis_size(slabs)
-    up = [(i, i + 1) for i in range(n - 1)]
-    down = [(i + 1, i) for i in range(n - 1)]
-    head, tail, amp = pl.pallas_call(
+    between = [(i, i + 1) for i in range(1, n - 1, 2)] + [(i, i - 1) for i in range(2, n, 2)]
+    ends, cross, chip, amp = pl.pallas_call(
         pack_kernel,
-        out_shape=(shape(1040, 128), shape(1040, 128), shape(128, 128)),
+        out_shape=(shape(2, 1040, 128), shape(1040, 128), shape(1040, 128), shape(128, 128)),
         in_specs=[pl.BlockSpec(memory_space=pltpu.HBM)] * 5,
-        out_specs=(VMEM,) * 3,
+        out_specs=(VMEM,) * 4,
         scratch_shapes=[
             pltpu.VMEM((2048, 128), F32),
             pltpu.SMEM((1, 128), jnp.int32),
@@ -572,8 +580,8 @@
         )
     )
     bits = jnp.swapaxes(sketch_signs, 1, 2)
-    bef = lax.ppermute(tail, slabs, up)
-    aft = lax.ppermute(head, slabs, down)
+    cross = lax.ppermute(cross, slabs, between)
+    chip = shift(chip, "core", 1)
     last, prev, first_signs = call(
         inner_kernel,
         (
@@ -583,8 +591,7 @@
         ),
         1,
         step_counts,
-        head,
-        tail,
+        ends,
         amp,
         bits,
         scratch=[pltpu.VMEM((128, 128), F32)] * 3 + [pltpu.VMEM((2, 128, 128), F32)],
@@ -597,14 +604,17 @@
         step_counts,
         last,
         prev,
-        bef,
-        aft,
-        head,
-        tail,
+        cross,
+        chip,
+        ends,
         amp,
         first_signs,
         scratch=[pltpu.VMEM((256, 128), F32)] * 3
-        + [pltpu.VMEM((2, 256, 128), F32), pltpu.VMEM((4, 4, 64, 128), F32)],
+        + [
+            pltpu.VMEM((2, 256, 128), F32),
+            pltpu.VMEM((4, 4, 64, 128), F32),
+            pltpu.VMEM((2, 1040, 128), F32),
+        ],
     )
     yt, signs, signs_t = call(
         leaf_sum_kernel,

time: 131 us -> 129 us (0.985)
  starting transfers between devices: 30.6 us -> 28.7 us
    ppermute x2 -> x1, starting transfers between devices: 7.03 us -> 4.92 us  [per_device(): cross = lax.ppermute(cross, slabs, between)]
    ppermute x19 -> x20, starting transfers between devices: 23.6 us -> 23.8 us  [shift(): return lax.ppermute(value, axis, [(i, (i + by) % n) for i in range(n)])]
    ppermute x19 -> x20, waiting for transfers between devices: 27.3 us -> 27.1 us  [shift(): return lax.ppermute(value, axis, [(i, (i + by) % n) for i in range(n)])]
  transfers between devices with their start and end apart: 21 -> 21, of which waited for: 18 -> 17; matrix products, arithmetic and copies ran while one was open for 0% -> 0% of each run, Pallas kernels for 5% -> 5%
where the time goes in v4:
time: 129 us
  Pallas kernels  41 us (32%)
  waiting for transfers between devices  28.9 us (22%)
  blocking collectives  28.8 us (22%)
  starting transfers between devices  28.7 us (22%)
    pallas_call x8, Pallas kernels, call(): pl.pallas_call(kernel, out_shape=out_shapes, in_specs=specs, out_specs=ja...  39.5 us
    all_to_all x2, blocking collectives, sum_over(): return lax.all_to_all(sent, axis, 0, 0, tiled=True).sum(axis=0)  28.8 us
    ppermute x20, waiting for transfers between devices, shift(): return lax.ppermute(value, axis, [(i, (i + by) % n) for i in range(n)])  27.1 us
    ppermute x20, starting transfers between devices, shift(): return lax.ppermute(value, axis, [(i, (i + by) % n) for i in range(n)])  23.8 us
    ppermute x1, starting transfers between devices, per_device(): cross = lax.ppermute(cross, slabs, between)  4.92 us
  transfers between devices with their start and end apart: 21, of which 17 were waited for; matrix products, arithmetic and copies ran while one was open for 0% of the time, Pallas kernels for 5%

profile of v4, /device:TPU:1, one launch (start us, length us, event | category | flops | bytes accessed | tf_op | source)
XLA Modules:
  0.0 129.0 jit_solution(11912952672724826849)
XLA Ops:
  0.0 0.0 copy-start
  0.0 1.5 %shard_map.73 = (f32[2,1040,128]{2,1,0:T(8,128)S(1)}, f32[1040,128]{1,0:T(8,128)S(1)}, f32[1040,128]{1,0:T(8,128)S(1)}, f32[128,128]{1,0:T(8,128)S(1)}) custom-call(f32[2048,128]{1,0:T(8,128)} %bitcast.6, f32[16,128]{1,0:T(8,128)} %bitcast.7, f32[16,128]{1,0:T(8,128)} %src_ref.1, s32[1,128]{1,0:T(1,128)} %pick_ref.1, f32[64]{0:T(128)} %table_ref.1), custom_call_target="tpu_custom_call" | custom-call | tf_op jit(solution)/shard_map/pallas_call | solution.py:564
  1.5 4.9 %collective-permute-start = (f32[1040,128]{1,0:T(8,128)S(1)}, f32[1040,128]{1,0:T(8,128)S(1)}, u32[]{:S(2)}, u32[]{:S(2)}) collective-permute-start(f32[1040,128]{1,0:T(8,128)S(1)} %get-tuple-element.31), channel_id=1, source_target_pairs={{1,2},{3,4},{5,6},{7,8},{9,10},{11,12},{13,14},{2,1},{4,3},{6,5},{... | collective-permute-start | bytes 1597448 | tf_op jit(solution)/shard_map/ppermute | solution.py:583
  6.4 0.1 collective-permute-start.1
  7.2 0.0 copy-done
  7.2 4.4 %shard_map.74 = (f32[16,128,128]{2,1,0:T(8,128)S(1)}, f32[16,128,128]{2,1,0:T(8,128)S(1)}, bf16[64,128]{1,0:T(8,128)(2,1)S(1)}) custom-call(s32[1]{0:T(128)S(6)} %copy.11.count_ref, f32[2,1040,128]{2,1,0:T(8,128)S(1)} %get-tuple-element.27.ends_ref, f32[128,128]{1,0:T(8,128)S(1)} %get-tuple-element.28.amp_ref, s32[5,64,128]{2,1,0:T(8,128)S(1)} %bitcast.4), custom_call_target="tpu_custom_call" | custom-call | flops 4000000000 | bytes 4000000 | tf_op jit(solution)/shard_map/pallas_call | solution.py:520
  11.6 1.8 %collective-permute-done.cross_ref = f32[1040,128]{1,0:T(8,128)S(1)} collective-permute-done((f32[1040,128]{1,0:T(8,128)S(1)}, f32[1040,128]{1,0:T(8,128)S(1)}, u32[]{:S(2)}, u32[]{:S(2)}) %collective-permute-start) | collective-permute-done | bytes 532512 | tf_op jit(solution)/shard_map/ppermute | solution.py:583
  13.4 0.0 collective-permute-done.1.chip_ref
  13.4 6.7 %shard_map.75 = (f32[16,128,128]{2,1,0:T(8,128)S(1)}, f32[16,64,128]{2,1,0:T(8,128)S(1)}, f32[4,64,128]{2,1,0:T(8,128)S(1)}, f32[4,64,128]{2,1,0:T(8,128)S(1)}, ...) custom-call(s32[1]{0:T(128)S(6)} %copy.11.count_ref, f32[16,128,128]{2,1,0:T(8,128)S(1)} %get-tuple-element.29.last_ref, ...), custom_call_target="tpu_custom_call" | custom-call | tf_op jit(solution)/shard_map/pallas_call | solution.py:520
  20.0 1.4 %collective-permute-start.2 = (f32[4,64,128]{2,1,0:T(8,128)S(1)}, f32[4,64,128]{2,1,0:T(8,128)S(1)}, u32[]{:S(2)}, u32[]{:S(2)}) collective-permute-start(f32[4,64,128]{2,1,0:T(8,128)S(1)} %get-tuple-element.38), channel_id=1, source_target_pairs={{0,16},{16,32},{32,48},{48,0},{1,17},{17,33},{33,49},{49,1},{2,18}... | collective-permute-start | bytes 393224 | tf_op jit(solution)/shard_map/ppermute | solution.py:541
  21.4 2.6 %collective-permute-start.3 = (f32[4,64,128]{2,1,0:T(8,128)S(1)}, f32[4,64,128]{2,1,0:T(8,128)S(1)}, u32[]{:S(2)}, u32[]{:S(2)}) collective-permute-start(f32[4,64,128]{2,1,0:T(8,128)S(1)} %get-tuple-element.39), channel_id=1, source_target_pairs={{0,32},{16,48},{32,0},{48,16},{1,33},{17,49},{33,1},{49,17},{2,34}... | collective-permute-start | bytes 393224 | tf_op jit(solution)/shard_map/ppermute | solution.py:541
  24.0 1.1 collective-permute-start.4
  25.1 2.1 %shard_map.76 = (f32[64,128]{1,0:T(8,128)S(1)}, bf16[5,128,64]{2,1,0:T(8,128)(2,1)S(1)}, bf16[5,64,128]{2,1,0:T(8,128)(2,1)S(1)}) custom-call(f32[16,128,128]{2,1,0:T(8,128)S(1)} %get-tuple-element.34.field_ref, f32[16,64,128]{2,1,0:T(8,128)S(1)} %get-tuple-element.35.sk_ref, s32[5,64,128]{2,1,0:T(8,128)S(1)} %bitcast.5), custom_call_target="tpu_custom_call" | custom-call | flops 2000000000 | bytes 2000000 | tf_op jit(solution)/shard_map/pallas_call | solution.py:520
  27.2 0.0 collective-permute-done.2.r1
  27.2 2.6 %collective-permute-done.3.r2 = f32[4,64,128]{2,1,0:T(8,128)S(1)} collective-permute-done((f32[4,64,128]{2,1,0:T(8,128)S(1)}, f32[4,64,128]{2,1,0:T(8,128)S(1)}, u32[]{:S(2)}, u32[]{:S(2)}) %collective-permute-start.3) | collective-permute-done | bytes 131104 | tf_op jit(solution)/shard_map/ppermute | solution.py:541
  29.8 0.0 collective-permute-done.4.r3
  29.8 1.9 %shard_map.77 = (f32[128,128]{1,0:T(8,128)S(1)}, f32[128,128]{1,0:T(8,128)S(1)}, f32[4,4,64,128]{3,2,1,0:T(8,128)S(1)}) custom-call(f32[64,128]{1,0:T(8,128)S(1)} %get-tuple-element.36.yt_ref, f32[4,64,128]{2,1,0:T(8,128)S(1)} %get-tuple-element.37.r0, f32[4,64,128]{2,1,0:T(8,128)S(1)} %collective-permute-done.2.r1, ...), custom_call_target="tpu_custom_call" | custom-call | tf_op jit(solution)/shard_map/pallas_call | solution.py:520
  31.7 0.1 collective-permute-start.5
  31.8 1.2 collective-permute-done.5
  33.1 2.4 %collective-permute-start.8 = (f32[24,128]{1,0:T(8,128)S(1)}, f32[24,128]{1,0:T(8,128)S(1)}, u32[]{:S(2)}, u32[]{:S(2)}) collective-permute-start(f32[24,128]{1,0:T(8,128)S(1)} %get-tuple-element.49), channel_id=1, source_target_pairs={{0,48},{16,0},{32,16},{48,32},{1,49},{17,1},{33,17},{49,33},{2,50}... | collective-permute-start | bytes 36872 | tf_op jit(solution)/shard_map/ppermute | solution.py:541
  35.4 0.9 collective-permute-start.7
  36.3 0.3 collective-permute-start.6
  36.6 0.0 collective-permute-done.8
  36.6 2.9 %collective-permute-done.7 = f32[24,128]{1,0:T(8,128)S(1)} collective-permute-done((f32[24,128]{1,0:T(8,128)S(1)}, f32[24,128]{1,0:T(8,128)S(1)}, u32[]{:S(2)}, u32[]{:S(2)}) %collective-permute-start.7) | collective-permute-done | bytes 12320 | tf_op jit(solution)/shard_map/ppermute | solution.py:541
  39.5 0.6 collective-permute-done.6
  40.1 17.7 %all_to_all.10 = f32[8,56,128]{2,1,0:T(8,128)S(1)} all-to-all(f32[8,56,128]{2,1,0:T(8,128)S(1)} %broadcast_in_dim.4), channel_id=1, replica_groups=mesh['x'=4,'y'=4,'z'=8,'core'=2] {'z'}, dimensions={0} | all-to-all | bytes 458752 | tf_op jit(solution)/shard_map/all_to_all | solution.py:555
  57.8 3.6 %collective-permute-start.9 = (f32[56,128]{1,0:T(8,128)S(1)}, f32[56,128]{1,0:T(8,128)S(1)}, u32[]{:S(2)}, u32[]{:S(2)}) collective-permute-start(f32[56,128]{1,0:T(8,128)S(1)} %reduce_sum.18.own_ref), channel_id=1, source_target_pairs={{0,1},{1,0},{2,3},{3,2},{4,5},{5,4},{6,7},{7,6},{8,9},{9,8},{10,11... | collective-permute-start | bytes 86024 | tf_op jit(solution)/shard_map/ppermute | solution.py:541
  61.4 0.9 collective-permute-done.9.other_ref
  62.2 3.9 %shard_map.78.p0 = f32[112,128]{1,0:T(8,128)S(1)} custom-call(f32[56,128]{1,0:T(8,128)S(1)} %reduce_sum.18.own_ref, f32[56,128]{1,0:T(8,128)S(1)} %collective-permute-done.9.other_ref, bf16[5,128,64]{2,1,0:T(8,128)(2,1)S(1)} %get-tuple-element.43.sg_ref, bf16[5,64,128]{2,1,0:T(8,128)(2,1)S(1)} %get-tuple-element.44.sgt_ref), custom_call_target="tpu_custom_call" | custom-call | tf_op jit(solution)/shard_map/pallas_call | solution.py:520
  66.1 0.4 collective-permute-start.12
  66.5 1.2 collective-permute-start.11
  67.7 0.8 collective-permute-start.10
  68.4 0.8 collective-permute-done.12.p3
  69.2 1.8 %collective-permute-done.11.p2 = f32[112,128]{1,0:T(8,128)S(1)} collective-permute-done((f32[112,128]{1,0:T(8,128)S(1)}, f32[112,128]{1,0:T(8,128)S(1)}, u32[]{:S(2)}, u32[]{:S(2)}) %collective-permute-start.11) | collective-permute-done | bytes 57376 | tf_op jit(solution)/shard_map/ppermute | solution.py:541
  71.0 1.9 %collective-permute-done.10.p1 = f32[112,128]{1,0:T(8,128)S(1)} collective-permute-done((f32[112,128]{1,0:T(8,128)S(1)}, f32[112,128]{1,0:T(8,128)S(1)}, u32[]{:S(2)}, u32[]{:S(2)}) %collective-permute-start.10) | collective-permute-done | bytes 57376 | tf_op jit(solution)/shard_map/ppermute | solution.py:541
  73.0 10.2 %shard_map.79.r0 = f32[288,128]{1,0:T(8,128)S(1)} custom-call(f32[112,128]{1,0:T(8,128)S(1)} %shard_map.78.p0, f32[112,128]{1,0:T(8,128)S(1)} %collective-permute-done.10.p1, f32[112,128]{1,0:T(8,128)S(1)} %collective-permute-done.11.p2, f32[112,128]{1,0:T(8,128)S(1)} %collective-permute-done.12.p3, f32[4,4,64,128]{3,2,1,0:T(8,128)S(1)} %get-tuple-element.45.all_ref, ...), custom_call_target="tpu_custom_call" | custom-call | tf_op jit(solution)/shard_map/pallas_call | solution.py:520
  83.2 2.8 %collective-permute-start.15 = (f32[288,128]{1,0:T(8,128)S(1)}, f32[288,128]{1,0:T(8,128)S(1)}, u32[]{:S(2)}, u32[]{:S(2)}) collective-permute-start(f32[288,128]{1,0:T(8,128)S(1)} %shard_map.79.r0), channel_id=1, source_target_pairs={{0,192},{64,0},{128,64},{192,128},{1,193},{65,1},{129,65},{193,129... | collective-permute-start | bytes 442376 | tf_op jit(solution)/shard_map/ppermute | solution.py:541
  85.9 0.5 collective-permute-start.14
  86.5 0.6 collective-permute-start.13
  87.1 2.2 %collective-permute-done.15.r3 = f32[288,128]{1,0:T(8,128)S(1)} collective-permute-done((f32[288,128]{1,0:T(8,128)S(1)}, f32[288,128]{1,0:T(8,128)S(1)}, u32[]{:S(2)}, u32[]{:S(2)}) %collective-permute-start.15) | collective-permute-done | bytes 147488 | tf_op jit(solution)/shard_map/ppermute | solution.py:541
  89.2 2.3 %collective-permute-done.14.r2 = f32[288,128]{1,0:T(8,128)S(1)} collective-permute-done((f32[288,128]{1,0:T(8,128)S(1)}, f32[288,128]{1,0:T(8,128)S(1)}, u32[]{:S(2)}, u32[]{:S(2)}) %collective-permute-start.14) | collective-permute-done | bytes 147488 | tf_op jit(solution)/shard_map/ppermute | solution.py:541
  91.5 4.6 %collective-permute-done.13.r1 = f32[288,128]{1,0:T(8,128)S(1)} collective-permute-done((f32[288,128]{1,0:T(8,128)S(1)}, f32[288,128]{1,0:T(8,128)S(1)}, u32[]{:S(2)}, u32[]{:S(2)}) %collective-permute-start.13) | collective-permute-done | bytes 147488 | tf_op jit(solution)/shard_map/ppermute | solution.py:541
  96.2 1.1 shard_map.80
  97.3 0.7 collective-permute-start.16
  98.0 0.8 collective-permute-done.16
  98.9 0.4 collective-permute-start.19
  99.3 0.6 collective-permute-start.18
  99.9 0.5 collective-permute-start.17
  100.4 1.2 collective-permute-done.19
  101.6 1.9 %collective-permute-done.18 = f32[48,128]{1,0:T(8,128)S(1)} collective-permute-done((f32[48,128]{1,0:T(8,128)S(1)}, f32[48,128]{1,0:T(8,128)S(1)}, u32[]{:S(2)}, u32[]{:S(2)}) %collective-permute-start.18) | collective-permute-done | bytes 24608 | tf_op jit(solution)/shard_map/ppermute | solution.py:541
  103.5 0.5 collective-permute-done.17
  104.0 11.1 %all_to_all.11 = f32[8,48,128]{2,1,0:T(8,128)S(1)} all-to-all(f32[8,48,128]{2,1,0:T(8,128)S(1)} %broadcast_in_dim.5), channel_id=1, replica_groups=mesh['x'=4,'y'=4,'z'=8,'core'=2] {'z'}, dimensions={0} | all-to-all | bytes 393216 | tf_op jit(solution)/shard_map/all_to_all | solution.py:555
  115.2 3.0 %collective-permute-start.20 = (f32[48,128]{1,0:T(8,128)S(1)}, f32[48,128]{1,0:T(8,128)S(1)}, u32[]{:S(2)}, u32[]{:S(2)}) collective-permute-start(f32[48,128]{1,0:T(8,128)S(1)} %reduce_sum.19.own_ref), channel_id=1, source_target_pairs={{0,1},{1,0},{2,3},{3,2},{4,5},{5,4},{6,7},{7,6},{8,9},{9,8},{10,11... | collective-permute-start | bytes 73736 | tf_op jit(solution)/shard_map/ppermute | solution.py:541
  118.2 0.8 collective-permute-done.20.other_ref
  119.0 9.3 %shard_map.81 = f32[64,128]{1,0:T(8,128)S(1)} custom-call(f32[48,128]{1,0:T(8,128)S(1)} %reduce_sum.19.own_ref, f32[48,128]{1,0:T(8,128)S(1)} %collective-permute-done.20.other_ref, f32[288,128]{1,0:T(8,128)S(1)} %shard_map.79.r0, f32[288,128]{1,0:T(8,128)S(1)} %collective-permute-done.13.r1, f32[288,128]{1,0:T(8,128)S(1)} %collective-permute-done.14.r2, ...), custom_call_target="tpu_custom_call" | custom-call | tf_op jit(solution)/shard_map/pallas_call | solution.py:520
  128.3 0.7 copy.10
  (11 shorter events, 0.1 us)
Async XLA Ops:
  0.0 7.2 %copy-start = (s32[5,128,64]{1,2,0:T(8,128)S(1)}, s32[5,128,64]{1,2,0:T(8,128)}, u32[]{:S(2)}) copy-start(s32[5,128,64]{1,2,0:T(8,128)} %param.13) | copy-start | bytes 491524
  1.5 11.9 %collective-permute-start = (f32[1040,128]{1,0:T(8,128)S(1)}, f32[1040,128]{1,0:T(8,128)S(1)}, u32[]{:S(2)}, u32[]{:S(2)}) collective-permute-start(f32[1040,128]{1,0:T(8,128)S(1)} %get-tuple-element.31), channel_id=1, source_target_pairs={{1,2},{3,4},{5,6},{7,8},{9,10},{11,12},{13,14},{2,1},{4,3},{6,5},{... | collective-permute-start | bytes 1597448 | tf_op jit(solution)/shard_map/ppermute | solution.py:583
  6.4 6.9 %collective-permute-start.1 = (f32[1040,128]{1,0:T(8,128)S(1)}, f32[1040,128]{1,0:T(8,128)S(1)}, u32[]{:S(2)}, u32[]{:S(2)}) collective-permute-start(f32[1040,128]{1,0:T(8,128)S(1)} %get-tuple-element.32), channel_id=1, source_target_pairs={{0,1},{1,0},{2,3},{3,2},{4,5},{5,4},{6,7},{7,6},{8,9},{9,8},{10,11... | collective-permute-start | bytes 1597448 | tf_op jit(solution)/shard_map/ppermute | solution.py:541
  20.0 7.2 %collective-permute-start.2 = (f32[4,64,128]{2,1,0:T(8,128)S(1)}, f32[4,64,128]{2,1,0:T(8,128)S(1)}, u32[]{:S(2)}, u32[]{:S(2)}) collective-permute-start(f32[4,64,128]{2,1,0:T(8,128)S(1)} %get-tuple-element.38), channel_id=1, source_target_pairs={{0,16},{16,32},{32,48},{48,0},{1,17},{17,33},{33,49},{49,1},{2,18}... | collective-permute-start | bytes 393224 | tf_op jit(solution)/shard_map/ppermute | solution.py:541
  21.4 8.4 %collective-permute-start.3 = (f32[4,64,128]{2,1,0:T(8,128)S(1)}, f32[4,64,128]{2,1,0:T(8,128)S(1)}, u32[]{:S(2)}, u32[]{:S(2)}) collective-permute-start(f32[4,64,128]{2,1,0:T(8,128)S(1)} %get-tuple-element.39), channel_id=1, source_target_pairs={{0,32},{16,48},{32,0},{48,16},{1,33},{17,49},{33,1},{49,17},{2,34}... | collective-permute-start | bytes 393224 | tf_op jit(solution)/shard_map/ppermute | solution.py:541
  24.0 5.8 %collective-permute-start.4 = (f32[4,64,128]{2,1,0:T(8,128)S(1)}, f32[4,64,128]{2,1,0:T(8,128)S(1)}, u32[]{:S(2)}, u32[]{:S(2)}) collective-permute-start(f32[4,64,128]{2,1,0:T(8,128)S(1)} %get-tuple-element.40), channel_id=1, source_target_pairs={{0,48},{16,0},{32,16},{48,32},{1,49},{17,1},{33,17},{49,33},{2,50}... | collective-permute-start | bytes 393224 | tf_op jit(solution)/shard_map/ppermute | solution.py:541
  31.7 1.3 %collective-permute-start.5 = (f32[128,128]{1,0:T(8,128)S(1)}, f32[128,128]{1,0:T(8,128)S(1)}, u32[]{:S(2)}, u32[]{:S(2)}) collective-permute-start(f32[128,128]{1,0:T(8,128)S(1)} %get-tuple-element.42), channel_id=1, source_target_pairs={{0,1},{1,0},{2,3},{3,2},{4,5},{5,4},{6,7},{7,6},{8,9},{9,8},{10,11... | collective-permute-start | bytes 196616 | tf_op jit(solution)/shard_map/ppermute | solution.py:541
  33.1 3.5 %collective-permute-start.8 = (f32[24,128]{1,0:T(8,128)S(1)}, f32[24,128]{1,0:T(8,128)S(1)}, u32[]{:S(2)}, u32[]{:S(2)}) collective-permute-start(f32[24,128]{1,0:T(8,128)S(1)} %get-tuple-element.49), channel_id=1, source_target_pairs={{0,48},{16,0},{32,16},{48,32},{1,49},{17,1},{33,17},{49,33},{2,50}... | collective-permute-start | bytes 36872 | tf_op jit(solution)/shard_map/ppermute | solution.py:541
  35.4 4.0 %collective-permute-start.7 = (f32[24,128]{1,0:T(8,128)S(1)}, f32[24,128]{1,0:T(8,128)S(1)}, u32[]{:S(2)}, u32[]{:S(2)}) collective-permute-start(f32[24,128]{1,0:T(8,128)S(1)} %get-tuple-element.50), channel_id=1, source_target_pairs={{0,32},{16,48},{32,0},{48,16},{1,33},{17,49},{33,1},{49,17},{2,34}... | collective-permute-start | bytes 36872 | tf_op jit(solution)/shard_map/ppermute | solution.py:541
  36.3 3.8 %collective-permute-start.6 = (f32[24,128]{1,0:T(8,128)S(1)}, f32[24,128]{1,0:T(8,128)S(1)}, u32[]{:S(2)}, u32[]{:S(2)}) collective-permute-start(f32[24,128]{1,0:T(8,128)S(1)} %get-tuple-element.51), channel_id=1, source_target_pairs={{0,16},{16,32},{32,48},{48,0},{1,17},{17,33},{33,49},{49,1},{2,18}... | collective-permute-start | bytes 36872 | tf_op jit(solution)/shard_map/ppermute | solution.py:541
  57.8 4.4 %collective-permute-start.9 = (f32[56,128]{1,0:T(8,128)S(1)}, f32[56,128]{1,0:T(8,128)S(1)}, u32[]{:S(2)}, u32[]{:S(2)}) collective-permute-start(f32[56,128]{1,0:T(8,128)S(1)} %reduce_sum.18.own_ref), channel_id=1, source_target_pairs={{0,1},{1,0},{2,3},{3,2},{4,5},{5,4},{6,7},{7,6},{8,9},{9,8},{10,11... | collective-permute-start | bytes 86024 | tf_op jit(solution)/shard_map/ppermute | solution.py:541
  66.1 3.1 %collective-permute-start.12 = (f32[112,128]{1,0:T(8,128)S(1)}, f32[112,128]{1,0:T(8,128)S(1)}, u32[]{:S(2)}, u32[]{:S(2)}) collective-permute-start(f32[112,128]{1,0:T(8,128)S(1)} %shard_map.78.p0), channel_id=1, source_target_pairs={{0,48},{16,0},{32,16},{48,32},{1,49},{17,1},{33,17},{49,33},{2,50}... | collective-permute-start | bytes 172040 | tf_op jit(solution)/shard_map/ppermute | solution.py:541
  66.5 4.5 %collective-permute-start.11 = (f32[112,128]{1,0:T(8,128)S(1)}, f32[112,128]{1,0:T(8,128)S(1)}, u32[]{:S(2)}, u32[]{:S(2)}) collective-permute-start(f32[112,128]{1,0:T(8,128)S(1)} %shard_map.78.p0), channel_id=1, source_target_pairs={{0,32},{16,48},{32,0},{48,16},{1,33},{17,49},{33,1},{49,17},{2,34}... | collective-permute-start | bytes 172040 | tf_op jit(solution)/shard_map/ppermute | solution.py:541
  67.7 5.3 %collective-permute-start.10 = (f32[112,128]{1,0:T(8,128)S(1)}, f32[112,128]{1,0:T(8,128)S(1)}, u32[]{:S(2)}, u32[]{:S(2)}) collective-permute-start(f32[112,128]{1,0:T(8,128)S(1)} %shard_map.78.p0), channel_id=1, source_target_pairs={{0,16},{16,32},{32,48},{48,0},{1,17},{17,33},{33,49},{49,1},{2,18}... | collective-permute-start | bytes 172040 | tf_op jit(solution)/shard_map/ppermute | solution.py:541
  83.2 6.1 %collective-permute-start.15 = (f32[288,128]{1,0:T(8,128)S(1)}, f32[288,128]{1,0:T(8,128)S(1)}, u32[]{:S(2)}, u32[]{:S(2)}) collective-permute-start(f32[288,128]{1,0:T(8,128)S(1)} %shard_map.79.r0), channel_id=1, source_target_pairs={{0,192},{64,0},{128,64},{192,128},{1,193},{65,1},{129,65},{193,129... | collective-permute-start | bytes 442376 | tf_op jit(solution)/shard_map/ppermute | solution.py:541
  85.9 5.6 %collective-permute-start.14 = (f32[288,128]{1,0:T(8,128)S(1)}, f32[288,128]{1,0:T(8,128)S(1)}, u32[]{:S(2)}, u32[]{:S(2)}) collective-permute-start(f32[288,128]{1,0:T(8,128)S(1)} %shard_map.79.r0), channel_id=1, source_target_pairs={{0,128},{64,192},{128,0},{192,64},{1,129},{65,193},{129,1},{193,65... | collective-permute-start | bytes 442376 | tf_op jit(solution)/shard_map/ppermute | solution.py:541
  86.5 9.7 %collective-permute-start.13 = (f32[288,128]{1,0:T(8,128)S(1)}, f32[288,128]{1,0:T(8,128)S(1)}, u32[]{:S(2)}, u32[]{:S(2)}) collective-permute-start(f32[288,128]{1,0:T(8,128)S(1)} %shard_map.79.r0), channel_id=1, source_target_pairs={{0,64},{64,128},{128,192},{192,0},{1,65},{65,129},{129,193},{193,1... | collective-permute-start | bytes 442376 | tf_op jit(solution)/shard_map/ppermute | solution.py:541
  97.3 1.6 %collective-permute-start.16 = (f32[48,128]{1,0:T(8,128)S(1)}, f32[48,128]{1,0:T(8,128)S(1)}, u32[]{:S(2)}, u32[]{:S(2)}) collective-permute-start(f32[48,128]{1,0:T(8,128)S(1)} %get-tuple-element.47), channel_id=1, source_target_pairs={{0,1},{1,0},{2,3},{3,2},{4,5},{5,4},{6,7},{7,6},{8,9},{9,8},{10,11... | collective-permute-start | bytes 73736 | tf_op jit(solution)/shard_map/ppermute | solution.py:541
  98.9 2.7 %collective-permute-start.19 = (f32[48,128]{1,0:T(8,128)S(1)}, f32[48,128]{1,0:T(8,128)S(1)}, u32[]{:S(2)}, u32[]{:S(2)}) collective-permute-start(f32[48,128]{1,0:T(8,128)S(1)} %add.28), channel_id=1, source_target_pairs={{0,48},{16,0},{32,16},{48,32},{1,49},{17,1},{33,17},{49,33},{2,50}... | collective-permute-start | bytes 73736 | tf_op jit(solution)/shard_map/ppermute | solution.py:541
  99.3 4.2 %collective-permute-start.18 = (f32[48,128]{1,0:T(8,128)S(1)}, f32[48,128]{1,0:T(8,128)S(1)}, u32[]{:S(2)}, u32[]{:S(2)}) collective-permute-start(f32[48,128]{1,0:T(8,128)S(1)} %add.28), channel_id=1, source_target_pairs={{0,32},{16,48},{32,0},{48,16},{1,33},{17,49},{33,1},{49,17},{2,34}... | collective-permute-start | bytes 73736 | tf_op jit(solution)/shard_map/ppermute | solution.py:541
  99.9 4.1 %collective-permute-start.17 = (f32[48,128]{1,0:T(8,128)S(1)}, f32[48,128]{1,0:T(8,128)S(1)}, u32[]{:S(2)}, u32[]{:S(2)}) collective-permute-start(f32[48,128]{1,0:T(8,128)S(1)} %add.28), channel_id=1, source_target_pairs={{0,16},{16,32},{32,48},{48,0},{1,17},{17,33},{33,49},{49,1},{2,18}... | collective-permute-start | bytes 73736 | tf_op jit(solution)/shard_map/ppermute | solution.py:541
  115.2 3.8 %collective-permute-start.20 = (f32[48,128]{1,0:T(8,128)S(1)}, f32[48,128]{1,0:T(8,128)S(1)}, u32[]{:S(2)}, u32[]{:S(2)}) collective-permute-start(f32[48,128]{1,0:T(8,128)S(1)} %reduce_sum.19.own_ref), channel_id=1, source_target_pairs={{0,1},{1,0},{2,3},{3,2},{4,5},{5,4},{6,7},{7,6},{8,9},{9,8},{10,11... | collective-permute-start | bytes 73736 | tf_op jit(solution)/shard_map/ppermute | solution.py:541

commit v5 on v4

--- a/solution.py
+++ b/solution.py
@@ -44,6 +44,31 @@
 def mm_signs(x, signs):
     hi, mid, lo = (jnp.dot(t, signs, preferred_element_type=F32) for t in thirds(x))
     return (hi + (mid + lo)) * SCALE
+
+
+def product(a, b):
+    (ah, am, _), (bh, bm, _) = thirds(a), thirds(b)
+    left = jnp.concatenate([ah, am], axis=0)
+    high = jnp.dot(left, bh, preferred_element_type=F32)
+    low = jnp.dot(left, bm, preferred_element_type=F32)
+    rows = a.shape[0]
+    return high[:rows] + (high[rows:] + low[:rows]) + low[rows:]
+
+
+def halves(x):
+    hi = x.astype(jnp.bfloat16)
+    mid = (x - hi.astype(F32)).astype(jnp.bfloat16)
+    return jnp.concatenate([hi, mid], axis=1), jnp.concatenate([mid, hi], axis=1)
+
+
+def inner_products(left, right):
+    dims = (((1,), (1,)), ((), ()))
+    same = lax.dot_general(left[0], right[0], dims, preferred_element_type=F32)
+    return same + lax.dot_general(left[0], right[1], dims, preferred_element_type=F32)
+
+
+def stacked(first, second):
+    return tuple(jnp.concatenate([a, b], axis=0) for a, b in zip(first, second))
 
 
 def rows_of(v, i):
@@ -389,12 +414,12 @@
         all_s[rest_of(place, -d)] = ref[...]
     slabs = [jnp.zeros((64, 128), F32)] * 3
     for q in range(4):
-        s0, s1, s2, s3 = (all_s[g, q] for g in range(4))
-        upper = jnp.concatenate([s2, s3], axis=0)
-        first = mm_nt(s0, jnp.concatenate([s1, s3], axis=0))
-        slabs[1] = slabs[1] + mm_nt(s0, upper)
-        slabs[2] = slabs[2] + mm_nt(s1, upper)
-        slabs[0] = slabs[0] + jnp.concatenate([first[:, :64], mm_nt(s2, s3)], axis=1)
+        s0, s1, s2, s3 = (halves(all_s[g, q]) for g in range(4))
+        upper = stacked(s2, s3)
+        slabs[1] = slabs[1] + inner_products(s0, upper)
+        slabs[2] = slabs[2] + inner_products(s1, upper)
+        first, second = inner_products(s0, s1), inner_products(s2, s3)
+        slabs[0] = slabs[0] + jnp.concatenate([first, second], axis=1)
     for n in range(3):
         z_s[64 * n : 64 * n + 64] = slabs[n]
     for c in range(2):
@@ -445,9 +470,8 @@
     high = signs_mm(signs_t[:, 64:], ws[1])
     w = mm(b, jnp.concatenate([low, high], axis=1)) * half
     for q in range(4):
-        out_ref[64 * q : 64 * q + 64] = mm(
-            w, jnp.concatenate([all_ref[g, q] for g in range(4)], axis=0)
-        )
+        own = jnp.concatenate([all_ref[g, q] for g in range(4)], axis=0)
+        out_ref[64 * q : 64 * q + 64] = product(w, own)
     gram = gram_of(b, moment)
     out_ref[256:288] = jnp.concatenate([gram[:32], gram[32:]], axis=1)
 
@@ -466,8 +490,8 @@
             sk = signs_mm(signs_t, jnp.concatenate([low, high], axis=0)) * (0.5**0.5)
             s_ref[n, q] = sk
             sks.append(sk)
-            slabs[n] = slabs[n] + mm_nt(low, high)
-        slabs[2] = slabs[2] + mm_nt(*sks)
+            slabs[n] = slabs[n] + inner_products(halves(low), halves(high))
+        slabs[2] = slabs[2] + inner_products(halves(sks[0]), halves(sks[1]))
     for c in range(2):
         at = slice(32 * c, 32 * c + 32)
         pay_s[c, 0:32] = jnp.concatenate([slabs[0][at], slabs[1][at]], axis=1)
@@ -512,7 +536,7 @@
         own = jnp.concatenate([s_ref[0, q], s_ref[1, q]], axis=0)
         turned = pltpu.roll(own, lax.rem(32 * q - 32 * place + 128, 128), 1)
         mine = jnp.where(block == q, turned, mine)
-    out_ref[...] = mm(w, mine)
+    out_ref[...] = product(w, mine)
 
 
 def call(kernel, out_shapes, smem, *args, scratch=(), limit=16, cost=None):

time: 129 us -> 128 us (level)
  no operation moved by 1% of the time
where the time goes in v5:
time: 128 us
  Pallas kernels  39.8 us (31%)
  waiting for transfers between devices  28.9 us (23%)
  blocking collectives  28.8 us (22%)
  starting transfers between devices  28.7 us (22%)
    pallas_call x8, Pallas kernels, call(): pl.pallas_call(kernel, out_shape=out_shapes, in_specs=specs, out_specs=ja...  38.3 us
    all_to_all x2, blocking collectives, sum_over(): return lax.all_to_all(sent, axis, 0, 0, tiled=True).sum(axis=0)  28.8 us
    ppermute x20, waiting for transfers between devices, shift(): return lax.ppermute(value, axis, [(i, (i + by) % n) for i in range(n)])  27.2 us
    ppermute x20, starting transfers between devices, shift(): return lax.ppermute(value, axis, [(i, (i + by) % n) for i in range(n)])  23.8 us
    ppermute x1, starting transfers between devices, per_device(): cross = lax.ppermute(cross, slabs, between)  4.92 us
  transfers between devices with their start and end apart: 21, of which 17 were waited for; matrix products, arithmetic and copies ran while one was open for 0% of the time, Pallas kernels for 5%

profile of v5, /device:TPU:1, one launch (start us, length us, event | category | flops | bytes accessed | tf_op | source)
XLA Modules:
  0.0 127.8 jit_solution(7227667334161761309)
XLA Ops:
  0.0 0.0 copy-start
  0.0 1.5 %shard_map.73 = (f32[2,1040,128]{2,1,0:T(8,128)S(1)}, f32[1040,128]{1,0:T(8,128)S(1)}, f32[1040,128]{1,0:T(8,128)S(1)}, f32[128,128]{1,0:T(8,128)S(1)}) custom-call(f32[2048,128]{1,0:T(8,128)} %bitcast.6, f32[16,128]{1,0:T(8,128)} %bitcast.7, f32[16,128]{1,0:T(8,128)} %src_ref.1, s32[1,128]{1,0:T(1,128)} %pick_ref.1, f32[64]{0:T(128)} %table_ref.1), custom_call_target="tpu_custom_call" | custom-call | tf_op jit(solution)/shard_map/pallas_call | solution.py:588
  1.5 4.9 %collective-permute-start = (f32[1040,128]{1,0:T(8,128)S(1)}, f32[1040,128]{1,0:T(8,128)S(1)}, u32[]{:S(2)}, u32[]{:S(2)}) collective-permute-start(f32[1040,128]{1,0:T(8,128)S(1)} %get-tuple-element.31), channel_id=1, source_target_pairs={{1,2},{3,4},{5,6},{7,8},{9,10},{11,12},{13,14},{2,1},{4,3},{6,5},{... | collective-permute-start | bytes 1597448 | tf_op jit(solution)/shard_map/ppermute | solution.py:607
  6.4 0.1 collective-permute-start.1
  7.2 0.0 copy-done
  7.2 4.4 %shard_map.74 = (f32[16,128,128]{2,1,0:T(8,128)S(1)}, f32[16,128,128]{2,1,0:T(8,128)S(1)}, bf16[64,128]{1,0:T(8,128)(2,1)S(1)}) custom-call(s32[1]{0:T(128)S(6)} %copy.11.count_ref, f32[2,1040,128]{2,1,0:T(8,128)S(1)} %get-tuple-element.27.ends_ref, f32[128,128]{1,0:T(8,128)S(1)} %get-tuple-element.28.amp_ref, s32[5,64,128]{2,1,0:T(8,128)S(1)} %bitcast.4), custom_call_target="tpu_custom_call" | custom-call | flops 4000000000 | bytes 4000000 | tf_op jit(solution)/shard_map/pallas_call | solution.py:544
  11.6 1.8 %collective-permute-done.cross_ref = f32[1040,128]{1,0:T(8,128)S(1)} collective-permute-done((f32[1040,128]{1,0:T(8,128)S(1)}, f32[1040,128]{1,0:T(8,128)S(1)}, u32[]{:S(2)}, u32[]{:S(2)}) %collective-permute-start) | collective-permute-done | bytes 532512 | tf_op jit(solution)/shard_map/ppermute | solution.py:607
  13.4 0.0 collective-permute-done.1.chip_ref
  13.4 6.7 %shard_map.75 = (f32[16,128,128]{2,1,0:T(8,128)S(1)}, f32[16,64,128]{2,1,0:T(8,128)S(1)}, f32[4,64,128]{2,1,0:T(8,128)S(1)}, f32[4,64,128]{2,1,0:T(8,128)S(1)}, ...) custom-call(s32[1]{0:T(128)S(6)} %copy.11.count_ref, f32[16,128,128]{2,1,0:T(8,128)S(1)} %get-tuple-element.29.last_ref, ...), custom_call_target="tpu_custom_call" | custom-call | tf_op jit(solution)/shard_map/pallas_call | solution.py:544
  20.0 1.4 %collective-permute-start.2 = (f32[4,64,128]{2,1,0:T(8,128)S(1)}, f32[4,64,128]{2,1,0:T(8,128)S(1)}, u32[]{:S(2)}, u32[]{:S(2)}) collective-permute-start(f32[4,64,128]{2,1,0:T(8,128)S(1)} %get-tuple-element.38), channel_id=1, source_target_pairs={{0,16},{16,32},{32,48},{48,0},{1,17},{17,33},{33,49},{49,1},{2,18}... | collective-permute-start | bytes 393224 | tf_op jit(solution)/shard_map/ppermute | solution.py:565
  21.4 2.6 %collective-permute-start.3 = (f32[4,64,128]{2,1,0:T(8,128)S(1)}, f32[4,64,128]{2,1,0:T(8,128)S(1)}, u32[]{:S(2)}, u32[]{:S(2)}) collective-permute-start(f32[4,64,128]{2,1,0:T(8,128)S(1)} %get-tuple-element.39), channel_id=1, source_target_pairs={{0,32},{16,48},{32,0},{48,16},{1,33},{17,49},{33,1},{49,17},{2,34}... | collective-permute-start | bytes 393224 | tf_op jit(solution)/shard_map/ppermute | solution.py:565
  24.0 1.1 collective-permute-start.4
  25.1 2.1 %shard_map.76 = (f32[64,128]{1,0:T(8,128)S(1)}, bf16[5,128,64]{2,1,0:T(8,128)(2,1)S(1)}, bf16[5,64,128]{2,1,0:T(8,128)(2,1)S(1)}) custom-call(f32[16,128,128]{2,1,0:T(8,128)S(1)} %get-tuple-element.34.field_ref, f32[16,64,128]{2,1,0:T(8,128)S(1)} %get-tuple-element.35.sk_ref, s32[5,64,128]{2,1,0:T(8,128)S(1)} %bitcast.5), custom_call_target="tpu_custom_call" | custom-call | flops 2000000000 | bytes 2000000 | tf_op jit(solution)/shard_map/pallas_call | solution.py:544
  27.2 0.0 collective-permute-done.2.r1
  27.2 2.6 %collective-permute-done.3.r2 = f32[4,64,128]{2,1,0:T(8,128)S(1)} collective-permute-done((f32[4,64,128]{2,1,0:T(8,128)S(1)}, f32[4,64,128]{2,1,0:T(8,128)S(1)}, u32[]{:S(2)}, u32[]{:S(2)}) %collective-permute-start.3) | collective-permute-done | bytes 131104 | tf_op jit(solution)/shard_map/ppermute | solution.py:565
  29.8 0.0 collective-permute-done.4.r3
  29.8 0.8 shard_map.77
  30.6 0.1 collective-permute-start.5
  30.7 1.2 collective-permute-done.5
  31.9 2.4 %collective-permute-start.8 = (f32[24,128]{1,0:T(8,128)S(1)}, f32[24,128]{1,0:T(8,128)S(1)}, u32[]{:S(2)}, u32[]{:S(2)}) collective-permute-start(f32[24,128]{1,0:T(8,128)S(1)} %get-tuple-element.49), channel_id=1, source_target_pairs={{0,48},{16,0},{32,16},{48,32},{1,49},{17,1},{33,17},{49,33},{2,50}... | collective-permute-start | bytes 36872 | tf_op jit(solution)/shard_map/ppermute | solution.py:565
  34.3 0.9 collective-permute-start.7
  35.2 0.3 collective-permute-start.6
  35.4 0.0 collective-permute-done.8
  35.5 2.9 %collective-permute-done.7 = f32[24,128]{1,0:T(8,128)S(1)} collective-permute-done((f32[24,128]{1,0:T(8,128)S(1)}, f32[24,128]{1,0:T(8,128)S(1)}, u32[]{:S(2)}, u32[]{:S(2)}) %collective-permute-start.7) | collective-permute-done | bytes 12320 | tf_op jit(solution)/shard_map/ppermute | solution.py:565
  38.4 0.6 collective-permute-done.6
  39.0 17.7 %all_to_all.10 = f32[8,56,128]{2,1,0:T(8,128)S(1)} all-to-all(f32[8,56,128]{2,1,0:T(8,128)S(1)} %broadcast_in_dim.4), channel_id=1, replica_groups=mesh['x'=4,'y'=4,'z'=8,'core'=2] {'z'}, dimensions={0} | all-to-all | bytes 458752 | tf_op jit(solution)/shard_map/all_to_all | solution.py:579
  56.7 3.6 %collective-permute-start.9 = (f32[56,128]{1,0:T(8,128)S(1)}, f32[56,128]{1,0:T(8,128)S(1)}, u32[]{:S(2)}, u32[]{:S(2)}) collective-permute-start(f32[56,128]{1,0:T(8,128)S(1)} %reduce_sum.18.own_ref), channel_id=1, source_target_pairs={{0,1},{1,0},{2,3},{3,2},{4,5},{5,4},{6,7},{7,6},{8,9},{9,8},{10,11... | collective-permute-start | bytes 86024 | tf_op jit(solution)/shard_map/ppermute | solution.py:565
  60.2 0.9 collective-permute-done.9.other_ref
  61.1 3.9 %shard_map.78.p0 = f32[112,128]{1,0:T(8,128)S(1)} custom-call(f32[56,128]{1,0:T(8,128)S(1)} %reduce_sum.18.own_ref, f32[56,128]{1,0:T(8,128)S(1)} %collective-permute-done.9.other_ref, bf16[5,128,64]{2,1,0:T(8,128)(2,1)S(1)} %get-tuple-element.43.sg_ref, bf16[5,64,128]{2,1,0:T(8,128)(2,1)S(1)} %get-tuple-element.44.sgt_ref), custom_call_target="tpu_custom_call" | custom-call | tf_op jit(solution)/shard_map/pallas_call | solution.py:544
  65.0 0.4 collective-permute-start.12
  65.4 1.2 collective-permute-start.11
  66.6 0.8 collective-permute-start.10
  67.3 0.8 collective-permute-done.12.p3
  68.1 1.8 %collective-permute-done.11.p2 = f32[112,128]{1,0:T(8,128)S(1)} collective-permute-done((f32[112,128]{1,0:T(8,128)S(1)}, f32[112,128]{1,0:T(8,128)S(1)}, u32[]{:S(2)}, u32[]{:S(2)}) %collective-permute-start.11) | collective-permute-done | bytes 57376 | tf_op jit(solution)/shard_map/ppermute | solution.py:565
  69.9 1.9 %collective-permute-done.10.p1 = f32[112,128]{1,0:T(8,128)S(1)} collective-permute-done((f32[112,128]{1,0:T(8,128)S(1)}, f32[112,128]{1,0:T(8,128)S(1)}, u32[]{:S(2)}, u32[]{:S(2)}) %collective-permute-start.10) | collective-permute-done | bytes 57376 | tf_op jit(solution)/shard_map/ppermute | solution.py:565
  71.8 10.2 %shard_map.79.r0 = f32[288,128]{1,0:T(8,128)S(1)} custom-call(f32[112,128]{1,0:T(8,128)S(1)} %shard_map.78.p0, f32[112,128]{1,0:T(8,128)S(1)} %collective-permute-done.10.p1, f32[112,128]{1,0:T(8,128)S(1)} %collective-permute-done.11.p2, f32[112,128]{1,0:T(8,128)S(1)} %collective-permute-done.12.p3, f32[4,4,64,128]{3,2,1,0:T(8,128)S(1)} %get-tuple-element.45.all_ref, ...), custom_call_target="tpu_custom_call" | custom-call | tf_op jit(solution)/shard_map/pallas_call | solution.py:544
  82.0 2.8 %collective-permute-start.15 = (f32[288,128]{1,0:T(8,128)S(1)}, f32[288,128]{1,0:T(8,128)S(1)}, u32[]{:S(2)}, u32[]{:S(2)}) collective-permute-start(f32[288,128]{1,0:T(8,128)S(1)} %shard_map.79.r0), channel_id=1, source_target_pairs={{0,192},{64,0},{128,64},{192,128},{1,193},{65,1},{129,65},{193,129... | collective-permute-start | bytes 442376 | tf_op jit(solution)/shard_map/ppermute | solution.py:565
  84.8 0.5 collective-permute-start.14
  85.3 0.6 collective-permute-start.13
  85.9 2.2 %collective-permute-done.15.r3 = f32[288,128]{1,0:T(8,128)S(1)} collective-permute-done((f32[288,128]{1,0:T(8,128)S(1)}, f32[288,128]{1,0:T(8,128)S(1)}, u32[]{:S(2)}, u32[]{:S(2)}) %collective-permute-start.15) | collective-permute-done | bytes 147488 | tf_op jit(solution)/shard_map/ppermute | solution.py:565
  88.1 2.3 %collective-permute-done.14.r2 = f32[288,128]{1,0:T(8,128)S(1)} collective-permute-done((f32[288,128]{1,0:T(8,128)S(1)}, f32[288,128]{1,0:T(8,128)S(1)}, u32[]{:S(2)}, u32[]{:S(2)}) %collective-permute-start.14) | collective-permute-done | bytes 147488 | tf_op jit(solution)/shard_map/ppermute | solution.py:565
  90.4 4.7 %collective-permute-done.13.r1 = f32[288,128]{1,0:T(8,128)S(1)} collective-permute-done((f32[288,128]{1,0:T(8,128)S(1)}, f32[288,128]{1,0:T(8,128)S(1)}, u32[]{:S(2)}, u32[]{:S(2)}) %collective-permute-start.13) | collective-permute-done | bytes 147488 | tf_op jit(solution)/shard_map/ppermute | solution.py:565
  95.1 1.0 shard_map.80
  96.1 0.8 collective-permute-start.16
  96.8 0.8 collective-permute-done.16
  97.7 0.4 collective-permute-start.19
  98.1 0.6 collective-permute-start.18
  98.7 0.5 collective-permute-start.17
  99.1 1.2 collective-permute-done.19
  100.4 1.9 %collective-permute-done.18 = f32[48,128]{1,0:T(8,128)S(1)} collective-permute-done((f32[48,128]{1,0:T(8,128)S(1)}, f32[48,128]{1,0:T(8,128)S(1)}, u32[]{:S(2)}, u32[]{:S(2)}) %collective-permute-start.18) | collective-permute-done | bytes 24608 | tf_op jit(solution)/shard_map/ppermute | solution.py:565
  102.3 0.5 collective-permute-done.17
  102.8 11.1 %all_to_all.11 = f32[8,48,128]{2,1,0:T(8,128)S(1)} all-to-all(f32[8,48,128]{2,1,0:T(8,128)S(1)} %broadcast_in_dim.5), channel_id=1, replica_groups=mesh['x'=4,'y'=4,'z'=8,'core'=2] {'z'}, dimensions={0} | all-to-all | bytes 393216 | tf_op jit(solution)/shard_map/all_to_all | solution.py:579
  113.9 3.0 %collective-permute-start.20 = (f32[48,128]{1,0:T(8,128)S(1)}, f32[48,128]{1,0:T(8,128)S(1)}, u32[]{:S(2)}, u32[]{:S(2)}) collective-permute-start(f32[48,128]{1,0:T(8,128)S(1)} %reduce_sum.19.own_ref), channel_id=1, source_target_pairs={{0,1},{1,0},{2,3},{3,2},{4,5},{5,4},{6,7},{7,6},{8,9},{9,8},{10,11... | collective-permute-start | bytes 73736 | tf_op jit(solution)/shard_map/ppermute | solution.py:565
  116.9 0.8 collective-permute-done.20.other_ref
  117.8 9.3 %shard_map.81 = f32[64,128]{1,0:T(8,128)S(1)} custom-call(f32[48,128]{1,0:T(8,128)S(1)} %reduce_sum.19.own_ref, f32[48,128]{1,0:T(8,128)S(1)} %collective-permute-done.20.other_ref, f32[288,128]{1,0:T(8,128)S(1)} %shard_map.79.r0, f32[288,128]{1,0:T(8,128)S(1)} %collective-permute-done.13.r1, f32[288,128]{1,0:T(8,128)S(1)} %collective-permute-done.14.r2, ...), custom_call_target="tpu_custom_call" | custom-call | tf_op jit(solution)/shard_map/pallas_call | solution.py:544
  127.1 0.8 copy.10
  (11 shorter events, 0.1 us)
Async XLA Ops:
  0.0 7.2 %copy-start = (s32[5,128,64]{1,2,0:T(8,128)S(1)}, s32[5,128,64]{1,2,0:T(8,128)}, u32[]{:S(2)}) copy-start(s32[5,128,64]{1,2,0:T(8,128)} %param.13) | copy-start | bytes 491524
  1.5 11.9 %collective-permute-start = (f32[1040,128]{1,0:T(8,128)S(1)}, f32[1040,128]{1,0:T(8,128)S(1)}, u32[]{:S(2)}, u32[]{:S(2)}) collective-permute-start(f32[1040,128]{1,0:T(8,128)S(1)} %get-tuple-element.31), channel_id=1, source_target_pairs={{1,2},{3,4},{5,6},{7,8},{9,10},{11,12},{13,14},{2,1},{4,3},{6,5},{... | collective-permute-start | bytes 1597448 | tf_op jit(solution)/shard_map/ppermute | solution.py:607
  6.4 6.9 %collective-permute-start.1 = (f32[1040,128]{1,0:T(8,128)S(1)}, f32[1040,128]{1,0:T(8,128)S(1)}, u32[]{:S(2)}, u32[]{:S(2)}) collective-permute-start(f32[1040,128]{1,0:T(8,128)S(1)} %get-tuple-element.32), channel_id=1, source_target_pairs={{0,1},{1,0},{2,3},{3,2},{4,5},{5,4},{6,7},{7,6},{8,9},{9,8},{10,11... | collective-permute-start | bytes 1597448 | tf_op jit(solution)/shard_map/ppermute | solution.py:565
  20.0 7.2 %collective-permute-start.2 = (f32[4,64,128]{2,1,0:T(8,128)S(1)}, f32[4,64,128]{2,1,0:T(8,128)S(1)}, u32[]{:S(2)}, u32[]{:S(2)}) collective-permute-start(f32[4,64,128]{2,1,0:T(8,128)S(1)} %get-tuple-element.38), channel_id=1, source_target_pairs={{0,16},{16,32},{32,48},{48,0},{1,17},{17,33},{33,49},{49,1},{2,18}... | collective-permute-start | bytes 393224 | tf_op jit(solution)/shard_map/ppermute | solution.py:565
  21.4 8.4 %collective-permute-start.3 = (f32[4,64,128]{2,1,0:T(8,128)S(1)}, f32[4,64,128]{2,1,0:T(8,128)S(1)}, u32[]{:S(2)}, u32[]{:S(2)}) collective-permute-start(f32[4,64,128]{2,1,0:T(8,128)S(1)} %get-tuple-element.39), channel_id=1, source_target_pairs={{0,32},{16,48},{32,0},{48,16},{1,33},{17,49},{33,1},{49,17},{2,34}... | collective-permute-start | bytes 393224 | tf_op jit(solution)/shard_map/ppermute | solution.py:565
  24.0 5.8 %collective-permute-start.4 = (f32[4,64,128]{2,1,0:T(8,128)S(1)}, f32[4,64,128]{2,1,0:T(8,128)S(1)}, u32[]{:S(2)}, u32[]{:S(2)}) collective-permute-start(f32[4,64,128]{2,1,0:T(8,128)S(1)} %get-tuple-element.40), channel_id=1, source_target_pairs={{0,48},{16,0},{32,16},{48,32},{1,49},{17,1},{33,17},{49,33},{2,50}... | collective-permute-start | bytes 393224 | tf_op jit(solution)/shard_map/ppermute | solution.py:565
  30.6 1.3 %collective-permute-start.5 = (f32[128,128]{1,0:T(8,128)S(1)}, f32[128,128]{1,0:T(8,128)S(1)}, u32[]{:S(2)}, u32[]{:S(2)}) collective-permute-start(f32[128,128]{1,0:T(8,128)S(1)} %get-tuple-element.42), channel_id=1, source_target_pairs={{0,1},{1,0},{2,3},{3,2},{4,5},{5,4},{6,7},{7,6},{8,9},{9,8},{10,11... | collective-permute-start | bytes 196616 | tf_op jit(solution)/shard_map/ppermute | solution.py:565
  31.9 3.5 %collective-permute-start.8 = (f32[24,128]{1,0:T(8,128)S(1)}, f32[24,128]{1,0:T(8,128)S(1)}, u32[]{:S(2)}, u32[]{:S(2)}) collective-permute-start(f32[24,128]{1,0:T(8,128)S(1)} %get-tuple-element.49), channel_id=1, source_target_pairs={{0,48},{16,0},{32,16},{48,32},{1,49},{17,1},{33,17},{49,33},{2,50}... | collective-permute-start | bytes 36872 | tf_op jit(solution)/shard_map/ppermute | solution.py:565
  34.3 4.0 %collective-permute-start.7 = (f32[24,128]{1,0:T(8,128)S(1)}, f32[24,128]{1,0:T(8,128)S(1)}, u32[]{:S(2)}, u32[]{:S(2)}) collective-permute-start(f32[24,128]{1,0:T(8,128)S(1)} %get-tuple-element.50), channel_id=1, source_target_pairs={{0,32},{16,48},{32,0},{48,16},{1,33},{17,49},{33,1},{49,17},{2,34}... | collective-permute-start | bytes 36872 | tf_op jit(solution)/shard_map/ppermute | solution.py:565
  35.2 3.8 %collective-permute-start.6 = (f32[24,128]{1,0:T(8,128)S(1)}, f32[24,128]{1,0:T(8,128)S(1)}, u32[]{:S(2)}, u32[]{:S(2)}) collective-permute-start(f32[24,128]{1,0:T(8,128)S(1)} %get-tuple-element.51), channel_id=1, source_target_pairs={{0,16},{16,32},{32,48},{48,0},{1,17},{17,33},{33,49},{49,1},{2,18}... | collective-permute-start | bytes 36872 | tf_op jit(solution)/shard_map/ppermute | solution.py:565
  56.7 4.4 %collective-permute-start.9 = (f32[56,128]{1,0:T(8,128)S(1)}, f32[56,128]{1,0:T(8,128)S(1)}, u32[]{:S(2)}, u32[]{:S(2)}) collective-permute-start(f32[56,128]{1,0:T(8,128)S(1)} %reduce_sum.18.own_ref), channel_id=1, source_target_pairs={{0,1},{1,0},{2,3},{3,2},{4,5},{5,4},{6,7},{7,6},{8,9},{9,8},{10,11... | collective-permute-start | bytes 86024 | tf_op jit(solution)/shard_map/ppermute | solution.py:565
  65.0 3.1 %collective-permute-start.12 = (f32[112,128]{1,0:T(8,128)S(1)}, f32[112,128]{1,0:T(8,128)S(1)}, u32[]{:S(2)}, u32[]{:S(2)}) collective-permute-start(f32[112,128]{1,0:T(8,128)S(1)} %shard_map.78.p0), channel_id=1, source_target_pairs={{0,48},{16,0},{32,16},{48,32},{1,49},{17,1},{33,17},{49,33},{2,50}... | collective-permute-start | bytes 172040 | tf_op jit(solution)/shard_map/ppermute | solution.py:565
  65.4 4.5 %collective-permute-start.11 = (f32[112,128]{1,0:T(8,128)S(1)}, f32[112,128]{1,0:T(8,128)S(1)}, u32[]{:S(2)}, u32[]{:S(2)}) collective-permute-start(f32[112,128]{1,0:T(8,128)S(1)} %shard_map.78.p0), channel_id=1, source_target_pairs={{0,32},{16,48},{32,0},{48,16},{1,33},{17,49},{33,1},{49,17},{2,34}... | collective-permute-start | bytes 172040 | tf_op jit(solution)/shard_map/ppermute | solution.py:565
  66.6 5.3 %collective-permute-start.10 = (f32[112,128]{1,0:T(8,128)S(1)}, f32[112,128]{1,0:T(8,128)S(1)}, u32[]{:S(2)}, u32[]{:S(2)}) collective-permute-start(f32[112,128]{1,0:T(8,128)S(1)} %shard_map.78.p0), channel_id=1, source_target_pairs={{0,16},{16,32},{32,48},{48,0},{1,17},{17,33},{33,49},{49,1},{2,18}... | collective-permute-start | bytes 172040 | tf_op jit(solution)/shard_map/ppermute | solution.py:565
  82.0 6.1 %collective-permute-start.15 = (f32[288,128]{1,0:T(8,128)S(1)}, f32[288,128]{1,0:T(8,128)S(1)}, u32[]{:S(2)}, u32[]{:S(2)}) collective-permute-start(f32[288,128]{1,0:T(8,128)S(1)} %shard_map.79.r0), channel_id=1, source_target_pairs={{0,192},{64,0},{128,64},{192,128},{1,193},{65,1},{129,65},{193,129... | collective-permute-start | bytes 442376 | tf_op jit(solution)/shard_map/ppermute | solution.py:565
  84.8 5.6 %collective-permute-start.14 = (f32[288,128]{1,0:T(8,128)S(1)}, f32[288,128]{1,0:T(8,128)S(1)}, u32[]{:S(2)}, u32[]{:S(2)}) collective-permute-start(f32[288,128]{1,0:T(8,128)S(1)} %shard_map.79.r0), channel_id=1, source_target_pairs={{0,128},{64,192},{128,0},{192,64},{1,129},{65,193},{129,1},{193,65... | collective-permute-start | bytes 442376 | tf_op jit(solution)/shard_map/ppermute | solution.py:565
  85.3 9.7 %collective-permute-start.13 = (f32[288,128]{1,0:T(8,128)S(1)}, f32[288,128]{1,0:T(8,128)S(1)}, u32[]{:S(2)}, u32[]{:S(2)}) collective-permute-start(f32[288,128]{1,0:T(8,128)S(1)} %shard_map.79.r0), channel_id=1, source_target_pairs={{0,64},{64,128},{128,192},{192,0},{1,65},{65,129},{129,193},{193,1... | collective-permute-start | bytes 442376 | tf_op jit(solution)/shard_map/ppermute | solution.py:565
  96.1 1.6 %collective-permute-start.16 = (f32[48,128]{1,0:T(8,128)S(1)}, f32[48,128]{1,0:T(8,128)S(1)}, u32[]{:S(2)}, u32[]{:S(2)}) collective-permute-start(f32[48,128]{1,0:T(8,128)S(1)} %get-tuple-element.47), channel_id=1, source_target_pairs={{0,1},{1,0},{2,3},{3,2},{4,5},{5,4},{6,7},{7,6},{8,9},{9,8},{10,11... | collective-permute-start | bytes 73736 | tf_op jit(solution)/shard_map/ppermute | solution.py:565
  97.7 2.7 %collective-permute-start.19 = (f32[48,128]{1,0:T(8,128)S(1)}, f32[48,128]{1,0:T(8,128)S(1)}, u32[]{:S(2)}, u32[]{:S(2)}) collective-permute-start(f32[48,128]{1,0:T(8,128)S(1)} %add.28), channel_id=1, source_target_pairs={{0,48},{16,0},{32,16},{48,32},{1,49},{17,1},{33,17},{49,33},{2,50}... | collective-permute-start | bytes 73736 | tf_op jit(solution)/shard_map/ppermute | solution.py:565
  98.1 4.2 %collective-permute-start.18 = (f32[48,128]{1,0:T(8,128)S(1)}, f32[48,128]{1,0:T(8,128)S(1)}, u32[]{:S(2)}, u32[]{:S(2)}) collective-permute-start(f32[48,128]{1,0:T(8,128)S(1)} %add.28), channel_id=1, source_target_pairs={{0,32},{16,48},{32,0},{48,16},{1,33},{17,49},{33,1},{49,17},{2,34}... | collective-permute-start | bytes 73736 | tf_op jit(solution)/shard_map/ppermute | solution.py:565
  98.7 4.1 %collective-permute-start.17 = (f32[48,128]{1,0:T(8,128)S(1)}, f32[48,128]{1,0:T(8,128)S(1)}, u32[]{:S(2)}, u32[]{:S(2)}) collective-permute-start(f32[48,128]{1,0:T(8,128)S(1)} %add.28), channel_id=1, source_target_pairs={{0,16},{16,32},{32,48},{48,0},{1,17},{17,33},{33,49},{49,1},{2,18}... | collective-permute-start | bytes 73736 | tf_op jit(solution)/shard_map/ppermute | solution.py:565
  113.9 3.8 %collective-permute-start.20 = (f32[48,128]{1,0:T(8,128)S(1)}, f32[48,128]{1,0:T(8,128)S(1)}, u32[]{:S(2)}, u32[]{:S(2)}) collective-permute-start(f32[48,128]{1,0:T(8,128)S(1)} %reduce_sum.19.own_ref), channel_id=1, source_target_pairs={{0,1},{1,0},{2,3},{3,2},{4,5},{5,4},{6,7},{7,6},{8,9},{9,8},{10,11... | collective-permute-start | bytes 73736 | tf_op jit(solution)/shard_map/ppermute | solution.py:565
